TPU v7x, 32 devices: a whole 2x2x4 slice. The times are simulated.
32 devices in a mesh: dp: 8 (over z, y), pair: 4 (over x, core).
Axes of the slice: x: 2, y: 2, z: 4, core: 2. Of those that a mesh axis runs over, the one named last changes fastest.
Arguments:
- token_owner: int32 [64, 512, 1], P(('dp', 'pair')), may hold values from 0 to 7; in each aligned block of 1024 rows (0 to 1023, 1024 to 2047, ..., all dimensions but the last counted through in order) at most 256 rows name the same one
- token_row: int32 [64, 512], P(('dp', 'pair')), may hold values from 0 to 4015
- lengths: int32 [64], P(('dp', 'pair')), may hold values from 1 to 512, 20480 in all
- positives: int32 [64], replicated, may hold values from 0 to 63
- negatives: int32 [64, 7], replicated, may hold values from 0 to 63
- neg_counts: int32 [64], replicated, may hold values from 1 to 7
- embed_table: float32 [32128, 768], P('dp'), may hold values from -6 to 6
- embed_first: float32 [32128, 768], P('dp'), may hold values from -2.861023e-06 to 2.861023e-06
- embed_second: float32 [32128, 768], P('dp'), may hold values from 1.968368e-14 to 7.873472e-14
- qkv_weight: float32 [768, 2304], P(('dp', 'pair')), may hold values from -0.21875 to 0.21875
- qkv_first: float32 [768, 2304], P(('dp', 'pair')), may hold values from -5.722046e-06 to 5.722046e-06
- qkv_second: float32 [768, 2304], P(('dp', 'pair')), may hold values from 7.873472e-14 to 3.1493888e-13
- out_weight: float32 [768, 768], P(('dp', 'pair')), may hold values from -1.75 to 1.75
- out_first: float32 [768, 768], P(('dp', 'pair')), may hold values from -5.722046e-06 to 5.722046e-06
- out_second: float32 [768, 768], P(('dp', 'pair')), may hold values from 7.873472e-14 to 3.1493888e-13
- in_weight: float32 [768, 3072], P(('dp', 'pair')), may hold values from -0.21875 to 0.21875
- in_first: float32 [768, 3072], P(('dp', 'pair')), may hold values from -5.722046e-06 to 5.722046e-06
- in_second: float32 [768, 3072], P(('dp', 'pair')), may hold values from 7.873472e-14 to 3.1493888e-13
- down_weight: float32 [3072, 768], P(('dp', 'pair')), may hold values from -0.109375 to 0.109375
- down_first: float32 [3072, 768], P(('dp', 'pair')), may hold values from -5.722046e-06 to 5.722046e-06
- down_second: float32 [3072, 768], P(('dp', 'pair')), may hold values from 7.873472e-14 to 3.1493888e-13
- norm_gains: float32 [3, 768], replicated, may hold values from 0.5 to 1.5
- gains_first: float32 [3, 768], replicated, may hold values from -2.2888184e-05 to 2.2888184e-05
- gains_second: float32 [3, 768], replicated, may hold values from 1.2597555e-12 to 5.039022e-12
- position_bias: float32 [32, 12], replicated, may hold values from -3 to 3
- bias_first: float32 [32, 12], replicated, may hold values from -2.2888184e-05 to 2.2888184e-05
- bias_second: float32 [32, 12], replicated, may hold values from 1.2597555e-12 to 5.039022e-12
Outputs:
- loss_value: float32 [], replicated
- clip_norm: float32 [], replicated
- embed_new: float32 [32128, 768], P('dp')
- embed_first_new: float32 [32128, 768], P('dp')
- embed_second_new: float32 [32128, 768], P('dp')
- qkv_new: float32 [768, 2304], P(('dp', 'pair'))
- qkv_first_new: float32 [768, 2304], P(('dp', 'pair'))
- qkv_second_new: float32 [768, 2304], P(('dp', 'pair'))
- out_new: float32 [768, 768], P(('dp', 'pair'))
- out_first_new: float32 [768, 768], P(('dp', 'pair'))
- out_second_new: float32 [768, 768], P(('dp', 'pair'))
- in_new: float32 [768, 3072], P(('dp', 'pair'))
- in_first_new: float32 [768, 3072], P(('dp', 'pair'))
- in_second_new: float32 [768, 3072], P(('dp', 'pair'))
- down_new: float32 [3072, 768], P(('dp', 'pair'))
- down_first_new: float32 [3072, 768], P(('dp', 'pair'))
- down_second_new: float32 [3072, 768], P(('dp', 'pair'))
- gains_new: float32 [3, 768], replicated
- gains_first_new: float32 [3, 768], replicated
- gains_second_new: float32 [3, 768], replicated
- bias_new: float32 [32, 12], replicated
- bias_first_new: float32 [32, 12], replicated
- bias_second_new: float32 [32, 12], replicated
Inputs may be any that keep to these rules, and one draw needn't show every extreme that they name: `token_owner`: within each aligned block of 1024 tokens, no owner is named by more than 256 tokens, a bound that some block reaches. The lengths add up to 20480, and the longest is exactly 512.
All inputs are finite; a program needn't handle non-finite values. No bound on the sum of `lengths` on one device may be relied on, other than what follows from the above.
Results may differ from a plain program's by a relative error of at most 0.012.
The roundings to bfloat16 on the way count: a program that leaves them out, or rounds other values in their place, can miss the bound.
Values may be sent and summed in bfloat16 or wider, within the bound.
A program may use at most 256 MiB of HBM per device.

v0:
```python
import math

import jax
import jax.numpy as jnp
from jax import lax
from jax.sharding import PartitionSpec as P

REACH = 128
STEP = 5


rms_eps = 1e-06
clip_limit = 0.05
margin = 1.0
sim_scale = 20.0
beta_one = 0.9
beta_two = 0.999
adam_eps = 1e-08
HIGHEST = lax.Precision.HIGHEST
CONTRACT_ROWS = (((0,), (0,)), ((), ()))
CONTRACT_COLS = (((1,), (1,)), ((), ()))


def bucket_of(offsets, bucket_count, reach_limit):
    half_count = bucket_count // 2
    exact_count = half_count // 2
    sign_base = jnp.where(offsets > 0, half_count, 0).astype(jnp.int32)
    distance = jnp.abs(offsets)
    far_bucket = jnp.full(offsets.shape, exact_count, jnp.int32)
    for level_index in range(1, half_count - exact_count):
        threshold = int(
            math.ceil(
                exact_count
                * (reach_limit / exact_count) ** (level_index / (half_count - exact_count))
                - 1e-09
            )
        )
        far_bucket = far_bucket + (distance >= threshold).astype(jnp.int32)
    return sign_base + jnp.where(distance < exact_count, distance, far_bucket)


def rms_forward(values, gain):
    inverse = lax.rsqrt(jnp.mean(values * values, axis=-1, keepdims=True) + rms_eps)
    return (values * inverse * gain, inverse)


def rms_backward(values, inverse, gain, upstream):
    scaled = upstream * gain
    normed = values * inverse
    grad_values = inverse * (scaled - normed * jnp.mean(scaled * normed, axis=-1, keepdims=True))
    return (grad_values, jnp.sum(upstream * normed, axis=0))


def margin_loss(pooled, positives, negatives, neg_counts):
    unit = pooled * lax.rsqrt(jnp.sum(pooled * pooled, axis=-1, keepdims=True) + 1e-06)
    similar = sim_scale * jnp.dot(unit, unit.T, precision=HIGHEST)
    chosen = jnp.take_along_axis(similar, positives[:, None], axis=1)
    against = jnp.take_along_axis(similar, negatives, axis=1)
    live_slots = jnp.arange(negatives.shape[1])[None, :] < neg_counts[:, None]
    terms = jnp.where(live_slots, jax.nn.softplus(margin - chosen + against), 0.0)
    return jnp.mean(jnp.sum(terms, axis=1) / neg_counts.astype(jnp.float32))


def doc_scores(query_heads, key_heads, bias_full, live_keys):
    scores = (
        jnp.einsum("qhd,khd->hqk", query_heads, key_heads, preferred_element_type=jnp.float32)
        * 0.125
        + bias_full
    )
    return jnp.where(live_keys[None, None, :], scores, -1000000000.0)


def attend_forward(query_heads, key_heads, value_heads, bias_full, live_keys):
    scores = doc_scores(query_heads, key_heads, bias_full, live_keys)
    highest = jnp.max(scores, axis=-1, keepdims=True)
    weights = jnp.exp(scores - highest)
    totals = jnp.sum(weights, axis=-1, keepdims=True)
    probabilities = (weights / totals).astype(jnp.bfloat16)
    attended = jnp.einsum(
        "hqk,khd->qhd", probabilities, value_heads, preferred_element_type=jnp.float32
    )
    return (attended, highest + jnp.log(totals))


def attend_backward(
    query_heads, key_heads, value_heads, bias_full, live_keys, logsum, grad_attended
):
    probabilities = jnp.exp(doc_scores(query_heads, key_heads, bias_full, live_keys) - logsum)
    grad_value = jnp.einsum(
        "hqk,qhd->khd",
        probabilities.astype(jnp.bfloat16),
        grad_attended,
        preferred_element_type=jnp.float32,
    )
    grad_prob = jnp.einsum(
        "qhd,khd->hqk", grad_attended, value_heads, preferred_element_type=jnp.float32
    )
    grad_score = probabilities * (
        grad_prob - jnp.sum(probabilities * grad_prob, axis=-1, keepdims=True)
    )
    grad_low = grad_score.astype(jnp.bfloat16)
    grad_query = (
        jnp.einsum("hqk,khd->qhd", grad_low, key_heads, preferred_element_type=jnp.float32) * 0.125
    )
    grad_key = (
        jnp.einsum("hqk,qhd->khd", grad_low, query_heads, preferred_element_type=jnp.float32)
        * 0.125
    )
    return (grad_query, grad_key, grad_value, grad_low)


def adam_step(weight, first, second, grad, rate, shrink):
    first_new = beta_one * first + (1.0 - beta_one) * grad
    second_new = beta_two * second + (1.0 - beta_two) * grad * grad
    first_hat = first_new / (1.0 - beta_one**STEP)
    second_hat = second_new / (1.0 - beta_two**STEP)
    weight_new = weight - rate * (first_hat / (jnp.sqrt(second_hat) + adam_eps) + shrink * weight)
    return (weight_new, first_new, second_new)


def local(
    token_owner,
    token_row,
    lengths,
    positives,
    negatives,
    neg_counts,
    embed_table,
    embed_first,
    embed_second,
    qkv_weight,
    qkv_first,
    qkv_second,
    out_weight,
    out_first,
    out_second,
    in_weight,
    in_first,
    in_second,
    down_weight,
    down_first,
    down_second,
    norm_gains,
    gains_first,
    gains_second,
    position_bias,
    bias_first,
    bias_second,
):
    doc_count = lengths.shape[0]
    seq_len = token_row.shape[1]
    model_width = embed_table.shape[1]
    head_count = position_bias.shape[1]
    bucket_count = position_bias.shape[0]
    tok_total = doc_count * seq_len
    owners = lax.axis_size("dp")
    capacity = max(2, 2 * tok_total // owners)
    low_mats = (
        qkv_weight.astype(jnp.bfloat16),
        out_weight.astype(jnp.bfloat16),
        in_weight.astype(jnp.bfloat16),
        down_weight.astype(jnp.bfloat16),
    )
    qkv_full, out_full, in_full, down_full = (
        lax.all_gather(low_mats[0], ("dp", "pair"), axis=0, tiled=True),
        lax.all_gather(low_mats[1], ("dp", "pair"), axis=0, tiled=True),
        lax.all_gather(low_mats[2], ("dp", "pair"), axis=0, tiled=True),
        lax.all_gather(low_mats[3], ("dp", "pair"), axis=0, tiled=True),
    )
    tok_owner = token_owner.reshape(-1)
    tok_row = token_row.reshape(-1)
    owner_hits = (tok_owner[:, None] == jnp.arange(owners, dtype=jnp.int32)[None, :]).astype(
        jnp.int32
    )
    slot_rank = jnp.sum((jnp.cumsum(owner_hits, axis=0) - 1) * owner_hits, axis=1)
    requests = jnp.zeros((owners, capacity), jnp.int32).at[tok_owner, slot_rank].set(tok_row)
    asked_rows = lax.all_to_all(requests, "dp", split_axis=0, concat_axis=0, tiled=True)
    looked = jnp.take(embed_table, asked_rows.reshape(-1), axis=0).astype(jnp.bfloat16)
    answer = lax.all_to_all(
        looked.reshape(asked_rows.shape + (model_width,)),
        "dp",
        split_axis=0,
        concat_axis=0,
        tiled=True,
    )
    replies, asked_rows = (answer, asked_rows)
    embedded = replies[tok_owner, slot_rank].astype(jnp.float32)
    positions = jnp.arange(seq_len)
    live = positions[None, :] < lengths[:, None]
    pair_buckets = bucket_of(
        (positions[None, :] - positions[:, None]).reshape(-1), bucket_count, REACH
    )
    pair_hits = (jnp.arange(bucket_count)[:, None] == pair_buckets[None, :]).astype(jnp.float32)
    bias_full = jnp.dot(position_bias.T, pair_hits, precision=HIGHEST).reshape(
        head_count, seq_len, seq_len
    )
    bucket_map = pair_hits.astype(jnp.bfloat16)

    def split_doc(source, doc_index):
        doc_rows = source[doc_index * seq_len : (doc_index + 1) * seq_len]
        return tuple(
            (
                doc_rows[:, member * model_width : (member + 1) * model_width].reshape(
                    seq_len, head_count, -1
                )
                for member in range(3)
            )
        )

    normed_one, inverse_one = rms_forward(embedded, norm_gains[0])
    normed_one = normed_one.astype(jnp.bfloat16)
    qkv_rows = jnp.dot(normed_one, qkv_full, preferred_element_type=jnp.float32).astype(
        jnp.bfloat16
    )
    attended_parts = []
    logsum_parts = []
    for doc_index in range(doc_count):
        query_heads, key_heads, value_heads = split_doc(qkv_rows, doc_index)
        doc_out, logsum = attend_forward(
            query_heads, key_heads, value_heads, bias_full, live[doc_index]
        )
        attended_parts.append(doc_out.reshape(seq_len, model_width))
        logsum_parts.append(logsum)
    attended = jnp.concatenate(attended_parts, axis=0).astype(jnp.bfloat16)
    residual = embedded + jnp.dot(attended, out_full, preferred_element_type=jnp.float32)
    normed_two, inverse_two = rms_forward(residual, norm_gains[1])
    normed_two = normed_two.astype(jnp.bfloat16)
    hidden = jax.nn.relu(jnp.dot(normed_two, in_full, preferred_element_type=jnp.float32)).astype(
        jnp.bfloat16
    )
    output_rows = residual + jnp.dot(hidden, down_full, preferred_element_type=jnp.float32)
    normed_three, inverse_three = rms_forward(output_rows, norm_gains[2])
    live_rows = live.reshape(-1, 1)
    length_float = lengths.astype(jnp.float32)
    pooled_local = (
        jnp.sum(
            jnp.where(live_rows, normed_three, 0.0).reshape(doc_count, seq_len, model_width), axis=1
        )
        / length_float[:, None]
    )
    pooled_all = lax.all_gather(pooled_local, ("dp", "pair"), axis=0, tiled=True)
    loss_value, loss_pullback = jax.vjp(
        lambda pooled_in: margin_loss(pooled_in, positives, negatives, neg_counts), pooled_all
    )
    grad_pooled_all = loss_pullback(jnp.ones((), jnp.float32))[0]
    grad_pooled = lax.dynamic_slice_in_dim(
        grad_pooled_all, lax.axis_index(("dp", "pair")) * doc_count, doc_count, 0
    )
    grad_three = jnp.where(
        live_rows, jnp.repeat(grad_pooled / length_float[:, None], seq_len, axis=0), 0.0
    )
    qkv_back, out_back, in_back, down_back = (qkv_full, out_full, in_full, down_full)
    grad_output, gain_three = rms_backward(output_rows, inverse_three, norm_gains[2], grad_three)
    grad_branch = grad_output.astype(jnp.bfloat16)
    grad_down = lax.dot_general(
        hidden, grad_branch, CONTRACT_ROWS, preferred_element_type=jnp.float32
    )
    grad_hidden = lax.dot_general(
        grad_branch, down_back, CONTRACT_COLS, preferred_element_type=jnp.float32
    )
    grad_pre = jnp.where(hidden > 0, grad_hidden, 0.0).astype(jnp.bfloat16)
    grad_in = lax.dot_general(
        normed_two, grad_pre, CONTRACT_ROWS, preferred_element_type=jnp.float32
    )
    grad_normed_two = lax.dot_general(
        grad_pre, in_back, CONTRACT_COLS, preferred_element_type=jnp.float32
    )
    grad_res_part, gain_two = rms_backward(residual, inverse_two, norm_gains[1], grad_normed_two)
    grad_residual = grad_output + grad_res_part
    grad_attn_branch = grad_residual.astype(jnp.bfloat16)
    grad_out = lax.dot_general(
        attended, grad_attn_branch, CONTRACT_ROWS, preferred_element_type=jnp.float32
    )
    grad_attended = lax.dot_general(
        grad_attn_branch, out_back, CONTRACT_COLS, preferred_element_type=jnp.float32
    ).astype(jnp.bfloat16)
    grad_qkv_parts = []
    bias_grad_heads = jnp.zeros((head_count, bucket_count), jnp.float32)
    for doc_index in range(doc_count):
        query_heads, key_heads, value_heads = split_doc(qkv_rows, doc_index)
        grad_doc = grad_attended[doc_index * seq_len : (doc_index + 1) * seq_len].reshape(
            seq_len, head_count, -1
        )
        grad_query, grad_key, grad_value, grad_low = attend_backward(
            query_heads,
            key_heads,
            value_heads,
            bias_full,
            live[doc_index],
            logsum_parts[doc_index],
            grad_doc,
        )
        grad_qkv_parts.append(
            jnp.concatenate(
                [
                    grad_query.reshape(seq_len, model_width),
                    grad_key.reshape(seq_len, model_width),
                    grad_value.reshape(seq_len, model_width),
                ],
                axis=1,
            )
        )
        bias_grad_heads = bias_grad_heads + lax.dot_general(
            grad_low.reshape(head_count, -1),
            bucket_map,
            CONTRACT_COLS,
            preferred_element_type=jnp.float32,
        )
    bias_grad_local = bias_grad_heads.T
    grad_qkv_rows = jnp.concatenate(grad_qkv_parts, axis=0).astype(jnp.bfloat16)
    grad_qkv = lax.dot_general(
        normed_one, grad_qkv_rows, CONTRACT_ROWS, preferred_element_type=jnp.float32
    )
    grad_normed_one = lax.dot_general(
        grad_qkv_rows, qkv_back, CONTRACT_COLS, preferred_element_type=jnp.float32
    )
    grad_emb_part, gain_one = rms_backward(embedded, inverse_one, norm_gains[0], grad_normed_one)
    grad_embedded = grad_residual + grad_emb_part
    sendback = (
        jnp.zeros((owners, capacity, model_width), jnp.float32)
        .at[tok_owner, slot_rank]
        .set(grad_embedded)
    )
    arrived = lax.all_to_all(sendback, "dp", split_axis=0, concat_axis=0, tiled=True)
    table_grad = jax.ops.segment_sum(
        arrived.reshape(-1, model_width), asked_rows.reshape(-1), num_segments=embed_table.shape[0]
    )
    table_grad = lax.psum(table_grad, "pair")
    weight_grads = (
        lax.psum_scatter(grad_qkv, ("dp", "pair"), scatter_dimension=0, tiled=True),
        lax.psum_scatter(grad_out, ("dp", "pair"), scatter_dimension=0, tiled=True),
        lax.psum_scatter(grad_in, ("dp", "pair"), scatter_dimension=0, tiled=True),
        lax.psum_scatter(grad_down, ("dp", "pair"), scatter_dimension=0, tiled=True),
    )
    pair_first = (lax.axis_index("pair") == 0).astype(jnp.float32)
    square_part = jnp.sum(
        jnp.stack([jnp.sum(grad_piece * grad_piece) for grad_piece in weight_grads])
    ) + pair_first * jnp.sum(table_grad * table_grad)
    gain_grad, bias_grad, square_sum = lax.psum(
        (jnp.stack([gain_one, gain_two, gain_three]), bias_grad_local, square_part), ("dp", "pair")
    )
    clip_norm = jnp.sqrt(
        square_sum + jnp.sum(gain_grad * gain_grad) + jnp.sum(bias_grad * bias_grad)
    )
    factor = jnp.minimum(1.0, clip_limit / clip_norm)
    table_out = adam_step(embed_table, embed_first, embed_second, table_grad * factor, 1.0, 0.01)
    qkv_out = adam_step(qkv_weight, qkv_first, qkv_second, weight_grads[0] * factor, 0.05, 0.01)
    out_out = adam_step(out_weight, out_first, out_second, weight_grads[1] * factor, 0.05, 0.01)
    in_out = adam_step(in_weight, in_first, in_second, weight_grads[2] * factor, 0.05, 0.01)
    down_out = adam_step(down_weight, down_first, down_second, weight_grads[3] * factor, 0.05, 0.01)
    gains_out = adam_step(norm_gains, gains_first, gains_second, gain_grad * factor, 1.0, 0.0)
    bias_out = adam_step(position_bias, bias_first, bias_second, bias_grad * factor, 0.3, 0.0)
    return (
        loss_value,
        clip_norm,
        table_out[0],
        table_out[1],
        table_out[2],
        qkv_out[0],
        qkv_out[1],
        qkv_out[2],
        out_out[0],
        out_out[1],
        out_out[2],
        in_out[0],
        in_out[1],
        in_out[2],
        down_out[0],
        down_out[1],
        down_out[2],
        gains_out[0],
        gains_out[1],
        gains_out[2],
        bias_out[0],
        bias_out[1],
        bias_out[2],
    )


def solution(mesh):
    return jax.shard_map(
        local,
        mesh=mesh,
        in_specs=(
            P(("dp", "pair"), None, None),
            P(("dp", "pair"), None),
            P(("dp", "pair")),
            P(),
            P(),
            P(),
            P("dp", None),
            P("dp", None),
            P("dp", None),
            P(("dp", "pair"), None),
            P(("dp", "pair"), None),
            P(("dp", "pair"), None),
            P(("dp", "pair"), None),
            P(("dp", "pair"), None),
            P(("dp", "pair"), None),
            P(("dp", "pair"), None),
            P(("dp", "pair"), None),
            P(("dp", "pair"), None),
            P(("dp", "pair"), None),
            P(("dp", "pair"), None),
            P(("dp", "pair"), None),
            P(),
            P(),
            P(),
            P(),
            P(),
            P(),
        ),
        out_specs=(
            P(),
            P(),
            P("dp", None),
            P("dp", None),
            P("dp", None),
            P(("dp", "pair"), None),
            P(("dp", "pair"), None),
            P(("dp", "pair"), None),
            P(("dp", "pair"), None),
            P(("dp", "pair"), None),
            P(("dp", "pair"), None),
            P(("dp", "pair"), None),
            P(("dp", "pair"), None),
            P(("dp", "pair"), None),
            P(("dp", "pair"), None),
            P(("dp", "pair"), None),
            P(("dp", "pair"), None),
            P(),
            P(),
            P(),
            P(),
            P(),
            P(),
        ),
        check_vma=False,
    )
```

profile of v0, /device:TPU:0, one launch (start us, length us, event | category | flops | bytes accessed | tf_op | source)
XLA Modules:
  0.0 1295.5 jit_solution(5997042993812791887)
XLA Ops:
  38.5 13.1 %gather_fusion = bf16[2048,768]{1,0:T(8,128)(2,1)S(1)} fusion(f32[4016,768]{1,0:T(8,128)} %param.33, s32[2048]{0:T(1024)S(1)} %broadcast_clamp_fusion), kind=kCustom, calls=%fused_computation | custom fusion | bytes 6299648 | tf_op jit(solution)/shard_map/jit(_take)/gather | solution.py:178
  62.2 11.2 fusion
  73.4 19.1 %copy.151 = f32[2,8,512,512]{3,2,1,0:T(8,128)} copy(f32[2,8,512,512]{3,1,2,0:T(8,128)S(1)} %bitcast.169) | data formatting | bytes 33554432
  92.5 10.7 slice.102
  103.2 12.6 copy.119
  115.9 21.7 %all-to-all-done.1 = bf16[8,256,768]{2,1,0:T(8,128)(2,1)S(1)} async-done(((bf16[8,256,768]{2,1,0:T(8,128)(2,1)}), bf16[8,256,768]{2,1,0:T(8,128)(2,1)S(1)}, u32[]{:S(2)}, u32[]{:S(2)}) %all-to-all-start.1) | async-done | bytes 3145760 | tf_op jit(solution)/shard_map/all_to_all | solution.py:179
  137.6 14.1 %gather_fusion.1 = bf16[1024,768]{1,0:T(8,128)(2,1)} fusion(bf16[8,256,768]{2,1,0:T(8,128)(2,1)S(1)} %all-to-all-done.1, s32[1024]{0:T(1024)S(1)} %bitcast.170), kind=kCustom, calls=%fused_computation.1 | custom fusion | bytes 3153920 | tf_op jit(solution)/shard_map/gather | solution.py:187
  177.2 11.7 fusion.115
  209.7 26.4 %all-gather.10.cloned.1.call-done = bf16[768,3072]{1,0:T(8,128)(2,1)} async-done(((bf16[24,3072]{1,0:T(8,128)(2,1)}), bf16[768,3072]{1,0:T(8,128)(2,1)}) %all-gather.10.cloned.1.call-update) | async-done | bytes 4718608 | tf_op jit(solution)/shard_map/all_gather | solution.py:167
  246.1 55.8 %all-gather.12.cloned.1.call-done = bf16[3072,768]{1,0:T(8,128)(2,1)} async-done(((bf16[96,768]{1,0:T(8,128)(2,1)}), bf16[3072,768]{1,0:T(8,128)(2,1)}) %all-gather.12.cloned.1.call-update) | async-done | bytes 4718608 | tf_op jit(solution)/shard_map/all_gather | solution.py:168
  311.7 42.5 %all-gather = f32[32,2,768]{2,1,0:T(2,128)} all-gather(f32[1,2,768]{2,1,0:T(2,128)S(1)} %divide_bitcast_fusion), channel_id=1, replica_groups=mesh['dp'=8,'pair'=4] {'dp','pair'}, dimensions={0}, use_global_device_ids=true | all-gather | bytes 202752 | tf_op jit(solution)/shard_map/all_gather | solution.py:241
  361.5 23.5 %scatter_fusion = f32[64,64]{1,0:T(8,128)S(1)} fusion(f32[64,64]{1,0:T(8,128)S(1)} %fusion.78, s32[448]{0:T(512)S(1)} %reshape.503, f32[448]{0:T(512)S(1)} %reshape.505), kind=kCustom, calls=%fused_computation.5 | custom fusion | flops 448 | bytes 8960 | tf_op jit(solution)/shard_map/transpose(jvp(jit(take_along_axis)))/scatter-add | solution.py:58
  413.9 10.9 multiply_reduce_fusion.1
  484.8 11.0 fusion.102
  509.2 14.7 %fusion.32 = (f32[768]{0:T(1024)S(1)}, f32[1024]{0:T(1024)S(1)}, f32[1024,768]{1,0:T(8,128)}) fusion(bf16[1024,768]{1,0:T(8,128)(2,1)S(1)} %copy-done.5, f32[1024]{0:T(1024)S(1)} %copy-done.58, f32[768]{0:T(1024)S(1)} %copy-done.60, bf16[768,2304]{1,0:T(8,128)(2,1)} %all-gather.6.cloned.1.call-done, bf16[512,768]{0,1:T(8,128)(2,1)} %bitcast.205, ...), kind=kOutput, calls=%fused_computation.63 | convolution fusion | flops 3657693440 | bytes 12990464 | tf_op jit(solution)/shard_map/dot_general | solution.py:314
  533.9 177.6 %all_to_all.19 = f32[8,256,768]{2,1,0:T(8,128)} all-to-all(f32[8,256,768]{2,1,0:T(8,128)} %bitcast.176), channel_id=1, replica_groups=mesh['dp'=8,'pair'=4] {'dp'}, dimensions={0} | all-to-all | bytes 12582912 | tf_op jit(solution)/shard_map/all_to_all | solution.py:324
  711.4 20.0 %scatter_custom_fusion = f32[4016,768]{1,0:T(8,128)} fusion(s32[2048]{0:T(1024)} %bitcast.214, f32[2048,768]{1,0:T(8,128)} %bitcast.194, f32[]{:T(128)} %constant.63.clone.1), kind=kCustom, calls=%fused_computation.46 | custom fusion | flops 1572864 | bytes 12337664 | tf_op jit(solution)/shard_map/scatter-add | solution.py:325
  756.7 11.5 copy.152
  772.5 11.8 copy.153
  801.7 31.9 %reduce-scatter.9.cloned.1.call-done = f32[24,3072]{1,0:T(8,128)} async-done(((f32[768,3072]{1,0:T(8,128)}), f32[24,3072]{1,0:T(8,128)}) %reduce-scatter.9.cloned.1.call-update) | async-done | bytes 294928 | tf_op jit(solution)/shard_map/reduce_scatter | solution.py:332
  836.0 140.0 %reduce-scatter.11.cloned.1.call-done = f32[96,768]{1,0:T(8,128)} async-done(((f32[3072,768]{1,0:T(8,128)}), f32[96,768]{1,0:T(8,128)}) %reduce-scatter.11.cloned.1.call-update) | async-done | bytes 294928 | tf_op jit(solution)/shard_map/reduce_scatter | solution.py:333
  978.4 216.8 %all-reduce.3.cloned.1.call-done = f32[4016,768]{1,0:T(8,128)} async-done(((f32[4016,768]{1,0:T(8,128)}), f32[4016,768]{1,0:T(8,128)}) %all-reduce.3.cloned.1.call-update) | async-done | bytes 12337168 | tf_op jit(solution)/shard_map/psum | solution.py:328
  1204.8 40.3 %all-reduce = (f32[]{:T(128)}, f32[3,768]{1,0:T(4,128)}, f32[32,12]{0,1:T(8,128)}) all-reduce(f32[]{:T(128)S(6)} %add.411, f32[3,768]{1,0:T(4,128)S(1)} %pad_maximum_fusion.3, f32[32,12]{0,1:T(8,128)} %fusion.55), channel_id=1, replica_groups=mesh['dp'=8,'pair'=4] {'dp','pair'}, use_global_device_ids=true, to_apply=%region_35.36 | all-reduce | flops 2689 | bytes 21512 | tf_op jit(solution)/shard_map/psum | solution.py:339
  1256.3 30.2 %add_subtract_fusion = (f32[4016,768]{1,0:T(8,128)}, f32[4016,768]{1,0:T(8,128)}, f32[4016,768]{1,0:T(8,128)}) fusion(f32[4016,768]{1,0:T(8,128)} %param.33, f32[4016,768]{1,0:T(8,128)} %all-reduce.3.cloned.1.call-done, f32[]{:T(128)S(6)} %min.3, f32[4016,768]{1,0:T(8,128)} %param.34, f32[4016,768]{1,0:T(8,128)} %param.35), kind=kLoop, calls=%fused_computation.32 | loop fusion | flops 46264320 | bytes 86360064 | tf_op jit(solution)/shard_map/sub | solution.py:117
  (337 shorter events, 292.9 us)
Async XLA Ops:
  7.2 146.4 %all-gather.6.cloned.1.call-start = ((), (), s32[]{:S(2)}) async-start(), calls=%async_computation.7 | async-start | bytes 3649536 | tf_op jit(solution)/shard_map/all_gather | solution.py:165
  8.9 196.1 %all-gather.8.cloned.1.call-start = ((), (), s32[]{:S(2)}) async-start(), calls=%async_computation.8 | async-start | bytes 1216512 | tf_op jit(solution)/shard_map/all_gather | solution.py:166
  10.4 225.7 %all-gather.10.cloned.1.call-start = ((), (), s32[]{:S(2)}) async-start(), calls=%async_computation.9 | async-start | bytes 4866048 | tf_op jit(solution)/shard_map/all_gather | solution.py:167
  24.1 14.3 %all-to-all-start = ((s32[8,1,256]{2,1,0:T(1,128)}), s32[8,1,256]{2,1,0:T(1,128)S(1)}, u32[]{:S(2)}, u32[]{:S(2)}) async-start(s32[8,1,256]{2,1,0:T(1,128)} %bitcast.5), calls=%async_computation | async-start | bytes 16384 | tf_op jit(solution)/shard_map/all_to_all | solution.py:177
  31.4 270.5 %all-gather.12.cloned.1.call-start = ((), (), s32[]{:S(2)}) async-start(), calls=%async_computation.10 | async-start | bytes 4866048 | tf_op jit(solution)/shard_map/all_gather | solution.py:168
  53.6 84.0 %all-to-all-start.1 = ((bf16[8,256,768]{2,1,0:T(8,128)(2,1)}), bf16[8,256,768]{2,1,0:T(8,128)(2,1)S(1)}, u32[]{:S(2)}, u32[]{:S(2)}) async-start(bf16[8,256,768]{2,1,0:T(8,128)(2,1)} %select_convert_fusion.1), calls=%async_computation.1 | async-start | bytes 6291456 | tf_op jit(solution)/shard_map/all_to_all | solution.py:179
  59.7 737.6 %reduce-scatter.7.cloned.1.call-start = ((), (), s32[]{:S(2)}) async-start(), calls=%async_computation.12 | async-start | bytes 2433024 | tf_op jit(solution)/shard_map/reduce_scatter | solution.py:331
  438.9 360.0 %reduce-scatter.5.cloned.1.call-start = ((), (), s32[]{:S(2)}) async-start(), calls=%async_computation.11 | async-start | bytes 7299072 | tf_op jit(solution)/shard_map/reduce_scatter | solution.py:330
  482.9 350.7 %reduce-scatter.9.cloned.1.call-start = ((), (), s32[]{:S(2)}) async-start(), calls=%async_computation.13 | async-start | bytes 9732096 | tf_op jit(solution)/shard_map/reduce_scatter | solution.py:332
  495.8 480.1 %reduce-scatter.11.cloned.1.call-start = ((), (), s32[]{:S(2)}) async-start(), calls=%async_computation.14 | async-start | bytes 9732096 | tf_op jit(solution)/shard_map/reduce_scatter | solution.py:333
  507.4 687.8 %all-reduce.3.cloned.1.call-start = ((), (), s32[]{:S(2)}) async-start(), calls=%async_computation.15 | async-start | bytes 24674304 | tf_op jit(solution)/shard_map/psum | solution.py:328
  978.2 274.2 %copy-start.47 = (f32[24,768]{1,0:T(8,128)S(1)}, f32[24,768]{1,0:T(8,128)}, u32[]{:S(2)}) copy-start(f32[24,768]{1,0:T(8,128)} %param.39) | copy-start | bytes 221188
  978.3 274.9 %copy-start.37 = (f32[24,2304]{1,0:T(8,128)S(1)}, f32[24,2304]{1,0:T(8,128)}, u32[]{:S(2)}) copy-start(f32[24,2304]{1,0:T(8,128)} %reduce-scatter.5.cloned.1.call-done) | copy-start | bytes 663556
  978.3 274.9 %copy-start.38 = (f32[24,2304]{1,0:T(8,128)S(1)}, f32[24,2304]{1,0:T(8,128)}, u32[]{:S(2)}) copy-start(f32[24,2304]{1,0:T(8,128)} %param.36) | copy-start | bytes 663556
  978.3 274.9 %copy-start.49 = (f32[24,2304]{1,0:T(8,128)S(1)}, f32[24,2304]{1,0:T(8,128)}, u32[]{:S(2)}) copy-start(f32[24,2304]{1,0:T(8,128)} %param.37) | copy-start | bytes 663556
  978.3 274.9 %copy-start.50 = (f32[24,2304]{1,0:T(8,128)S(1)}, f32[24,2304]{1,0:T(8,128)}, u32[]{:S(2)}) copy-start(f32[24,2304]{1,0:T(8,128)} %param.38) | copy-start | bytes 663556
  978.3 275.9 %copy-start.33 = (f32[96,768]{1,0:T(8,128)S(1)}, f32[96,768]{1,0:T(8,128)}, u32[]{:S(2)}) copy-start(f32[96,768]{1,0:T(8,128)} %param.45) | copy-start | bytes 884740
  978.3 275.8 %copy-start.36 = (f32[96,768]{1,0:T(8,128)S(1)}, f32[96,768]{1,0:T(8,128)}, u32[]{:S(2)}) copy-start(f32[96,768]{1,0:T(8,128)} %reduce-scatter.11.cloned.1.call-done) | copy-start | bytes 884740
  978.3 275.8 %copy-start.43 = (f32[96,768]{1,0:T(8,128)S(1)}, f32[96,768]{1,0:T(8,128)}, u32[]{:S(2)}) copy-start(f32[96,768]{1,0:T(8,128)} %param.46) | copy-start | bytes 884740
  978.4 275.8 %copy-start.44 = (f32[96,768]{1,0:T(8,128)S(1)}, f32[96,768]{1,0:T(8,128)}, u32[]{:S(2)}) copy-start(f32[96,768]{1,0:T(8,128)} %param.47) | copy-start | bytes 884740
  978.4 276.9 %copy-start.34 = (f32[24,3072]{1,0:T(8,128)S(1)}, f32[24,3072]{1,0:T(8,128)}, u32[]{:S(2)}) copy-start(f32[24,3072]{1,0:T(8,128)} %param.42) | copy-start | bytes 884740
  978.4 276.9 %copy-start.35 = (f32[24,3072]{1,0:T(8,128)S(1)}, f32[24,3072]{1,0:T(8,128)}, u32[]{:S(2)}) copy-start(f32[24,3072]{1,0:T(8,128)} %reduce-scatter.9.cloned.1.call-done) | copy-start | bytes 884740
  978.4 276.9 %copy-start.45 = (f32[24,3072]{1,0:T(8,128)S(1)}, f32[24,3072]{1,0:T(8,128)}, u32[]{:S(2)}) copy-start(f32[24,3072]{1,0:T(8,128)} %param.43) | copy-start | bytes 884740
  978.4 276.9 %copy-start.46 = (f32[24,3072]{1,0:T(8,128)S(1)}, f32[24,3072]{1,0:T(8,128)}, u32[]{:S(2)}) copy-start(f32[24,3072]{1,0:T(8,128)} %param.44) | copy-start | bytes 884740
  (75 other events, 1409.2 us)
Sparse Core Ops, SparseCore 0:
  11.5 81.4 all-gather.5
  96.5 73.5 all-gather.7
  173.5 62.5 all-gather.9
  239.5 62.4 all-gather.11
  439.0 95.0 reduce-scatter.6
  540.6 151.4 reduce-scatter.4
  698.5 135.1 reduce-scatter.8
  841.1 134.7 reduce-scatter.10
  979.0 216.1 all-reduce.2
where the time goes:
time: 1300 us
  waiting for transfers between devices  493 us (38%)
  blocking collectives  260 us (20%)
  matrix products  186 us (14%)
  local copies, waits for them, and re-layouts  161 us (12%)
  other arithmetic  158 us (12%)
  between operations  23.6 us (2%)
  starting transfers between devices  13.7 us (1%)
    psum x1, waiting for transfers between devices, local(): table_grad = lax.psum(table_grad, 'pair')  217 us
    all_to_all x1, blocking collectives, local(): lax.all_to_all(sendback, 'dp', split_axis=0, concat_axis=0, tiled=True)  178 us
    reduce_scatter x1, waiting for transfers between devices, local(): lax.psum_scatter(grad_down, ('dp', 'pair'), scatter_dimension=0, tiled=True)  140 us
    unnamed x187, local copies, waits for them, and re-layouts  78.5 us
    all_gather x1, waiting for transfers between devices, local(): lax.all_gather(low_mats[3], ('dp', 'pair'), axis=0, tiled=True)  55.8 us
    all_gather x1, blocking collectives, local(): lax.all_gather(pooled_local, ('dp', 'pair'), axis=0, tiled=True)  42.5 us
    psum x1, blocking collectives, local(): lax.psum((jnp.stack([gain_one, gain_two, gain_three]), bias_grad_local, s...  40.3 us
    sub x7, other arithmetic, adam_step(): weight - rate * (first_hat / (jnp.sqrt(second_hat) + adam_eps) + shrink *...  36.7 us
  transfers between devices with their start and end apart: 11, of which 6 were waited for; matrix products, arithmetic and copies ran while one was open for 27% of the time, Pallas kernels for 0%

commit v1 on v0

--- a/solution.py
+++ b/solution.py
@@ -317,20 +317,22 @@
     grad_emb_part, gain_one = rms_backward(embedded, inverse_one, norm_gains[0], grad_normed_one)
     grad_embedded = grad_residual + grad_emb_part
     sendback = (
-        jnp.zeros((owners, capacity, model_width), jnp.float32)
+        jnp.zeros((owners, capacity, model_width), jnp.bfloat16)
         .at[tok_owner, slot_rank]
-        .set(grad_embedded)
+        .set(grad_embedded.astype(jnp.bfloat16))
     )
     arrived = lax.all_to_all(sendback, "dp", split_axis=0, concat_axis=0, tiled=True)
     table_grad = jax.ops.segment_sum(
-        arrived.reshape(-1, model_width), asked_rows.reshape(-1), num_segments=embed_table.shape[0]
-    )
-    table_grad = lax.psum(table_grad, "pair")
+        arrived.reshape(-1, model_width).astype(jnp.float32),
+        asked_rows.reshape(-1),
+        num_segments=embed_table.shape[0],
+    )
+    table_grad = lax.psum(table_grad.astype(jnp.bfloat16), "pair").astype(jnp.float32)
     weight_grads = (
-        lax.psum_scatter(grad_qkv, ("dp", "pair"), scatter_dimension=0, tiled=True),
-        lax.psum_scatter(grad_out, ("dp", "pair"), scatter_dimension=0, tiled=True),
-        lax.psum_scatter(grad_in, ("dp", "pair"), scatter_dimension=0, tiled=True),
-        lax.psum_scatter(grad_down, ("dp", "pair"), scatter_dimension=0, tiled=True),
+        lax.psum_scatter(grad_qkv.astype(jnp.bfloat16), ("dp", "pair"), scatter_dimension=0, tiled=True).astype(jnp.float32),
+        lax.psum_scatter(grad_out.astype(jnp.bfloat16), ("dp", "pair"), scatter_dimension=0, tiled=True).astype(jnp.float32),
+        lax.psum_scatter(grad_in.astype(jnp.bfloat16), ("dp", "pair"), scatter_dimension=0, tiled=True).astype(jnp.float32),
+        lax.psum_scatter(grad_down.astype(jnp.bfloat16), ("dp", "pair"), scatter_dimension=0, tiled=True).astype(jnp.float32),
     )
     pair_first = (lax.axis_index("pair") == 0).astype(jnp.float32)
     square_part = jnp.sum(

time: 1300 us -> 1100 us (0.85)
  waiting for transfers between devices: 493 us -> 384 us
  blocking collectives: 260 us -> 168 us
    psum x1, waiting for transfers between devices: 217 us -> 117 us  [local(): lax.psum(table_grad.astype(jnp.bfloat16), 'pair').astype(jnp.float32)]
    all_to_all x1, blocking collectives: 178 us -> 84.9 us  [local(): lax.all_to_all(sendback, 'dp', split_axis=0, concat_axis=0, tiled=True)]
    dot_general x1, matrix products: 7.11 us -> 26 us  [local(): lax.dot_general(normed_one, grad_qkv_rows, CONTRACT_ROWS, preferred_eleme...]
    reduce_scatter x4, waiting for transfers between devices: 172 us -> 159 us  [the longest x1 110 us: local(): lax.psum_scatter(grad_down.astype(jnp.bfloat16), ('dp', 'pair'), scatter_...]
    unnamed x187 -> x171, local copies, waits for them, and re-layouts: 78.5 us -> 72.4 us
  transfers between devices with their start and end apart: 11 -> 11, of which waited for: 6 -> 6; matrix products, arithmetic and copies ran while one was open for 27% -> 32% of each run, Pallas kernels for 0% -> 0%
where the time goes in v1:
time: 1100 us
  waiting for transfers between devices  384 us (35%)
  matrix products  193 us (18%)
  blocking collectives  168 us (15%)
  other arithmetic  161 us (15%)
  local copies, waits for them, and re-layouts  155 us (14%)
  between operations  23.5 us (2%)
  starting transfers between devices  13.7 us (1%)
    psum x1, waiting for transfers between devices, local(): lax.psum(table_grad.astype(jnp.bfloat16), 'pair').astype(jnp.float32)  117 us
    reduce_scatter x1, waiting for transfers between devices, local(): lax.psum_scatter(grad_down.astype(jnp.bfloat16), ('dp', 'pair'), scatter_...  110 us
    all_to_all x1, blocking collectives, local(): lax.all_to_all(sendback, 'dp', split_axis=0, concat_axis=0, tiled=True)  84.9 us
    unnamed x171, local copies, waits for them, and re-layouts  72.4 us
    all_gather x1, waiting for transfers between devices, local(): lax.all_gather(low_mats[3], ('dp', 'pair'), axis=0, tiled=True)  55.8 us
    reduce_scatter x1, waiting for transfers between devices, local(): lax.psum_scatter(grad_in.astype(jnp.bfloat16), ('dp', 'pair'), scatter_di...  48.4 us
    all_gather x1, blocking collectives, local(): lax.all_gather(pooled_local, ('dp', 'pair'), axis=0, tiled=True)  42.5 us
    psum x1, blocking collectives, local(): lax.psum((jnp.stack([gain_one, gain_two, gain_three]), bias_grad_local, s...  40.2 us
  transfers between devices with their start and end apart: 11, of which 6 were waited for; matrix products, arithmetic and copies ran while one was open for 32% of the time, Pallas kernels for 0%

profile of v1, /device:TPU:0, one launch (start us, length us, event | category | flops | bytes accessed | tf_op | source)
XLA Modules:
  0.0 1097.4 jit_solution(4546849531026565448)
XLA Ops:
  38.5 13.1 %gather_fusion = bf16[2048,768]{1,0:T(8,128)(2,1)S(1)} fusion(f32[4016,768]{1,0:T(8,128)} %param.33, s32[2048]{0:T(1024)S(1)} %broadcast_clamp_fusion), kind=kCustom, calls=%fused_computation | custom fusion | bytes 6299648 | tf_op jit(solution)/shard_map/jit(_take)/gather | solution.py:178
  62.2 11.2 %fusion = f32[262144,12]{0,1:T(8,128)S(1)} fusion(f32[32,12]{0,1:T(8,128)S(1)} %copy-done.45, s32[262144]{0:T(1024)S(1)} %fusion.60), kind=kOutput, calls=%fused_computation.10 | convolution fusion | flops 1216348160 | bytes 13633024 | tf_op jit(solution)/shard_map/dot_general | solution.py:194
  73.4 19.1 %copy.151 = f32[2,8,512,512]{3,2,1,0:T(8,128)} copy(f32[2,8,512,512]{3,1,2,0:T(8,128)S(1)} %bitcast.168) | data formatting | bytes 33554432
  92.5 10.6 slice.102
  103.1 12.6 %copy.119 = f32[12,512,512]{1,2,0:T(8,128)} copy(f32[12,512,512]{2,1,0:T(8,128)} %slice.102) | data formatting | bytes 25165824 | tf_op jit(solution)/shard_map/reshape | solution.py:194
  115.9 21.8 %all-to-all-done.1 = bf16[8,256,768]{2,1,0:T(8,128)(2,1)S(1)} async-done(((bf16[8,256,768]{2,1,0:T(8,128)(2,1)}), bf16[8,256,768]{2,1,0:T(8,128)(2,1)S(1)}, u32[]{:S(2)}, u32[]{:S(2)}) %all-to-all-start.1) | async-done | bytes 3145760 | tf_op jit(solution)/shard_map/all_to_all | solution.py:179
  137.7 14.1 %gather_fusion.1 = bf16[1024,768]{1,0:T(8,128)(2,1)} fusion(bf16[8,256,768]{2,1,0:T(8,128)(2,1)S(1)} %all-to-all-done.1, s32[1024]{0:T(1024)S(1)} %bitcast.169), kind=kCustom, calls=%fused_computation.1 | custom fusion | bytes 3153920 | tf_op jit(solution)/shard_map/gather | solution.py:187
  205.5 30.6 %all-gather.10.cloned.1.call-done = bf16[768,3072]{1,0:T(8,128)(2,1)} async-done(((bf16[24,3072]{1,0:T(8,128)(2,1)}), bf16[768,3072]{1,0:T(8,128)(2,1)}) %all-gather.10.cloned.1.call-update) | async-done | bytes 4718608 | tf_op jit(solution)/shard_map/all_gather | solution.py:167
  236.1 10.0 maximum_convert_fusion
  246.1 55.8 %all-gather.12.cloned.1.call-done = bf16[3072,768]{1,0:T(8,128)(2,1)} async-done(((bf16[96,768]{1,0:T(8,128)(2,1)}), bf16[3072,768]{1,0:T(8,128)(2,1)}) %all-gather.12.cloned.1.call-update) | async-done | bytes 4718608 | tf_op jit(solution)/shard_map/all_gather | solution.py:168
  311.7 42.5 %all-gather = f32[32,2,768]{2,1,0:T(2,128)} all-gather(f32[1,2,768]{2,1,0:T(2,128)S(1)} %divide_bitcast_fusion), channel_id=1, replica_groups=mesh['dp'=8,'pair'=4] {'dp','pair'}, dimensions={0}, use_global_device_ids=true | all-gather | bytes 202752 | tf_op jit(solution)/shard_map/all_gather | solution.py:241
  361.5 23.5 %scatter_fusion = f32[64,64]{1,0:T(8,128)S(1)} fusion(f32[64,64]{1,0:T(8,128)S(1)} %fusion.92, s32[448]{0:T(512)S(1)} %reshape.503, f32[448]{0:T(512)S(1)} %reshape.505), kind=kCustom, calls=%fused_computation.5 | custom fusion | flops 448 | bytes 8960 | tf_op jit(solution)/shard_map/transpose(jvp(jit(take_along_axis)))/scatter-add | solution.py:58
  427.2 10.6 multiply_convert_fusion.1
  471.4 26.0 %convolution_convert_fusion.3 = bf16[768,2304]{1,0:T(8,128)(2,1)} fusion(bf16[1024,768]{1,0:T(8,128)(2,1)S(1)} %copy-done.4, f32[768]{0:T(1024)S(1)} %copy-done.51, f32[1024]{0:T(1024)S(1)} %copy-done.49, bf16[512,768]{0,1:T(8,128)(2,1)S(1)} %bitcast.207, bf16[512,768]{0,1:T(8,128)(2,1)S(1)} %bitcast.210, bf16[512,768]{0,1:T(8,128)(2,1)S(1)} %bitcast.202, ...), kind=kOutput, calls=%fused_computation.55 | convolution fusion | flops 3657105408 | bytes 9837568 | tf_op jit(solution)/shard_map/dot_general | solution.py:311
  516.7 14.7 %fusion.35 = (f32[768]{0:T(1024)S(1)}, f32[1024]{0:T(1024)S(1)}, f32[1024,768]{1,0:T(8,128)}) fusion(bf16[1024,768]{1,0:T(8,128)(2,1)S(1)} %copy-done.4, f32[1024]{0:T(1024)S(1)} %copy-done.49, f32[768]{0:T(1024)S(1)} %copy-done.51, bf16[768,2304]{1,0:T(8,128)(2,1)} %all-gather.6.cloned.1.call-done, bf16[512,768]{0,1:T(8,128)(2,1)} %bitcast.206, ...), kind=kOutput, calls=%fused_computation.70 | convolution fusion | flops 3657693440 | bytes 12990464 | tf_op jit(solution)/shard_map/dot_general | solution.py:314
  540.7 84.9 %all_to_all.19 = bf16[8,256,768]{2,1,0:T(8,128)(2,1)S(1)} all-to-all(bf16[8,256,768]{2,1,0:T(8,128)(2,1)} %bitcast.175), channel_id=1, replica_groups=mesh['dp'=8,'pair'=4] {'dp'}, dimensions={0} | all-to-all | bytes 6291456 | tf_op jit(solution)/shard_map/all_to_all | solution.py:324
  625.6 19.6 %scatter_custom_fusion = f32[4016,768]{1,0:T(8,128)} fusion(s32[2048]{0:T(1024)} %bitcast.213, bf16[2048,768]{1,0:T(8,128)(2,1)S(1)} %bitcast.177, f32[]{:T(128)} %constant.63.clone.1), kind=kCustom, calls=%fused_computation.44 | custom fusion | flops 3145728 | bytes 15483392 | tf_op jit(solution)/shard_map/scatter-add | solution.py:325
  677.5 11.9 %copy.152 = bf16[2,8,512,512]{3,1,2,0:T(8,128)(2,1)} copy(bf16[2,8,512,512]{3,2,1,0:T(8,128)(2,1)} %bitcast.172) | data formatting | bytes 16777216
  693.7 11.9 %copy.153 = bf16[2,8,512,512]{3,1,2,0:T(8,128)(2,1)} copy(bf16[2,8,512,512]{3,2,1,0:T(8,128)(2,1)} %bitcast.171) | data formatting | bytes 16777216
  722.6 48.4 %reduce-scatter.9.cloned.1.call-done = bf16[24,3072]{1,0:T(8,128)(2,1)} async-done(((bf16[768,3072]{1,0:T(8,128)(2,1)}), bf16[24,3072]{1,0:T(8,128)(2,1)}) %reduce-scatter.9.cloned.1.call-update) | async-done | bytes 147472 | tf_op jit(solution)/shard_map/reduce_scatter | solution.py:334
  773.2 110.2 %reduce-scatter.11.cloned.1.call-done = bf16[96,768]{1,0:T(8,128)(2,1)} async-done(((bf16[3072,768]{1,0:T(8,128)(2,1)}), bf16[96,768]{1,0:T(8,128)(2,1)}) %reduce-scatter.11.cloned.1.call-update) | async-done | bytes 147472 | tf_op jit(solution)/shard_map/reduce_scatter | solution.py:335
  885.8 117.0 %all-reduce.3.cloned.1.call-done = bf16[4016,768]{1,0:T(8,128)(2,1)} async-done(((bf16[4016,768]{1,0:T(8,128)(2,1)}), bf16[4016,768]{1,0:T(8,128)(2,1)}) %all-reduce.3.cloned.1.call-update) | async-done | bytes 6168592 | tf_op jit(solution)/shard_map/psum | solution.py:330
  1010.6 40.2 %all-reduce = (f32[]{:T(128)}, f32[3,768]{1,0:T(4,128)S(1)}, f32[32,12]{0,1:T(8,128)S(1)}) all-reduce(f32[]{:T(128)S(6)} %add.411, f32[3,768]{1,0:T(4,128)S(1)} %pad_maximum_fusion.3, f32[32,12]{0,1:T(8,128)S(1)} %fusion.59), channel_id=1, replica_groups=mesh['dp'=8,'pair'=4] {'dp','pair'}, use_global_device_ids=true, to_apply=%region_35.36 | all-reduce | flops 2689 | bytes 21512 | tf_op jit(solution)/shard_map/psum | solution.py:341
  1059.2 29.2 %add_subtract_fusion = (f32[4016,768]{1,0:T(8,128)}, f32[4016,768]{1,0:T(8,128)}, f32[4016,768]{1,0:T(8,128)}) fusion(f32[4016,768]{1,0:T(8,128)} %param.33, f32[]{:T(128)S(6)} %min.3, bf16[4016,768]{1,0:T(8,128)(2,1)} %all-reduce.3.cloned.1.call-done, f32[4016,768]{1,0:T(8,128)} %param.34, f32[4016,768]{1,0:T(8,128)} %param.35), kind=kLoop, calls=%fused_computation.37 | loop fusion | flops 49348608 | bytes 80191488 | tf_op jit(solution)/shard_map/sub | solution.py:117
  (321 shorter events, 284.3 us)
Async XLA Ops:
  7.2 146.4 %all-gather.6.cloned.1.call-start = ((), (), s32[]{:S(2)}) async-start(), calls=%async_computation.7 | async-start | bytes 3649536 | tf_op jit(solution)/shard_map/all_gather | solution.py:165
  8.9 191.9 %all-gather.8.cloned.1.call-start = ((), (), s32[]{:S(2)}) async-start(), calls=%async_computation.8 | async-start | bytes 1216512 | tf_op jit(solution)/shard_map/all_gather | solution.py:166
  10.4 225.7 %all-gather.10.cloned.1.call-start = ((), (), s32[]{:S(2)}) async-start(), calls=%async_computation.9 | async-start | bytes 4866048 | tf_op jit(solution)/shard_map/all_gather | solution.py:167
  24.1 14.3 %all-to-all-start = ((s32[8,1,256]{2,1,0:T(1,128)}), s32[8,1,256]{2,1,0:T(1,128)S(1)}, u32[]{:S(2)}, u32[]{:S(2)}) async-start(s32[8,1,256]{2,1,0:T(1,128)} %bitcast.5), calls=%async_computation | async-start | bytes 16384 | tf_op jit(solution)/shard_map/all_to_all | solution.py:177
  31.4 270.5 %all-gather.12.cloned.1.call-start = ((), (), s32[]{:S(2)}) async-start(), calls=%async_computation.10 | async-start | bytes 4866048 | tf_op jit(solution)/shard_map/all_gather | solution.py:168
  53.6 84.0 %all-to-all-start.1 = ((bf16[8,256,768]{2,1,0:T(8,128)(2,1)}), bf16[8,256,768]{2,1,0:T(8,128)(2,1)S(1)}, u32[]{:S(2)}, u32[]{:S(2)}) async-start(bf16[8,256,768]{2,1,0:T(8,128)(2,1)} %select_convert_fusion.1), calls=%async_computation.1 | async-start | bytes 6291456 | tf_op jit(solution)/shard_map/all_to_all | solution.py:179
  59.7 658.3 %reduce-scatter.7.cloned.1.call-start = ((), (), s32[]{:S(2)}) async-start(), calls=%async_computation.12 | async-start | bytes 1216512 | tf_op jit(solution)/shard_map/reduce_scatter | solution.py:333
  456.5 263.1 %reduce-scatter.5.cloned.1.call-start = ((), (), s32[]{:S(2)}) async-start(), calls=%async_computation.11 | async-start | bytes 3649536 | tf_op jit(solution)/shard_map/reduce_scatter | solution.py:332
  497.4 273.6 %reduce-scatter.9.cloned.1.call-start = ((), (), s32[]{:S(2)}) async-start(), calls=%async_computation.13 | async-start | bytes 4866048 | tf_op jit(solution)/shard_map/reduce_scatter | solution.py:334
  507.3 376.1 %reduce-scatter.11.cloned.1.call-start = ((), (), s32[]{:S(2)}) async-start(), calls=%async_computation.14 | async-start | bytes 4866048 | tf_op jit(solution)/shard_map/reduce_scatter | solution.py:335
  516.6 486.2 %all-reduce.3.cloned.1.call-start = ((), (), s32[]{:S(2)}) async-start(), calls=%async_computation.15 | async-start | bytes 12337152 | tf_op jit(solution)/shard_map/psum | solution.py:330
  717.8 336.9 %copy-start.44 = (f32[3,768]{1,0:T(4,128)S(1)}, f32[3,768]{1,0:T(4,128)}, u32[]{:S(2)}) copy-start(f32[3,768]{1,0:T(4,128)} %param.48) | copy-start | bytes 27652
  717.8 336.9 %copy-start.53 = (f32[3,768]{1,0:T(4,128)S(1)}, f32[3,768]{1,0:T(4,128)}, u32[]{:S(2)}) copy-start(f32[3,768]{1,0:T(4,128)} %param.49) | copy-start | bytes 27652
  717.9 336.9 %copy-start.54 = (f32[3,768]{1,0:T(4,128)S(1)}, f32[3,768]{1,0:T(4,128)}, u32[]{:S(2)}) copy-start(f32[3,768]{1,0:T(4,128)} %param.50) | copy-start | bytes 27652
  717.9 337.5 %copy-start.32 = (f32[24,768]{1,0:T(8,128)S(1)}, f32[24,768]{1,0:T(8,128)}, u32[]{:S(2)}) copy-start(f32[24,768]{1,0:T(8,128)} %param.39) | copy-start | bytes 221188
  717.9 337.5 %copy-start.41 = (f32[24,768]{1,0:T(8,128)S(1)}, f32[24,768]{1,0:T(8,128)}, u32[]{:S(2)}) copy-start(f32[24,768]{1,0:T(8,128)} %param.40) | copy-start | bytes 221188
  717.9 337.5 %copy-start.42 = (f32[24,768]{1,0:T(8,128)S(1)}, f32[24,768]{1,0:T(8,128)}, u32[]{:S(2)}) copy-start(f32[24,768]{1,0:T(8,128)} %param.41) | copy-start | bytes 221188
  717.9 338.2 %copy-start.24 = (f32[24,2304]{1,0:T(8,128)S(1)}, f32[24,2304]{1,0:T(8,128)}, u32[]{:S(2)}) copy-start(f32[24,2304]{1,0:T(8,128)} %param.36) | copy-start | bytes 663556
  717.9 338.2 %copy-start.37 = (f32[24,2304]{1,0:T(8,128)S(1)}, f32[24,2304]{1,0:T(8,128)}, u32[]{:S(2)}) copy-start(f32[24,2304]{1,0:T(8,128)} %param.37) | copy-start | bytes 663556
  717.9 338.2 %copy-start.38 = (f32[24,2304]{1,0:T(8,128)S(1)}, f32[24,2304]{1,0:T(8,128)}, u32[]{:S(2)}) copy-start(f32[24,2304]{1,0:T(8,128)} %param.38) | copy-start | bytes 663556
  717.9 339.1 %copy-start.22 = (f32[96,768]{1,0:T(8,128)S(1)}, f32[96,768]{1,0:T(8,128)}, u32[]{:S(2)}) copy-start(f32[96,768]{1,0:T(8,128)} %param.45) | copy-start | bytes 884740
  718.0 339.1 %copy-start.33 = (f32[96,768]{1,0:T(8,128)S(1)}, f32[96,768]{1,0:T(8,128)}, u32[]{:S(2)}) copy-start(f32[96,768]{1,0:T(8,128)} %param.46) | copy-start | bytes 884740
  718.0 339.1 %copy-start.34 = (f32[96,768]{1,0:T(8,128)S(1)}, f32[96,768]{1,0:T(8,128)}, u32[]{:S(2)}) copy-start(f32[96,768]{1,0:T(8,128)} %param.47) | copy-start | bytes 884740
  718.0 337.4 %copy-start.39 = (bf16[24,768]{1,0:T(8,128)(2,1)S(1)}, bf16[24,768]{1,0:T(8,128)(2,1)}, u32[]{:S(2)}) copy-start(bf16[24,768]{1,0:T(8,128)(2,1)} %reduce-scatter.7.cloned.1.call-done) | copy-start | bytes 110596
  (67 other events, 2723.1 us)
Sparse Core Ops, SparseCore 0:
  11.5 81.4 all-gather.5
  96.5 73.5 all-gather.7
  173.5 62.5 all-gather.9
  239.4 62.4 all-gather.11
  456.6 92.4 reduce-scatter.6
  554.4 105.1 reduce-scatter.4
  665.0 105.8 reduce-scatter.8
  777.3 106.0 reduce-scatter.10
  885.8 116.9 all-reduce.2

commit v2 on v0

--- a/solution.py
+++ b/solution.py
@@ -1,8 +1,11 @@
+import functools
 import math
 
 import jax
 import jax.numpy as jnp
 from jax import lax
+from jax.experimental import pallas as pl
+from jax.experimental.pallas import tpu as pltpu
 from jax.sharding import PartitionSpec as P
 
 REACH = 128
@@ -118,7 +121,466 @@
     return (weight_new, first_new, second_new)
 
 
-def local(
+MESH = pl.DeviceIdType.MESH
+VMEM_LIMIT = 64 * 1024 * 1024 - 65536
+ANY = pl.BlockSpec(memory_space=pl.ANY)
+VM = pl.BlockSpec(memory_space=pltpu.VMEM)
+
+
+def place(index, n_pair):
+    return {"dp": index // n_pair, "pair": lax.rem(index, n_pair)}
+
+
+def remote(src, dst, send, recv, target):
+    return pltpu.make_async_remote_copy(
+        src, dst, send, recv, device_id=target, device_id_type=MESH
+    )
+
+
+def greet(targets):
+    sem = pltpu.get_barrier_semaphore()
+    for target in targets:
+        pl.semaphore_signal(sem, inc=1, device_id=target, device_id_type=MESH)
+    pl.semaphore_wait(sem, len(targets))
+
+
+def my_index(n_pair):
+    return lax.axis_index("dp") * n_pair + lax.axis_index("pair")
+
+
+def bit_order(n_dp, n_pair, color):
+    dp_bits, pair_bits = (n_dp - 1).bit_length(), (n_pair - 1).bit_length()
+    high = list(reversed(range(pair_bits + 1, pair_bits + dp_bits))) + [pair_bits]
+    side = list(reversed(range(1, pair_bits)))
+    return high + side if color == 0 else side + high
+
+
+def offset(order, position):
+    return sum(((position >> step) & 1) << bit for step, bit in enumerate(order))
+
+
+def scatter_kernel(n_dp, n_pair, pieces, n_in, *refs):
+    k = len(pieces)
+    ins, outs = refs[:n_in], refs[n_in : 2 * n_in]
+    accs = refs[2 * n_in : 2 * n_in + k]
+    gots = refs[2 * n_in + k : 2 * n_in + 2 * k]
+    lsem, csend, crecv, send, recv = refs[2 * n_in + 2 * k :]
+    me = my_index(n_pair)
+    n = n_dp * n_pair
+    steps = (n - 1).bit_length() - 1
+    half = 1 << steps
+    orders = [bit_order(n_dp, n_pair, color) for _, _, _, color in pieces]
+    greet([place(me ^ (1 << bit), n_pair) for bit in range(steps + 1)])
+
+    def source(a, block):
+        which, low, high, _ = pieces[a]
+        return ins[which].at[block, :, pl.ds(low, high - low)]
+
+    def core_send(a, upper):
+        lo = half // 2 if upper else 0
+        for p in range(lo, lo + half // 2):
+            block = me ^ (offset(orders[a], p) + 1)
+            remote(source(a, block), gots[a].at[p], csend.at[a, upper], crecv.at[a, upper], place(me ^ 1, n_pair)).start()
+
+    def load(a):
+        for p in range(half):
+            pltpu.make_async_copy(source(a, me ^ offset(orders[a], p)), accs[a].at[p], lsem.at[a]).start()
+
+    def core_copy(a, upper):
+        lo = half // 2 if upper else 0
+        part = pl.ds(lo, half // 2)
+        return remote(gots[a].at[part], gots[a].at[part], csend.at[a, upper], crecv.at[a, upper], place(me ^ 1, n_pair))
+
+    def add(a, lo, count, base):
+        def body(j, carry):
+            accs[a][lo + j] = (
+                accs[a][lo + j].astype(jnp.float32) + gots[a][base + lo + j].astype(jnp.float32)
+            ).astype(jnp.bfloat16)
+            return carry
+        lax.fori_loop(0, count, body, 0)
+
+    def base_of(s):
+        return half + half - (2 << s)
+
+    def hop(a, s):
+        return remote(
+            accs[a].at[pl.ds(1 << s, 1 << s)], gots[a].at[pl.ds(base_of(s), 1 << s)],
+            send.at[a, s], recv.at[a, s], place(me ^ (1 << orders[a][s]), n_pair),
+        )
+
+    for upper in (1, 0):
+        for a in range(k):
+            core_send(a, upper)
+            if upper:
+                load(a)
+    for a in range(k):
+        pltpu.make_async_copy(accs[a], accs[a], lsem.at[a]).wait()
+        core_copy(a, 1).wait_recv()
+        add(a, half // 2, half // 2, 0)
+        hop(a, steps - 1).start()
+    for a in range(k):
+        core_copy(a, 0).wait_recv()
+        add(a, 0, half // 2, 0)
+    for s in reversed(range(steps)):
+        for a in range(k):
+            hop(a, s).wait_recv()
+            if s:
+                mid = 1 << (s - 1)
+                add(a, mid, mid, base_of(s))
+                hop(a, s - 1).start()
+                add(a, 0, mid, base_of(s))
+            else:
+                which, low, high, _ = pieces[a]
+                outs[which][:, low:high] = accs[a][0].astype(jnp.float32) + gots[a][
+                    base_of(0)
+                ].astype(jnp.float32)
+    for a in range(k):
+        core_copy(a, 1).wait_send()
+        core_copy(a, 0).wait_send()
+        for s in range(steps):
+            hop(a, s).wait_send()
+
+
+def scatter_all(grads, pieces, n_dp, n_pair, cid):
+    n, k = n_dp * n_pair, len(pieces)
+    steps = (n - 1).bit_length() - 1
+    half = n // 2
+    shape = lambda p, lead: (lead, grads[p[0]].shape[1], p[2] - p[1])
+    return pl.pallas_call(
+        functools.partial(scatter_kernel, n_dp, n_pair, pieces, len(grads)),
+        out_shape=[jax.ShapeDtypeStruct(g.shape[1:], jnp.float32) for g in grads],
+        in_specs=[ANY] * len(grads),
+        out_specs=[VM] * len(grads),
+        scratch_shapes=[pltpu.VMEM(shape(p, half), jnp.bfloat16) for p in pieces]
+        + [pltpu.VMEM(shape(p, 2 * half - 1), jnp.bfloat16) for p in pieces]
+        + [
+            pltpu.SemaphoreType.DMA((k,)),
+            pltpu.SemaphoreType.DMA((k, 2)),
+            pltpu.SemaphoreType.DMA((k, 2)),
+            pltpu.SemaphoreType.DMA((k, steps)),
+            pltpu.SemaphoreType.DMA((k, steps)),
+        ],
+        compiler_params=pltpu.CompilerParams(
+            collective_id=cid, has_side_effects=True, vmem_limit_bytes=VMEM_LIMIT
+        ),
+        name="weight_grads_sum",
+    )(*grads)
+
+
+def spread(n, n_pair, block, everyone, send, recv, own_sem):
+    me = my_index(n_pair)
+    sem = pltpu.get_barrier_semaphore()
+
+    def hello(k, carry):
+        pl.semaphore_signal(sem, inc=1, device_id=place(me ^ k, n_pair), device_id_type=MESH)
+        return carry
+
+    lax.fori_loop(1, n, hello, 0)
+    own = pltpu.make_async_copy(block, everyone.at[me], own_sem)
+    own.start()
+    pl.semaphore_wait(sem, n - 1)
+
+    def go(k, carry):
+        remote(block, everyone.at[me], send.at[k], recv.at[k], place(me ^ k, n_pair)).start()
+        return carry
+
+    lax.fori_loop(1, n, go, 0)
+    own.wait()
+
+    def done(k, carry):
+        remote(block, everyone.at[me ^ k], send.at[k], recv.at[k], place(me ^ k, n_pair)).wait()
+        return carry
+
+    lax.fori_loop(1, n, done, 0)
+
+
+def total_kernel(n, n_pair, x_ref, o_ref, everyone, send, recv, own_sem):
+    spread(n, n_pair, x_ref, everyone, send, recv, own_sem)
+    def add(j, total):
+        return total + everyone[j]
+    o_ref[...] = lax.fori_loop(1, n, add, everyone[0])
+
+
+def small_total(x, n_dp, n_pair, cid):
+    n = n_dp * n_pair
+    return pl.pallas_call(
+        functools.partial(total_kernel, n, n_pair),
+        out_shape=jax.ShapeDtypeStruct(x.shape, x.dtype),
+        in_specs=[VM], out_specs=VM,
+        scratch_shapes=[pltpu.VMEM((n,) + x.shape, x.dtype), pltpu.SemaphoreType.DMA((n,)), pltpu.SemaphoreType.DMA((n,)), pltpu.SemaphoreType.DMA],
+        compiler_params=pltpu.CompilerParams(collective_id=cid, has_side_effects=True),
+        name="small_total",
+    )(x)
+
+
+def loss_kernel(n, n_pair, docs, x_ref, pos_ref, neg_ref, count_ref, loss_ref, grad_ref, everyone, grads, send, recv, own_sem):
+    spread(n, n_pair, x_ref, everyone, send, recv, own_sem)
+    total = n * docs
+    width = x_ref.shape[1]
+    pooled = everyone[...].reshape(total, width)
+    inverse = lax.rsqrt(jnp.sum(pooled * pooled, axis=1, keepdims=True) + 1e-06)
+    unit = pooled * inverse
+    similar = 20.0 * lax.dot_general(unit, unit, (((1,), (1,)), ((), ())), precision=HIGHEST, preferred_element_type=jnp.float32)
+    columns = lax.broadcasted_iota(jnp.int32, (total, total), 1)
+    is_pos = columns == pos_ref[...]
+    chosen = jnp.sum(jnp.where(is_pos, similar, 0.0), axis=1, keepdims=True)
+    counts = count_ref[...]
+    weight = 1.0 / (counts.astype(jnp.float32) * total)
+    loss_rows = jnp.zeros((total, 1), jnp.float32)
+    grad_similar = jnp.zeros((total, total), jnp.float32)
+    pulled = jnp.zeros((total, 1), jnp.float32)
+    for slot in range(neg_ref.shape[1]):
+        is_neg = columns == neg_ref[:, slot : slot + 1]
+        against = jnp.sum(jnp.where(is_neg, similar, 0.0), axis=1, keepdims=True)
+        value = 1.0 - chosen + against
+        used = slot < counts
+        soft = jnp.maximum(value, 0.0) + jnp.log1p(jnp.exp(-jnp.abs(value)))
+        loss_rows = loss_rows + jnp.where(used, soft, 0.0)
+        slope = jnp.where(used, weight / (1.0 + jnp.exp(-value)), 0.0)
+        grad_similar = grad_similar + jnp.where(is_neg, slope, 0.0)
+        pulled = pulled + slope
+    grad_similar = grad_similar - jnp.where(is_pos, pulled, 0.0)
+    loss_ref[...] = jnp.sum(loss_rows * weight, axis=0, keepdims=True)
+    dims = (((1,), (0,)), ((), ()))
+    grad_unit = lax.dot_general(grad_similar, unit, dims, precision=HIGHEST, preferred_element_type=jnp.float32)
+    grad_unit = grad_unit + lax.dot_general(grad_similar, unit, (((0,), (0,)), ((), ())), precision=HIGHEST, preferred_element_type=jnp.float32)
+    grad_unit = 20.0 * grad_unit
+    inner = jnp.sum(grad_unit * unit, axis=1, keepdims=True)
+    grads[...] = (inverse * (grad_unit - unit * inner)).reshape(n, docs, width)
+    grad_ref[...] = grads[my_index(n_pair)]
+
+
+def pooled_loss(pooled, positives, negatives, counts, n_dp, n_pair, cid):
+    n = n_dp * n_pair
+    docs, width = pooled.shape
+    return pl.pallas_call(
+        functools.partial(loss_kernel, n, n_pair, docs),
+        out_shape=[jax.ShapeDtypeStruct((1, 1), jnp.float32), jax.ShapeDtypeStruct(pooled.shape, jnp.float32)],
+        in_specs=[VM] * 4, out_specs=[VM] * 2,
+        scratch_shapes=[pltpu.VMEM((n,) + pooled.shape, jnp.float32), pltpu.VMEM((n,) + pooled.shape, jnp.float32),
+            pltpu.SemaphoreType.DMA((n,)), pltpu.SemaphoreType.DMA((n,)), pltpu.SemaphoreType.DMA],
+        compiler_params=pltpu.CompilerParams(collective_id=cid, has_side_effects=True),
+        name="pooled_loss",
+    )(pooled, positives[:, None], negatives, counts[:, None])
+
+
+def table_kernel(n_pair, rows, chunk, arr_ref, ask_ref, out_ref, sq_ref, hot, stage, part, got_c, out_x, got_x, fin, fin_other,
+                 csend, crecv, xsend, xrecv, fsend, frecv, wsem):
+    me_dp, me_pair = lax.axis_index("dp"), lax.axis_index("pair")
+    core = lax.rem(me_pair, 2)
+    partner = {"dp": me_dp, "pair": me_pair ^ 1}
+    across = {"dp": me_dp, "pair": me_pair ^ 2}
+    count = rows // 2 // chunk
+    greet([partner, across])
+    slots = ask_ref.shape[1]
+
+    def summed(base):
+        ids = lax.broadcasted_iota(jnp.int32, (chunk, slots), 0) + base
+        hot[...] = jnp.where(ids == ask_ref[...], 1.0, 0.0).astype(jnp.bfloat16)
+        return jnp.dot(hot[...], arr_ref[...], preferred_element_type=jnp.float32)
+
+    def c_copy(i):
+        return remote(stage.at[i], got_c.at[i], csend.at[i], crecv.at[i], partner)
+
+    def x_copy(i):
+        return remote(out_x.at[i], got_x.at[i], xsend.at[i], xrecv.at[i], across)
+
+    def f_copy(i):
+        return remote(fin.at[i], fin_other.at[i], fsend.at[i], frecv.at[i], partner)
+
+    for i in range(count):
+        stage[i] = summed((1 - core) * (rows // 2) + i * chunk).astype(jnp.bfloat16)
+        c_copy(i).start()
+    for i in range(count):
+        part[...] = summed(core * (rows // 2) + i * chunk)
+        c_copy(i).wait_recv()
+        out_x[i] = (part[...] + got_c[i].astype(jnp.float32)).astype(jnp.bfloat16)
+        x_copy(i).start()
+    square = jnp.zeros((1, 1), jnp.float32)
+    for i in range(count):
+        x_copy(i).wait_recv()
+        value = (out_x[i].astype(jnp.float32) + got_x[i].astype(jnp.float32)).astype(jnp.bfloat16)
+        fin[i] = value
+        f_copy(i).start()
+        pltpu.make_async_copy(fin.at[i], out_ref.at[pl.ds(core * (rows // 2) + i * chunk, chunk)], wsem.at[0]).start()
+        wide = value.astype(jnp.float32)
+        square = square + jnp.sum(jnp.sum(wide * wide, axis=0, keepdims=True), axis=1, keepdims=True)
+    sq_ref[...] = jnp.where(me_pair < 2, square, 0.0)
+    for i in range(count):
+        f_copy(i).wait_recv()
+        pltpu.make_async_copy(fin_other.at[i], out_ref.at[pl.ds((1 - core) * (rows // 2) + i * chunk, chunk)], wsem.at[1]).start()
+    for i in range(count):
+        c_copy(i).wait_send()
+        x_copy(i).wait_send()
+        f_copy(i).wait_send()
+    pltpu.make_async_copy(fin, fin, wsem.at[0]).wait()
+    pltpu.make_async_copy(fin_other, fin_other, wsem.at[1]).wait()
+
+
+def table_total(arrived, asked, rows, n_pair, cid):
+    chunk, width = 512, arrived.shape[1]
+    count = rows // 2 // chunk
+    box = pltpu.VMEM((count, chunk, width), jnp.bfloat16)
+    sem = pltpu.SemaphoreType.DMA((count,))
+    return pl.pallas_call(
+        functools.partial(table_kernel, n_pair, rows, chunk),
+        out_shape=[jax.ShapeDtypeStruct((rows, width), jnp.bfloat16), jax.ShapeDtypeStruct((1, 1), jnp.float32)],
+        in_specs=[VM, VM], out_specs=[ANY, VM],
+        scratch_shapes=[pltpu.VMEM((chunk, asked.shape[1]), jnp.bfloat16), box, pltpu.VMEM((chunk, width), jnp.float32), box, box, box, box, box,
+            sem, sem, sem, sem, sem, sem, pltpu.SemaphoreType.DMA((2,))],
+        compiler_params=pltpu.CompilerParams(collective_id=cid, has_side_effects=True, vmem_limit_bytes=VMEM_LIMIT),
+        name="table_total",
+    )(arrived, asked)
+
+
+def gather_kernel(n_dp, n_pair, pieces, n_in, *refs):
+    k = len(pieces)
+    ins, outs = refs[:n_in], refs[n_in : 2 * n_in]
+    bufs = refs[2 * n_in : 2 * n_in + k]
+    send, recv, csend, crecv, wsem, isem = refs[2 * n_in + k :]
+    me = my_index(n_pair)
+    steps = (n_dp * n_pair - 1).bit_length() - 1
+    half = 1 << steps
+    orders = [bit_order(n_dp, n_pair, color) for _, _, _, color in pieces]
+
+    def load(a):
+        which, low, high, _ = pieces[a]
+        return pltpu.make_async_copy(
+            ins[which].at[:, pl.ds(low, high - low)], bufs[a].at[0], isem.at[a]
+        )
+
+    for a in range(k):
+        load(a).start()
+    greet([place(me ^ (1 << bit), n_pair) for bit in range(steps + 1)])
+
+    def write_out(a, lo, count, core):
+        which, low, high, _ = pieces[a]
+        for p in range(lo, lo + count):
+            block = me ^ (offset(orders[a], p) + core)
+            pltpu.make_async_copy(
+                bufs[a].at[p + core * half],
+                outs[which].at[block, :, pl.ds(low, high - low)],
+                wsem.at[a],
+            ).start()
+
+    def forward(a, s):
+        lo, count = (0, 1) if s == 0 else (1 << (s - 1), 1 << (s - 1))
+        return remote(
+            bufs[a].at[pl.ds(lo, count)],
+            bufs[a].at[pl.ds(half + lo, count)],
+            csend.at[a, s],
+            crecv.at[a, s],
+            place(me ^ 1, n_pair),
+        )
+
+    def hop(a, s):
+        return remote(
+            bufs[a].at[pl.ds(0, 1 << s)],
+            bufs[a].at[pl.ds(1 << s, 1 << s)],
+            send.at[a, s],
+            recv.at[a, s],
+            place(me ^ (1 << orders[a][s]), n_pair),
+        )
+
+    for a in range(k):
+        load(a).wait()
+        hop(a, 0).start()
+    for a in range(k):
+        forward(a, 0).start()
+        write_out(a, 0, 1, 0)
+    for s in range(steps):
+        for a in range(k):
+            hop(a, s).wait_recv()
+            if s + 1 < steps:
+                hop(a, s + 1).start()
+            forward(a, s + 1).start()
+            write_out(a, 1 << s, 1 << s, 0)
+        for a in range(k):
+            forward(a, s).wait_recv()
+            lo, count = (0, 1) if s == 0 else (1 << (s - 1), 1 << (s - 1))
+            write_out(a, lo, count, 1)
+    for a in range(k):
+        forward(a, steps).wait_recv()
+        write_out(a, half // 2, half // 2, 1)
+    for a in range(k):
+        for s in range(steps):
+            hop(a, s).wait_send()
+        for s in range(steps + 1):
+            forward(a, s).wait_send()
+        pltpu.make_async_copy(bufs[a], bufs[a], wsem.at[a]).wait()
+
+
+def gather_all(shards, pieces, n_dp, n_pair, cid):
+    n, k = n_dp * n_pair, len(pieces)
+    steps = (n - 1).bit_length() - 1
+    return pl.pallas_call(
+        functools.partial(gather_kernel, n_dp, n_pair, pieces, len(shards)),
+        out_shape=[jax.ShapeDtypeStruct((n,) + s.shape, s.dtype) for s in shards],
+        in_specs=[ANY] * len(shards),
+        out_specs=[ANY] * len(shards),
+        scratch_shapes=[
+            pltpu.VMEM((n, shards[p[0]].shape[0], p[2] - p[1]), jnp.bfloat16) for p in pieces
+        ]
+        + [
+            pltpu.SemaphoreType.DMA((k, steps)),
+            pltpu.SemaphoreType.DMA((k, steps)),
+            pltpu.SemaphoreType.DMA((k, steps + 1)),
+            pltpu.SemaphoreType.DMA((k, steps + 1)),
+            pltpu.SemaphoreType.DMA((k,)),
+            pltpu.SemaphoreType.DMA((k,)),
+        ],
+        compiler_params=pltpu.CompilerParams(
+            collective_id=cid, has_side_effects=True, vmem_limit_bytes=VMEM_LIMIT
+        ),
+        name="weights_gather",
+    )(*shards)
+
+def exchange_kernel(n_dp, x_ref, o_ref, send, recv, lsem):
+    me = lax.axis_index("dp"); pr = lax.axis_index("pair")
+    sem = pltpu.get_barrier_semaphore()
+    def greet(k, _):
+        pl.semaphore_signal(sem, inc=1, device_id={"dp": lax.rem(me + k, n_dp), "pair": pr}, device_id_type=MESH)
+        return 0
+    lax.fori_loop(1, n_dp, greet, 0)
+    pl.semaphore_wait(sem, n_dp - 1)
+    own = pltpu.make_async_copy(x_ref.at[me], o_ref.at[me], lsem); own.start()
+    def cp(k):
+        dst = lax.rem(me + k, n_dp)
+        return pltpu.make_async_remote_copy(x_ref.at[dst], o_ref.at[me], send.at[k], recv.at[k],
+            device_id={"dp": dst, "pair": pr}, device_id_type=MESH)
+    def go(k, _):
+        cp(k).start(); return 0
+    lax.fori_loop(1, n_dp, go, 0)
+    def done(k, _):
+        src = lax.rem(me + n_dp - k, n_dp)
+        c = pltpu.make_async_remote_copy(x_ref.at[me], o_ref.at[src], send.at[k], recv.at[k],
+            device_id={"dp": src, "pair": pr}, device_id_type=MESH)
+        c.wait(); return 0
+    own.wait()
+    lax.fori_loop(1, n_dp, done, 0)
+
+def exchange(x, n_dp, cid):
+    return pl.pallas_call(
+        functools.partial(exchange_kernel, n_dp),
+        out_shape=jax.ShapeDtypeStruct(x.shape, x.dtype),
+        in_specs=[pl.BlockSpec(memory_space=pltpu.VMEM)], out_specs=pl.BlockSpec(memory_space=pltpu.VMEM),
+        scratch_shapes=[pltpu.SemaphoreType.DMA((n_dp,)), pltpu.SemaphoreType.DMA((n_dp,)), pltpu.SemaphoreType.DMA],
+        compiler_params=pltpu.CompilerParams(collective_id=cid, has_side_effects=True, vmem_limit_bytes=VMEM_LIMIT),
+        name="rows_exchange",
+    )(x)
+
+def weight_pieces(widths):
+    qkv_cols, out_cols, in_cols, down_cols = widths
+    cut = down_cols * 2 // 3 // 128 * 128
+    return [
+        (2, 0, in_cols, 0),
+        (0, 0, qkv_cols, 1),
+        (1, 0, out_cols, 0),
+        (3, 0, cut, 0),
+        (3, cut, down_cols, 1),
+    ]
+
+def local_plain(
     token_owner,
     token_row,
     lengths,
@@ -377,6 +839,289 @@
     )
 
 
+def local_fast(
+    token_owner,
+    token_row,
+    lengths,
+    positives,
+    negatives,
+    neg_counts,
+    embed_table,
+    embed_first,
+    embed_second,
+    qkv_weight,
+    qkv_first,
+    qkv_second,
+    out_weight,
+    out_first,
+    out_second,
+    in_weight,
+    in_first,
+    in_second,
+    down_weight,
+    down_first,
+    down_second,
+    norm_gains,
+    gains_first,
+    gains_second,
+    position_bias,
+    bias_first,
+    bias_second,
+):
+    doc_count = lengths.shape[0]
+    seq_len = token_row.shape[1]
+    model_width = embed_table.shape[1]
+    head_count = position_bias.shape[1]
+    bucket_count = position_bias.shape[0]
+    tok_total = doc_count * seq_len
+    owners = lax.axis_size("dp")
+    capacity = max(2, 2 * tok_total // owners)
+    low_mats = (
+        qkv_weight.astype(jnp.bfloat16),
+        out_weight.astype(jnp.bfloat16),
+        in_weight.astype(jnp.bfloat16),
+        down_weight.astype(jnp.bfloat16),
+    )
+    holders = lax.axis_size("pair")
+    pieces = weight_pieces([low.shape[1] for low in low_mats])
+    qkv_full, out_full, in_full, down_full = (
+        full.reshape(-1, full.shape[2])
+        for full in gather_all(low_mats, pieces, owners, holders, 1)
+    )
+    tok_owner = token_owner.reshape(-1)
+    tok_row = token_row.reshape(-1)
+    owner_hits = (tok_owner[:, None] == jnp.arange(owners, dtype=jnp.int32)[None, :]).astype(
+        jnp.int32
+    )
+    slot_rank = jnp.sum((jnp.cumsum(owner_hits, axis=0) - 1) * owner_hits, axis=1)
+    requests = jnp.zeros((owners, capacity), jnp.int32).at[tok_owner, slot_rank].set(tok_row)
+    asked_rows = lax.all_to_all(requests, "dp", split_axis=0, concat_axis=0, tiled=True)
+    looked = jnp.take(embed_table, asked_rows.reshape(-1), axis=0).astype(jnp.bfloat16)
+    answer = exchange(looked.reshape(asked_rows.shape + (model_width,)), owners, 2)
+    replies, asked_rows = (answer, asked_rows)
+    embedded = replies[tok_owner, slot_rank].astype(jnp.float32)
+    positions = jnp.arange(seq_len)
+    live = positions[None, :] < lengths[:, None]
+    pair_buckets = bucket_of(
+        (positions[None, :] - positions[:, None]).reshape(-1), bucket_count, REACH
+    )
+    pair_hits = (jnp.arange(bucket_count)[:, None] == pair_buckets[None, :]).astype(jnp.float32)
+    bias_full = jnp.dot(position_bias.T, pair_hits, precision=HIGHEST).reshape(
+        head_count, seq_len, seq_len
+    )
+    bucket_map = pair_hits.astype(jnp.bfloat16)
+
+    def split_doc(source, doc_index):
+        doc_rows = source[doc_index * seq_len : (doc_index + 1) * seq_len]
+        return tuple(
+            (
+                doc_rows[:, member * model_width : (member + 1) * model_width].reshape(
+                    seq_len, head_count, -1
+                )
+                for member in range(3)
+            )
+        )
+
+    normed_one, inverse_one = rms_forward(embedded, norm_gains[0])
+    normed_one = normed_one.astype(jnp.bfloat16)
+    qkv_rows = jnp.dot(normed_one, qkv_full, preferred_element_type=jnp.float32).astype(
+        jnp.bfloat16
+    )
+    attended_parts = []
+    logsum_parts = []
+    for doc_index in range(doc_count):
+        query_heads, key_heads, value_heads = split_doc(qkv_rows, doc_index)
+        doc_out, logsum = attend_forward(
+            query_heads, key_heads, value_heads, bias_full, live[doc_index]
+        )
+        attended_parts.append(doc_out.reshape(seq_len, model_width))
+        logsum_parts.append(logsum)
+    attended = jnp.concatenate(attended_parts, axis=0).astype(jnp.bfloat16)
+    residual = embedded + jnp.dot(attended, out_full, preferred_element_type=jnp.float32)
+    normed_two, inverse_two = rms_forward(residual, norm_gains[1])
+    normed_two = normed_two.astype(jnp.bfloat16)
+    hidden = jax.nn.relu(jnp.dot(normed_two, in_full, preferred_element_type=jnp.float32)).astype(
+        jnp.bfloat16
+    )
+    output_rows = residual + jnp.dot(hidden, down_full, preferred_element_type=jnp.float32)
+    normed_three, inverse_three = rms_forward(output_rows, norm_gains[2])
+    live_rows = live.reshape(-1, 1)
+    length_float = lengths.astype(jnp.float32)
+    pooled_local = (
+        jnp.sum(
+            jnp.where(live_rows, normed_three, 0.0).reshape(doc_count, seq_len, model_width), axis=1
+        )
+        / length_float[:, None]
+    )
+    loss_cell, grad_pooled = pooled_loss(
+        pooled_local, positives, negatives, neg_counts, owners, holders, 3
+    )
+    loss_value = loss_cell[0, 0]
+    grad_three = jnp.where(
+        live_rows, jnp.repeat(grad_pooled / length_float[:, None], seq_len, axis=0), 0.0
+    )
+    qkv_back, out_back, in_back, down_back = (qkv_full, out_full, in_full, down_full)
+    grad_output, gain_three = rms_backward(output_rows, inverse_three, norm_gains[2], grad_three)
+    grad_branch = grad_output.astype(jnp.bfloat16)
+    grad_down = lax.dot_general(
+        hidden, grad_branch, CONTRACT_ROWS, preferred_element_type=jnp.float32
+    )
+    grad_hidden = lax.dot_general(
+        grad_branch, down_back, CONTRACT_COLS, preferred_element_type=jnp.float32
+    )
+    grad_pre = jnp.where(hidden > 0, grad_hidden, 0.0).astype(jnp.bfloat16)
+    grad_in = lax.dot_general(
+        normed_two, grad_pre, CONTRACT_ROWS, preferred_element_type=jnp.float32
+    )
+    grad_normed_two = lax.dot_general(
+        grad_pre, in_back, CONTRACT_COLS, preferred_element_type=jnp.float32
+    )
+    grad_res_part, gain_two = rms_backward(residual, inverse_two, norm_gains[1], grad_normed_two)
+    grad_residual = grad_output + grad_res_part
+    grad_attn_branch = grad_residual.astype(jnp.bfloat16)
+    grad_out = lax.dot_general(
+        attended, grad_attn_branch, CONTRACT_ROWS, preferred_element_type=jnp.float32
+    )
+    grad_attended = lax.dot_general(
+        grad_attn_branch, out_back, CONTRACT_COLS, preferred_element_type=jnp.float32
+    ).astype(jnp.bfloat16)
+    grad_qkv_parts = []
+    bias_grad_heads = jnp.zeros((head_count, bucket_count), jnp.float32)
+    for doc_index in range(doc_count):
+        query_heads, key_heads, value_heads = split_doc(qkv_rows, doc_index)
+        grad_doc = grad_attended[doc_index * seq_len : (doc_index + 1) * seq_len].reshape(
+            seq_len, head_count, -1
+        )
+        grad_query, grad_key, grad_value, grad_low = attend_backward(
+            query_heads,
+            key_heads,
+            value_heads,
+            bias_full,
+            live[doc_index],
+            logsum_parts[doc_index],
+            grad_doc,
+        )
+        grad_qkv_parts.append(
+            jnp.concatenate(
+                [
+                    grad_query.reshape(seq_len, model_width),
+                    grad_key.reshape(seq_len, model_width),
+                    grad_value.reshape(seq_len, model_width),
+                ],
+                axis=1,
+            )
+        )
+        bias_grad_heads = bias_grad_heads + lax.dot_general(
+            grad_low.reshape(head_count, -1),
+            bucket_map,
+            CONTRACT_COLS,
+            preferred_element_type=jnp.float32,
+        )
+    bias_grad_local = bias_grad_heads.T
+    grad_qkv_rows = jnp.concatenate(grad_qkv_parts, axis=0).astype(jnp.bfloat16)
+    grad_qkv = lax.dot_general(
+        normed_one, grad_qkv_rows, CONTRACT_ROWS, preferred_element_type=jnp.float32
+    )
+    grad_normed_one = lax.dot_general(
+        grad_qkv_rows, qkv_back, CONTRACT_COLS, preferred_element_type=jnp.float32
+    )
+    grad_emb_part, gain_one = rms_backward(embedded, inverse_one, norm_gains[0], grad_normed_one)
+    grad_embedded = grad_residual + grad_emb_part
+    sendback = (
+        jnp.zeros((owners, capacity, model_width), jnp.bfloat16)
+        .at[tok_owner, slot_rank]
+        .set(grad_embedded.astype(jnp.bfloat16))
+    )
+    arrived = exchange(sendback, owners, 4)
+    table_rows = embed_table.shape[0]
+    table_grad, table_square = table_total(
+        arrived.reshape(-1, model_width),
+        asked_rows.reshape(1, -1),
+        -(-table_rows // 1024) * 1024,
+        holders,
+        5,
+    )
+    table_grad = table_grad[:table_rows].astype(jnp.float32)
+    parts = owners * holders
+    weight_grads = scatter_all(
+        [
+            grad.astype(jnp.bfloat16).reshape(parts, -1, grad.shape[1])
+            for grad in (grad_qkv, grad_out, grad_in, grad_down)
+        ],
+        pieces,
+        owners,
+        holders,
+        6,
+    )
+    square_part = table_square[0, 0] + jnp.sum(
+        jnp.stack([jnp.sum(grad_piece * grad_piece) for grad_piece in weight_grads])
+    )
+    small = jnp.concatenate(
+        [
+            jnp.stack([gain_one, gain_two, gain_three]).reshape(-1),
+            bias_grad_local.reshape(-1),
+            square_part.reshape(1),
+        ]
+    )
+    small_size = small.shape[0]
+    small_rows = -(-small_size // 1024) * 8
+    small = jnp.pad(small, (0, small_rows * 128 - small_size)).reshape(small_rows, 128)
+    small = small_total(small, owners, holders, 7).reshape(-1)
+    gain_grad = small[: 3 * model_width].reshape(3, model_width)
+    bias_grad = small[3 * model_width : small_size - 1].reshape(bucket_count, head_count)
+    square_sum = small[small_size - 1]
+    clip_norm = jnp.sqrt(
+        square_sum + jnp.sum(gain_grad * gain_grad) + jnp.sum(bias_grad * bias_grad)
+    )
+    factor = jnp.minimum(1.0, clip_limit / clip_norm)
+    table_out = adam_step(embed_table, embed_first, embed_second, table_grad * factor, 1.0, 0.01)
+    qkv_out = adam_step(qkv_weight, qkv_first, qkv_second, weight_grads[0] * factor, 0.05, 0.01)
+    out_out = adam_step(out_weight, out_first, out_second, weight_grads[1] * factor, 0.05, 0.01)
+    in_out = adam_step(in_weight, in_first, in_second, weight_grads[2] * factor, 0.05, 0.01)
+    down_out = adam_step(down_weight, down_first, down_second, weight_grads[3] * factor, 0.05, 0.01)
+    gains_out = adam_step(norm_gains, gains_first, gains_second, gain_grad * factor, 1.0, 0.0)
+    bias_out = adam_step(position_bias, bias_first, bias_second, bias_grad * factor, 0.3, 0.0)
+    return (
+        loss_value,
+        clip_norm,
+        table_out[0],
+        table_out[1],
+        table_out[2],
+        qkv_out[0],
+        qkv_out[1],
+        qkv_out[2],
+        out_out[0],
+        out_out[1],
+        out_out[2],
+        in_out[0],
+        in_out[1],
+        in_out[2],
+        down_out[0],
+        down_out[1],
+        down_out[2],
+        gains_out[0],
+        gains_out[1],
+        gains_out[2],
+        bias_out[0],
+        bias_out[1],
+        bias_out[2],
+    )
+
+
+def local(*arrays):
+    n_dp, n_pair = lax.axis_size("dp"), lax.axis_size("pair")
+    lengths, qkv_weight, down_weight = arrays[2], arrays[9], arrays[18]
+    fits = (
+        n_pair == 4
+        and n_dp & (n_dp - 1) == 0
+        and qkv_weight.shape[0] % 8 == 0
+        and down_weight.shape[0] % 8 == 0
+        and lengths.shape[0] == 2
+        and 2 * arrays[1].size // n_dp % 128 == 0
+    )
+    return (local_fast if fits else local_plain)(*arrays)
+
+
 def solution(mesh):
     return jax.shard_map(
         local,

time: 1300 us -> 906 us (0.70)
  waiting for transfers between devices: 493 us -> 0.01 us
  Pallas kernels: 0 us -> 446 us
  blocking collectives: 260 us -> 0 us
  other arithmetic: 158 us -> 102 us
  matrix products: 186 us -> 166 us
  between operations: 23.6 us -> 10.3 us
    pallas_call x0 -> x7, Pallas kernels: none -> 446 us  [the longest x2 115 us: exchange(): pl.pallas_call(functools.partial(exchange_kernel, n_dp), out_shape=jax.Sh...]
    psum x1 -> x0, waiting for transfers between devices: 217 us -> none  [local(): table_grad = lax.psum(table_grad, 'pair')]
    all_to_all x1 -> x0, blocking collectives: 178 us -> none  [local(): lax.all_to_all(sendback, 'dp', split_axis=0, concat_axis=0, tiled=True)]
    reduce_scatter x4 -> x0, waiting for transfers between devices: 172 us -> none  [the longest x1 140 us: local(): lax.psum_scatter(grad_down, ('dp', 'pair'), scatter_dimension=0, tiled=True)]
    all_gather x4 -> x0, waiting for transfers between devices: 82.3 us -> none  [the longest x1 55.8 us: local(): lax.all_gather(low_mats[3], ('dp', 'pair'), axis=0, tiled=True)]
    scatter-add x3 -> x0, other arithmetic: 43.7 us -> none  [the longest x1 23.5 us: margin_loss(): against = jnp.take_along_axis(similar, negatives, axis=1)]
    all_gather x1 -> x0, blocking collectives: 42.5 us -> none  [local(): lax.all_gather(pooled_local, ('dp', 'pair'), axis=0, tiled=True)]
    psum x1 -> x0, blocking collectives: 40.3 us -> none  [local(): lax.psum((jnp.stack([gain_one, gain_two, gain_three]), bias_grad_local, s...]
  transfers between devices with their start and end apart: 11 -> 1, of which waited for: 6 -> 0; matrix products, arithmetic and copies ran while one was open for 27% -> 7% of each run, Pallas kernels for 0% -> 10%
where the time goes in v2:
time: 906 us; the launch traced here: 893 us
  Pallas kernels  446 us (49%)
  matrix products  166 us (18%)
  local copies, waits for them, and re-layouts  162 us (18%)
  other arithmetic  102 us (11%)
  between operations  10.3 us (1%)
    pallas_call x2, Pallas kernels, exchange(): pl.pallas_call(functools.partial(exchange_kernel, n_dp), out_shape=jax.Sh...  115 us
    pallas_call x1, Pallas kernels, scatter_all(): pl.pallas_call(functools.partial(scatter_kernel, n_dp, n_pair, pieces, le...  91.4 us
    pallas_call x1, Pallas kernels, gather_all(): pl.pallas_call(functools.partial(gather_kernel, n_dp, n_pair, pieces, len...  87.8 us
    pallas_call x1, Pallas kernels, table_total(): pl.pallas_call(functools.partial(table_kernel, n_pair, rows, chunk), out_...  86.6 us
    unnamed x150, local copies, waits for them, and re-layouts  71 us
    sub x7, other arithmetic, adam_step(): weight - rate * (first_hat / (jnp.sqrt(second_hat) + adam_eps) + shrink *...  39.1 us
    pallas_call x1, Pallas kernels, small_total(): pl.pallas_call(functools.partial(total_kernel, n, n_pair), out_shape=jax....  34.6 us
    pallas_call x1, Pallas kernels, pooled_loss(): pl.pallas_call(functools.partial(loss_kernel, n, n_pair, docs), out_shape...  31.2 us
  transfers between devices with their start and end apart: 1, of which 0 were waited for; matrix products, arithmetic and copies ran while one was open for 7% of the time, Pallas kernels for 10%

profile of v2, /device:TPU:0, one launch (start us, length us, event | category | flops | bytes accessed | tf_op | source)
XLA Modules:
  0.0 893.3 jit_solution(5830694091086602848)
XLA Ops:
  24.5 13.0 %fusion = f32[262144,12]{0,1:T(8,128)} fusion(f32[32,12]{0,1:T(8,128)S(1)} %copy-done.28, s32[262144]{0:T(1024)S(1)} %fusion.54), kind=kOutput, calls=%fused_computation.6 | convolution fusion | flops 1216348160 | bytes 13633024 | tf_op jit(solution)/shard_map/dot_general | solution.py:909
  43.9 17.7 %copy.172 = f32[2,8,512,512]{3,2,1,0:T(8,128)} copy(f32[2,8,512,512]{3,1,2,0:T(8,128)} %bitcast.163) | data formatting | bytes 33554432
  61.6 10.6 %slice.115 = f32[12,512,512]{2,1,0:T(8,128)} slice(f32[16,512,512]{2,1,0:T(8,128)} %bitcast.165), slice={[0:12], [0:512], [0:512]} | slice | bytes 25165824 | tf_op jit(solution)/shard_map/reshape | solution.py:909
  72.2 12.6 %copy.137 = f32[12,512,512]{1,2,0:T(8,128)} copy(f32[12,512,512]{2,1,0:T(8,128)} %slice.115) | data formatting | bytes 25165824 | tf_op jit(solution)/shard_map/reshape | solution.py:909
  84.8 87.8 %weights_gather.1 = (bf16[32,24,2304]{2,1,0:T(8,128)(2,1)}, bf16[32,24,768]{2,1,0:T(8,128)(2,1)}, bf16[32,24,3072]{2,1,0:T(8,128)(2,1)}, bf16[32,96,768]{2,1,0:T(8,128)(2,1)}) custom-call(bf16[24,2304]{1,0:T(8,128)(2,1)} %convert_element_type.182.refs_0_, bf16[24,768]{1,0:T(8,128)(2,1)} %convert_element_type.183.refs_1_, ...), custom_call_target="tpu_custom_call" | custom-call | tf_op jit(solution)/shard_map/weights_gather/pallas_call | solution.py:516
  173.3 13.2 %gather_fusion = bf16[2048,768]{1,0:T(8,128)(2,1)S(1)} fusion(f32[4016,768]{1,0:T(8,128)} %param.33, s32[2048]{0:T(1024)S(1)} %broadcast_clamp_fusion), kind=kCustom, calls=%fused_computation | custom fusion | bytes 6299648 | tf_op jit(solution)/shard_map/jit(_take)/gather | solution.py:899
  189.2 58.7 %rows_exchange.2 = bf16[8,256,768]{2,1,0:T(8,128)(2,1)} custom-call(bf16[8,256,768]{2,1,0:T(8,128)(2,1)} %select_convert_fusion.1.x_ref), custom_call_target="tpu_custom_call" | custom-call | tf_op jit(solution)/shard_map/rows_exchange/pallas_call | solution.py:563
  247.9 14.8 %gather_fusion.1 = bf16[1024,768]{1,0:T(8,128)(2,1)S(1)} fusion(bf16[8,256,768]{2,1,0:T(8,128)(2,1)} %rows_exchange.2, s32[1024]{0:T(1024)} %bitcast.164), kind=kCustom, calls=%fused_computation.1 | custom fusion | bytes 3153920 | tf_op jit(solution)/shard_map/gather | solution.py:902
  329.1 31.2 %pooled_loss.1 = (f32[1,1]{1,0:T(1,128)}, f32[2,768]{1,0:T(2,128)}) custom-call(f32[2,768]{1,0:T(2,128)} %broadcast_divide_fusion.1.x_ref, s32[64,1]{1,0:T(8,128)} %copy.144.pos_ref, s32[64,7]{1,0:T(8,128)} %copy.145.neg_ref, s32[64,1]{1,0:T(8,128)} %copy.146.count_ref), custom_call_target="tpu_custom_call" | custom-call | tf_op jit(solution)/shard_map/pooled_loss/pallas_call | solution.py:356
  363.6 7.8 select_convert_fusion
  371.5 10.3 %convolution_convert_fusion.1 = bf16[3072,768]{1,0:T(8,128)(2,1)} fusion(bf16[1024,3072]{1,0:T(8,128)(2,1)} %copy-done.54, bf16[1024,768]{1,0:T(8,128)(2,1)S(1)} %fusion.38), kind=kOutput, calls=%fused_computation.43 | convolution fusion | flops 4834197504 | bytes 12582912 | tf_op jit(solution)/shard_map/dot_general | solution.py:966
  421.5 8.6 copy.153
  436.9 8.9 multiply_reduce_fusion
  456.6 8.8 fusion.24
  465.4 26.0 %convolution_convert_fusion.3 = bf16[768,2304]{1,0:T(8,128)(2,1)} fusion(bf16[1024,768]{1,0:T(8,128)(2,1)S(1)} %copy-done.5, f32[768]{0:T(1024)S(1)} %copy-done.34, f32[1024]{0:T(1024)S(1)} %copy-done.32, bf16[512,768]{0,1:T(8,128)(2,1)S(1)} %bitcast.204, bf16[512,768]{0,1:T(8,128)(2,1)S(1)} %bitcast.208, bf16[512,768]{0,1:T(8,128)(2,1)S(1)} %bitcast.199, ...), kind=kOutput, calls=%fused_computation.45 | convolution fusion | flops 3657105408 | bytes 9837568 | tf_op jit(solution)/shard_map/dot_general | solution.py:1022
  491.4 8.6 copy.154
  508.1 11.5 %copy.173 = bf16[2,8,512,512]{3,1,2,0:T(8,128)(2,1)} copy(bf16[2,8,512,512]{3,2,1,0:T(8,128)(2,1)} %bitcast.167) | data formatting | bytes 16777216
  519.6 91.4 %weight_grads_sum.1 = (f32[24,2304]{1,0:T(8,128)}, f32[24,768]{1,0:T(8,128)}, f32[24,3072]{1,0:T(8,128)}, f32[96,768]{1,0:T(8,128)}) custom-call(bf16[32,24,2304]{2,1,0:T(8,128)(2,1)} %bitcast.191, bf16[32,24,768]{2,1,0:T(8,128)(2,1)} %bitcast.200, bf16[32,24,3072]{2,1,0:T(8,128)(2,1)} %bitcast.188, bf16[32,96,768]{2,1,0:T(8,128)(2,1)} %bitcast.187), custom_call_target="tpu_custom_call" | custom-call | tf_op jit(solution)/shard_map/weight_grads_sum/pallas_call | solution.py:249
  620.1 10.3 %scatter_custom_fusion.1 = bf16[2048,768]{1,0:T(8,128)(2,1)} fusion(s32[1024]{0:T(1024)} %copy-done.41, f32[1024,768]{1,0:T(8,128)} %copy-done.6, bf16[1024,768]{1,0:T(8,128)(2,1)} %copy-done.4, f32[1024,768]{1,0:T(8,128)} %get-tuple-element.149, bf16[]{:T(256)} %constant.52.clone.1, f32[1024]{0:T(1024)S(1)} %broadcast_multiply_fusion, ...), kind=kCustom, calls=%fused_computation.82 | custom fusion | flops 6291456 | bytes 11022848
  630.4 56.1 %rows_exchange.3 = bf16[8,256,768]{2,1,0:T(8,128)(2,1)} custom-call(bf16[8,256,768]{2,1,0:T(8,128)(2,1)} %bitcast.169), custom_call_target="tpu_custom_call" | custom-call | tf_op jit(solution)/shard_map/rows_exchange/pallas_call | solution.py:563
  693.5 11.7 %copy.174 = bf16[2,8,512,512]{3,1,2,0:T(8,128)(2,1)} copy(bf16[2,8,512,512]{3,2,1,0:T(8,128)(2,1)} %bitcast.166) | data formatting | bytes 16777216
  720.4 86.6 %table_total.1 = (bf16[4096,768]{1,0:T(8,128)(2,1)}, f32[1,1]{1,0:T(1,128)}) custom-call(bf16[2048,768]{1,0:T(8,128)(2,1)} %bitcast.168, s32[1,2048]{1,0:T(1,128)} %bitcast.46.ask_ref), custom_call_target="tpu_custom_call" | custom-call | tf_op jit(solution)/shard_map/table_total/pallas_call | solution.py:425
  809.0 34.6 %small_total.1 = f32[24,128]{1,0:T(8,128)} custom-call(f32[24,128]{1,0:T(8,128)} %fusion.68.x_ref), custom_call_target="tpu_custom_call" | custom-call | tf_op jit(solution)/shard_map/small_total/pallas_call | solution.py:306
  860.8 29.4 %add_subtract_fusion = (f32[4016,768]{1,0:T(8,128)}, f32[4016,768]{1,0:T(8,128)}, f32[4016,768]{1,0:T(8,128)}) fusion(f32[4016,768]{1,0:T(8,128)} %param.33, f32[]{:T(128)S(6)} %min.3, bf16[4096,768]{1,0:T(8,128)(2,1)} %get-tuple-element.46, f32[4016,768]{1,0:T(8,128)} %param.34, f32[4016,768]{1,0:T(8,128)} %param.35), kind=kLoop, calls=%fused_computation.28 | loop fusion | flops 49348608 | bytes 80191488 | tf_op jit(solution)/shard_map/sub | solution.py:120
  (257 shorter events, 212.9 us)
Async XLA Ops:
  8.3 15.2 %copy-start.41 = (s32[1024]{0:T(1024)}, s32[1024]{0:T(1024)S(1)}, u32[]{:S(2)}) copy-start(s32[1024]{0:T(1024)S(1)} %broadcast_select_fusion) | copy-start | bytes 12292
  13.2 159.4 %all-to-all-start = ((s32[8,1,256]{2,1,0:T(1,128)}), s32[8,1,256]{2,1,0:T(1,128)}, u32[]{:S(2)}, u32[]{:S(2)}) async-start(s32[8,1,256]{2,1,0:T(1,128)} %bitcast.5), calls=%async_computation | async-start | bytes 16384 | tf_op jit(solution)/shard_map/all_to_all | solution.py:898
  24.4 14.7 %copy-start.45 = (s32[64]{0:T(128)S(1)}, s32[64]{0:T(128)}, u32[]{:S(2)}) copy-start(s32[64]{0:T(128)} %param.30) | copy-start | bytes 772
  24.4 15.4 %copy-start.40 = (s32[64,7]{0,1:T(8,128)S(1)}, s32[64,7]{0,1:T(8,128)}, u32[]{:S(2)}) copy-start(s32[64,7]{0,1:T(8,128)} %param.31) | copy-start | bytes 5380
  24.4 16.1 %copy-start.46 = (s32[64]{0:T(128)S(1)}, s32[64]{0:T(128)}, u32[]{:S(2)}) copy-start(s32[64]{0:T(128)} %param.32) | copy-start | bytes 772
  24.4 16.8 %copy-start.25 = (f32[24,768]{1,0:T(8,128)S(1)}, f32[24,768]{1,0:T(8,128)}, u32[]{:S(2)}) copy-start(f32[24,768]{1,0:T(8,128)} %param.39) | copy-start | bytes 221188
  24.4 17.4 %copy-start.24 = (f32[24,2304]{1,0:T(8,128)S(1)}, f32[24,2304]{1,0:T(8,128)}, u32[]{:S(2)}) copy-start(f32[24,2304]{1,0:T(8,128)} %param.36) | copy-start | bytes 663556
  24.4 18.1 %copy-start.23 = (f32[24,3072]{1,0:T(8,128)S(1)}, f32[24,3072]{1,0:T(8,128)}, u32[]{:S(2)}) copy-start(f32[24,3072]{1,0:T(8,128)} %param.42) | copy-start | bytes 884740
  24.5 18.8 %copy-start.22 = (f32[96,768]{1,0:T(8,128)S(1)}, f32[96,768]{1,0:T(8,128)}, u32[]{:S(2)}) copy-start(f32[96,768]{1,0:T(8,128)} %param.45) | copy-start | bytes 884740
  247.9 15.2 %copy-start.33 = (f32[768]{0:T(1024)S(1)}, f32[768]{0:T(1024)}, u32[]{:S(2)}) copy-start(f32[768]{0:T(1024)} %get-tuple-element.101) | copy-start | bytes 9220
  262.6 52.3 %copy-start.4 = (bf16[1024,768]{1,0:T(8,128)(2,1)}, bf16[1024,768]{1,0:T(8,128)(2,1)S(1)}, u32[]{:S(2)}) copy-start(bf16[1024,768]{1,0:T(8,128)(2,1)S(1)} %gather_fusion.1) | copy-start | bytes 4718596
  271.8 17.7 %copy-start.9 = (bf16[512,768]{0,1:T(8,128)(2,1)}, bf16[512,768]{0,1:T(8,128)(2,1)S(1)}, u32[]{:S(2)}) copy-start(bf16[512,768]{0,1:T(8,128)(2,1)S(1)} %copy.136) | copy-start | bytes 2359300
  273.5 20.5 %copy-start.7 = (bf16[512,768]{0,1:T(8,128)(2,1)}, bf16[512,768]{0,1:T(8,128)(2,1)S(1)}, u32[]{:S(2)}) copy-start(bf16[512,768]{0,1:T(8,128)(2,1)S(1)} %copy.141) | copy-start | bytes 2359300
  362.6 19.2 %slice-start.10 = ((s8[4718592]{0:T(1024)(128)(4,1)}), s8[4194304]{0:T(1024)(128)(4,1)S(1)}, s32[]{:S(2)}) async-start(s8[4718592]{0:T(1024)(128)(4,1)} %bitcast.223), calls=%async_computation.11 | async-start | bytes 8388608
  363.6 18.1 %slice-start.11 = ((s8[4718592]{0:T(1024)(128)(4,1)}), s8[524288]{0:T(1024)(128)(4,1)S(1)}, s32[]{:S(2)}) async-start(s8[4718592]{0:T(1024)(128)(4,1)} %bitcast.223), calls=%async_computation.12 | async-start | bytes 1048576
  430.1 15.7 %slice-start = ((s8[12582912]{0:T(1024)(128)(4,1)}), s8[4194304]{0:T(1024)(128)(4,1)S(1)}, s32[]{:S(2)}) async-start(s8[12582912]{0:T(1024)(128)(4,1)} %bitcast.159), calls=%async_computation.1 | async-start | bytes 8388608
  430.1 15.7 %slice-start.1 = ((s8[12582912]{0:T(1024)(128)(4,1)}), s8[4194304]{0:T(1024)(128)(4,1)S(1)}, s32[]{:S(2)}) async-start(s8[12582912]{0:T(1024)(128)(4,1)} %bitcast.159), calls=%async_computation.2 | async-start | bytes 8388608
  693.5 19.0 %slice-start.6 = ((s8[8388608]{0:T(1024)(128)(4,1)}), s8[4194304]{0:T(1024)(128)(4,1)S(1)}, s32[]{:S(2)}) async-start(s8[8388608]{0:T(1024)(128)(4,1)} %bitcast.175), calls=%async_computation.7 | async-start | bytes 8388608
  807.0 52.6 %copy-start.29 = (f32[32,12]{0,1:T(8,128)S(1)}, f32[32,12]{0,1:T(8,128)}, u32[]{:S(2)}) copy-start(f32[32,12]{0,1:T(8,128)} %param.51) | copy-start | bytes 4612
  807.0 52.6 %copy-start.38 = (f32[32,12]{0,1:T(8,128)S(1)}, f32[32,12]{0,1:T(8,128)}, u32[]{:S(2)}) copy-start(f32[32,12]{0,1:T(8,128)} %param.52) | copy-start | bytes 4612
  807.0 52.6 %copy-start.39 = (f32[32,12]{0,1:T(8,128)S(1)}, f32[32,12]{0,1:T(8,128)}, u32[]{:S(2)}) copy-start(f32[32,12]{0,1:T(8,128)} %param.53) | copy-start | bytes 4612
  807.0 53.2 %copy-start.27 = (f32[3,768]{1,0:T(4,128)S(1)}, f32[3,768]{1,0:T(4,128)}, u32[]{:S(2)}) copy-start(f32[3,768]{1,0:T(4,128)} %param.48) | copy-start | bytes 27652
  807.0 53.2 %copy-start.36 = (f32[3,768]{1,0:T(4,128)S(1)}, f32[3,768]{1,0:T(4,128)}, u32[]{:S(2)}) copy-start(f32[3,768]{1,0:T(4,128)} %param.49) | copy-start | bytes 27652
  807.0 53.2 %copy-start.37 = (f32[3,768]{1,0:T(4,128)S(1)}, f32[3,768]{1,0:T(4,128)}, u32[]{:S(2)}) copy-start(f32[3,768]{1,0:T(4,128)} %param.50) | copy-start | bytes 27652
  (47 other events, 253.7 us)

commit v3 on v2

--- a/solution.py
+++ b/solution.py
@@ -569,16 +569,148 @@
         name="rows_exchange",
     )(x)
 
+
+NT = (((1,), (1,)), ((), ()))
+TN = (((0,), (0,)), ((), ()))
+
+def band(w_ref, h, table, seq):
+    tiles = seq // 128
+    for d in range(1 - tiles, tiles):
+        low = seq + 128 * d - 128
+        x = jnp.broadcast_to(w_ref[0, h : h + 1, low : low + 256], (128, 256))
+        tile = pltpu.roll(x, 0, 1, stride=1, stride_axis=0)[:, 128:]
+        for a in range(tiles):
+            if 0 <= a + d < tiles:
+                table[h, a * 128 : a * 128 + 128, (a + d) * 128 : (a + d) * 128 + 128] = tile
+
+def forward_kernel(len_ref, q_ref, k_ref, v_ref, w_ref, o_ref, table):
+    seq = q_ref.shape[0]
+    doc = pl.program_id(1)
+    @pl.when(doc == 0)
+    def _():
+        for h in range(2):
+            band(w_ref, h, table, seq)
+    length = len_ref[doc]
+    lane = lax.broadcasted_iota(jnp.int32, (seq, 128), 1)
+    column = lax.broadcasted_iota(jnp.int32, (1, seq), 1)
+    q = q_ref[...] * jnp.bfloat16(0.125)
+    k = k_ref[...]
+    v = v_ref[...]
+    got = []
+    for h in range(2):
+        mine = (lane < 64) == (h == 0)
+        s = lax.dot_general(jnp.where(mine, q, 0), k, NT, preferred_element_type=jnp.float32)
+        s = jnp.where(column < length, s + table[h], -1000000000.0)
+        e = jnp.exp(s - jnp.max(s, axis=1, keepdims=True))
+        p = (e * (1.0 / jnp.sum(e, axis=1, keepdims=True))).astype(jnp.bfloat16)
+        got.append(jnp.dot(p, v, preferred_element_type=jnp.float32))
+    o_ref[...] = jnp.where(lane < 64, got[0], got[1]).astype(o_ref.dtype)
+
+def attention(lengths, qkv, w, seq):
+    tokens = qkv.shape[0]
+    pairs = w.shape[0]
+    docs = tokens // seq
+    spec = lambda base: pl.BlockSpec((seq, 128), lambda h, d, *_: (d, base + h))
+    return pl.pallas_call(
+        forward_kernel,
+        grid_spec=pltpu.PrefetchScalarGridSpec(
+            num_scalar_prefetch=1, grid=(pairs, docs),
+            in_specs=[spec(0), spec(pairs), spec(2 * pairs), pl.BlockSpec((1, 2, 2 * seq), lambda h, d, *_: (h, 0, 0))],
+            out_specs=spec(0),
+            scratch_shapes=[pltpu.VMEM((2, seq, seq), jnp.float32)]),
+        out_shape=jax.ShapeDtypeStruct((tokens, pairs * 128), jnp.bfloat16),
+        compiler_params=pltpu.CompilerParams(dimension_semantics=("arbitrary", "arbitrary"), vmem_limit_bytes=50 * 1024 * 1024),
+        name="attention",
+    )(lengths, qkv, qkv, qkv, w)
+
+def backward_kernel(len_ref, q_ref, k_ref, v_ref, g_ref, w_ref, o_ref, z_ref, table, total):
+    seq = q_ref.shape[0]
+    tiles = seq // 128
+    doc = pl.program_id(1)
+    @pl.when(doc == 0)
+    def _():
+        for h in range(2):
+            band(w_ref, h, table, seq)
+        total[...] = jnp.zeros_like(total)
+    length = len_ref[doc]
+    lane = lax.broadcasted_iota(jnp.int32, (seq, 128), 1)
+    row = lax.broadcasted_iota(jnp.int32, (seq, 1), 0)
+    q = q_ref[...] * jnp.bfloat16(0.125)
+    k = k_ref[...]
+    v = v_ref[...]
+    g = g_ref[...]
+    parts = []
+    for h in range(2):
+        mine = (lane < 64) == (h == 0)
+        s = lax.dot_general(k, jnp.where(mine, q, 0), NT, preferred_element_type=jnp.float32)
+        s = jnp.where(row < length, s + table[h], -1000000000.0)
+        e = jnp.exp(s - jnp.max(s, axis=0, keepdims=True))
+        p = e * (1.0 / jnp.sum(e, axis=0, keepdims=True))
+        dv = jnp.dot(p.astype(jnp.bfloat16), g, preferred_element_type=jnp.float32)
+        dp = lax.dot_general(v, jnp.where(mine, g, 0), NT, preferred_element_type=jnp.float32)
+        ds = (p * (dp - jnp.sum(p * dp, axis=0, keepdims=True))).astype(jnp.bfloat16)
+        total[h] += ds.astype(jnp.float32)
+        dk = jnp.dot(ds, q, preferred_element_type=jnp.float32)
+        dq = lax.dot_general(ds, k, TN, preferred_element_type=jnp.float32) * 0.125
+        parts.append((dq, dk, dv))
+    for i in range(3):
+        o_ref[i] = jnp.where(lane < 64, parts[0][i], parts[1][i]).astype(o_ref.dtype)
+    @pl.when(doc == pl.num_programs(1) - 1)
+    def _():
+        r = lax.broadcasted_iota(jnp.int32, (128, 128), 0)
+        c = lax.broadcasted_iota(jnp.int32, (128, 128), 1)
+        flip = jnp.where(r + c == 127, 1.0, 0.0)
+        z_ref[...] = jnp.zeros_like(z_ref)
+        for h in range(2):
+            def block(d):
+                return sum(total[h, a * 128 : a * 128 + 128, (a - d) * 128 : (a - d) * 128 + 128] for a in range(tiles) if 0 <= a - d < tiles)
+            for d in (-1, 0, 1):
+                x = jnp.dot(flip, block(d), precision=HIGHEST, preferred_element_type=jnp.float32)
+                x = jnp.concatenate([x, jnp.zeros_like(x)], axis=1)
+                x = pltpu.roll(x, 0, 1, stride=1, stride_axis=0)
+                z_ref[0, h, d + 1 : d + 2, :] = jnp.sum(x, axis=0, keepdims=True)
+            z_ref[0, h, 3:4, 0:128] = jnp.sum(sum(block(-d) for d in range(2, tiles)), axis=0, keepdims=True)
+            z_ref[0, h, 4:5, 0:128] = jnp.sum(sum(block(d) for d in range(2, tiles)), axis=0, keepdims=True)
+
+def attention_back(lengths, qkv, g, w, seq):
+    tokens = qkv.shape[0]
+    pairs = w.shape[0]
+    docs = tokens // seq
+    spec = lambda base: pl.BlockSpec((seq, 128), lambda h, d, *_: (d, base + h))
+    return pl.pallas_call(
+        backward_kernel,
+        grid_spec=pltpu.PrefetchScalarGridSpec(
+            num_scalar_prefetch=1, grid=(pairs, docs),
+            in_specs=[spec(0), spec(pairs), spec(2 * pairs), spec(0), pl.BlockSpec((1, 2, 2 * seq), lambda h, d, *_: (h, 0, 0))],
+            out_specs=[pl.BlockSpec((3, seq, 128), lambda h, d, *_: (0, d, h)), pl.BlockSpec((1, 2, 8, 256), lambda h, d, *_: (h, 0, 0, 0))],
+            scratch_shapes=[pltpu.VMEM((2, seq, seq), jnp.float32), pltpu.VMEM((2, seq, seq), jnp.float32)]),
+        out_shape=[jax.ShapeDtypeStruct((3, tokens, pairs * 128), jnp.bfloat16), jax.ShapeDtypeStruct((pairs, 2, 8, 256), jnp.float32)],
+        compiler_params=pltpu.CompilerParams(dimension_semantics=("arbitrary", "arbitrary"), vmem_limit_bytes=50 * 1024 * 1024),
+        name="attention_back",
+    )(lengths, qkv, qkv, qkv, g, w)
+
+def bias_rows(position_bias, seq, sign):
+    nb, heads = position_bias.shape
+    buckets = bucket_of(sign * (jnp.arange(2 * seq) - seq), nb, REACH)
+    hits = (jnp.arange(nb)[:, None] == buckets[None, :]).astype(jnp.float32)
+    return jnp.dot(position_bias.T, hits, precision=HIGHEST).reshape(heads // 2, 2, 2 * seq)
+
+def bias_gradient(z, seq, nb):
+    heads = z.shape[0] * 2
+    j = jnp.arange(256)
+    offs = [jnp.where(j < 255, 128 * d + 127 - j, 0) for d in (-1, 0, 1)] + [jnp.full((256,), 1 - seq), jnp.full((256,), seq - 1)]
+    offs = jnp.concatenate(offs + [jnp.zeros((768,), jnp.int32)])
+    hits = (bucket_of(offs, nb, REACH)[:, None] == jnp.arange(nb)[None, :]).astype(jnp.float32)
+    return jnp.dot(z.reshape(heads, 2048), hits, precision=HIGHEST).T
+
 def weight_pieces(widths):
-    qkv_cols, out_cols, in_cols, down_cols = widths
-    cut = down_cols * 2 // 3 // 128 * 128
-    return [
-        (2, 0, in_cols, 0),
-        (0, 0, qkv_cols, 1),
-        (1, 0, out_cols, 0),
-        (3, 0, cut, 0),
-        (3, cut, down_cols, 1),
-    ]
+    down = len(widths) - 1
+    cut = widths[down] * 2 // 3 // 128 * 128
+    pieces = [(down - 1, 0, widths[down - 1], 0)]
+    pieces += [(which, 0, widths[which], 1) for which in range(down - 2)]
+    pieces += [(down - 2, 0, widths[down - 2], 0)]
+    return pieces + [(down, 0, cut, 0), (down, cut, widths[down], 1)]
+
 
 def local_plain(
     token_owner,
@@ -902,41 +1034,12 @@
     embedded = replies[tok_owner, slot_rank].astype(jnp.float32)
     positions = jnp.arange(seq_len)
     live = positions[None, :] < lengths[:, None]
-    pair_buckets = bucket_of(
-        (positions[None, :] - positions[:, None]).reshape(-1), bucket_count, REACH
-    )
-    pair_hits = (jnp.arange(bucket_count)[:, None] == pair_buckets[None, :]).astype(jnp.float32)
-    bias_full = jnp.dot(position_bias.T, pair_hits, precision=HIGHEST).reshape(
-        head_count, seq_len, seq_len
-    )
-    bucket_map = pair_hits.astype(jnp.bfloat16)
-
-    def split_doc(source, doc_index):
-        doc_rows = source[doc_index * seq_len : (doc_index + 1) * seq_len]
-        return tuple(
-            (
-                doc_rows[:, member * model_width : (member + 1) * model_width].reshape(
-                    seq_len, head_count, -1
-                )
-                for member in range(3)
-            )
-        )
-
     normed_one, inverse_one = rms_forward(embedded, norm_gains[0])
     normed_one = normed_one.astype(jnp.bfloat16)
     qkv_rows = jnp.dot(normed_one, qkv_full, preferred_element_type=jnp.float32).astype(
         jnp.bfloat16
     )
-    attended_parts = []
-    logsum_parts = []
-    for doc_index in range(doc_count):
-        query_heads, key_heads, value_heads = split_doc(qkv_rows, doc_index)
-        doc_out, logsum = attend_forward(
-            query_heads, key_heads, value_heads, bias_full, live[doc_index]
-        )
-        attended_parts.append(doc_out.reshape(seq_len, model_width))
-        logsum_parts.append(logsum)
-    attended = jnp.concatenate(attended_parts, axis=0).astype(jnp.bfloat16)
+    attended = attention(lengths, qkv_rows, bias_rows(position_bias, seq_len, 1), seq_len)
     residual = embedded + jnp.dot(attended, out_full, preferred_element_type=jnp.float32)
     normed_two, inverse_two = rms_forward(residual, norm_gains[1])
     normed_two = normed_two.astype(jnp.bfloat16)
@@ -985,45 +1088,22 @@
     grad_attended = lax.dot_general(
         grad_attn_branch, out_back, CONTRACT_COLS, preferred_element_type=jnp.float32
     ).astype(jnp.bfloat16)
-    grad_qkv_parts = []
-    bias_grad_heads = jnp.zeros((head_count, bucket_count), jnp.float32)
-    for doc_index in range(doc_count):
-        query_heads, key_heads, value_heads = split_doc(qkv_rows, doc_index)
-        grad_doc = grad_attended[doc_index * seq_len : (doc_index + 1) * seq_len].reshape(
-            seq_len, head_count, -1
-        )
-        grad_query, grad_key, grad_value, grad_low = attend_backward(
-            query_heads,
-            key_heads,
-            value_heads,
-            bias_full,
-            live[doc_index],
-            logsum_parts[doc_index],
-            grad_doc,
-        )
-        grad_qkv_parts.append(
-            jnp.concatenate(
-                [
-                    grad_query.reshape(seq_len, model_width),
-                    grad_key.reshape(seq_len, model_width),
-                    grad_value.reshape(seq_len, model_width),
-                ],
-                axis=1,
-            )
-        )
-        bias_grad_heads = bias_grad_heads + lax.dot_general(
-            grad_low.reshape(head_count, -1),
-            bucket_map,
+    grad_parts, diagonals = attention_back(
+        lengths, qkv_rows, grad_attended, bias_rows(position_bias, seq_len, -1), seq_len
+    )
+    bias_grad_local = bias_gradient(diagonals, seq_len, bucket_count)
+    grad_qkv = [
+        lax.dot_general(normed_one, part, CONTRACT_ROWS, preferred_element_type=jnp.float32)
+        for part in grad_parts
+    ]
+    grad_normed_one = sum(
+        lax.dot_general(
+            part,
+            qkv_back[:, index * model_width : (index + 1) * model_width],
             CONTRACT_COLS,
             preferred_element_type=jnp.float32,
         )
-    bias_grad_local = bias_grad_heads.T
-    grad_qkv_rows = jnp.concatenate(grad_qkv_parts, axis=0).astype(jnp.bfloat16)
-    grad_qkv = lax.dot_general(
-        normed_one, grad_qkv_rows, CONTRACT_ROWS, preferred_element_type=jnp.float32
-    )
-    grad_normed_one = lax.dot_general(
-        grad_qkv_rows, qkv_back, CONTRACT_COLS, preferred_element_type=jnp.float32
+        for index, part in enumerate(grad_parts)
     )
     grad_emb_part, gain_one = rms_backward(embedded, inverse_one, norm_gains[0], grad_normed_one)
     grad_embedded = grad_residual + grad_emb_part
@@ -1046,13 +1126,14 @@
     weight_grads = scatter_all(
         [
             grad.astype(jnp.bfloat16).reshape(parts, -1, grad.shape[1])
-            for grad in (grad_qkv, grad_out, grad_in, grad_down)
+            for grad in (*grad_qkv, grad_out, grad_in, grad_down)
         ],
-        pieces,
+        weight_pieces([model_width] * 4 + [grad_in.shape[1], model_width]),
         owners,
         holders,
         6,
     )
+    weight_grads = (jnp.concatenate(weight_grads[:3], axis=1), *weight_grads[3:])
     square_part = table_square[0, 0] + jnp.sum(
         jnp.stack([jnp.sum(grad_piece * grad_piece) for grad_piece in weight_grads])
     )

time: 906 us -> 753 us (0.83)
  local copies, waits for them, and re-layouts: 162 us -> 51.9 us
  matrix products: 166 us -> 76.8 us
  Pallas kernels: 446 us -> 511 us
  other arithmetic: 102 us -> 85.5 us
    dot_general x17 -> x9, matrix products: 113 us -> 20.5 us  [the longest x3 8.97 us: local_fast(): lax.dot_general(part, qkv_back[:, index * model_width:(index + 1) * model...]
    pallas_call x0 -> x2, Pallas kernels: none -> 63.3 us  [the longest x1 42.1 us: attention_back(): pl.pallas_call(backward_kernel, grid_spec=pltpu.PrefetchScalarGridSpec(nu...]
    unnamed x150 -> x89, local copies, waits for them, and re-layouts: 71 us -> 13.1 us
    reshape x2, local copies, waits for them, and re-layouts: 23.2 us -> 1.3 us  [bias_rows(): jnp.dot(position_bias.T, hits, precision=HIGHEST)]
    pallas_call x1, Pallas kernels: 34.6 us -> 16 us  [small_total(): pl.pallas_call(functools.partial(total_kernel, n, n_pair), out_shape=jax....]
    pallas_call x1, Pallas kernels: 91.4 us -> 109 us  [scatter_all(): pl.pallas_call(functools.partial(scatter_kernel, n_dp, n_pair, pieces, le...]
    convert_element_type x2 -> x0, local copies, waits for them, and re-layouts: 17.2 us -> none  [attend_backward(): grad_low = grad_score.astype(jnp.bfloat16)]
    slice x10 -> x1, local copies, waits for them, and re-layouts: 14.4 us -> 0.28 us  [the longest x7 13.5 us: split_doc(): doc_rows[:, member * model_width:(member + 1) * model_width]]
  transfers between devices with their start and end apart: 1 -> 1, of which waited for: 0 -> 0; matrix products, arithmetic and copies ran while one was open for 7% -> 2% of each run, Pallas kernels for 10% -> 12%
where the time goes in v3:
time: 753 us; the launch traced here: 743 us
  Pallas kernels  511 us (68%)
  other arithmetic  85.5 us (11%)
  matrix products  76.8 us (10%)
  local copies, waits for them, and re-layouts  51.9 us (7%)
  between operations  10.2 us (1%)
    pallas_call x2, Pallas kernels, exchange(): pl.pallas_call(functools.partial(exchange_kernel, n_dp), out_shape=jax.Sh...  117 us
    pallas_call x1, Pallas kernels, scatter_all(): pl.pallas_call(functools.partial(scatter_kernel, n_dp, n_pair, pieces, le...  109 us
    pallas_call x1, Pallas kernels, gather_all(): pl.pallas_call(functools.partial(gather_kernel, n_dp, n_pair, pieces, len...  87.8 us
    pallas_call x1, Pallas kernels, table_total(): pl.pallas_call(functools.partial(table_kernel, n_pair, rows, chunk), out_...  87.3 us
    pallas_call x1, Pallas kernels, attention_back(): pl.pallas_call(backward_kernel, grid_spec=pltpu.PrefetchScalarGridSpec(nu...  42.1 us
    sub x7, other arithmetic, adam_step(): weight - rate * (first_hat / (jnp.sqrt(second_hat) + adam_eps) + shrink *...  37.7 us
    pallas_call x1, Pallas kernels, pooled_loss(): pl.pallas_call(functools.partial(loss_kernel, n, n_pair, docs), out_shape...  31.3 us
    pallas_call x1, Pallas kernels, attention(): pl.pallas_call(forward_kernel, grid_spec=pltpu.PrefetchScalarGridSpec(num...  21.2 us
  transfers between devices with their start and end apart: 1, of which 0 were waited for; matrix products, arithmetic and copies ran while one was open for 2% of the time, Pallas kernels for 12%

profile of v3, /device:TPU:0, one launch (start us, length us, event | category | flops | bytes accessed | tf_op | source)
XLA Modules:
  0.0 742.8 jit_solution(4964698896412989841)
XLA Ops:
  8.3 4.9 scatter_custom_fusion
  13.2 7.3 all-to-all-start
  38.7 87.8 %weights_gather.1 = (bf16[32,24,2304]{2,1,0:T(8,128)(2,1)}, bf16[32,24,768]{2,1,0:T(8,128)(2,1)}, bf16[32,24,3072]{2,1,0:T(8,128)(2,1)}, bf16[32,96,768]{2,1,0:T(8,128)(2,1)}) custom-call(bf16[24,2304]{1,0:T(8,128)(2,1)} %convert_element_type.231.refs_0_, bf16[24,768]{1,0:T(8,128)(2,1)} %convert_element_type.232.refs_1_, ...), custom_call_target="tpu_custom_call" | custom-call | tf_op jit(solution)/shard_map/weights_gather/pallas_call | solution.py:516
  127.2 13.0 %gather_fusion = bf16[2048,768]{1,0:T(8,128)(2,1)S(1)} fusion(f32[4016,768]{1,0:T(8,128)} %param.33, s32[2048]{0:T(1024)S(1)} %broadcast_clamp_fusion), kind=kCustom, calls=%fused_computation | custom fusion | bytes 6299648 | tf_op jit(solution)/shard_map/jit(_take)/gather | solution.py:1031
  142.9 58.6 %rows_exchange.2 = bf16[8,256,768]{2,1,0:T(8,128)(2,1)} custom-call(bf16[8,256,768]{2,1,0:T(8,128)(2,1)} %select_convert_fusion.1.x_ref), custom_call_target="tpu_custom_call" | custom-call | tf_op jit(solution)/shard_map/rows_exchange/pallas_call | solution.py:563
  201.6 14.8 %gather_fusion.1 = bf16[1024,768]{1,0:T(8,128)(2,1)S(1)} fusion(bf16[8,256,768]{2,1,0:T(8,128)(2,1)} %rows_exchange.2, s32[1024]{0:T(1024)} %bitcast.124), kind=kCustom, calls=%fused_computation.1 | custom fusion | bytes 3153920 | tf_op jit(solution)/shard_map/gather | solution.py:1034
  216.8 7.8 %convolution_convert_fusion.q_ref.k_ref.v_ref = bf16[1024,2304]{1,0:T(8,128)(2,1)} fusion(bf16[768,2304]{1,0:T(8,128)(2,1)} %bitcast.135, bf16[1024,768]{1,0:T(8,128)(2,1)S(1)} %gather_fusion.1, f32[768]{0:T(1024)S(1)} %copy-done.19, f32[1024]{0:T(1024)S(1)} %add_rsqrt_fusion.2), kind=kOutput, calls=%fused_computation.12 | convolution fusion | flops 3629383680 | bytes 9837568 | tf_op jit(solution)/shard_map/dot_general | solution.py:1039
  224.6 21.2 %attention.1 = bf16[1024,768]{1,0:T(8,128)(2,1)S(1)} custom-call(s32[2]{0:T(128)S(1)} %copy-done.3, bf16[1024,2304]{1,0:T(8,128)(2,1)} %convolution_convert_fusion.q_ref.k_ref.v_ref, bf16[1024,2304]{1,0:T(8,128)(2,1)} %convolution_convert_fusion.q_ref.k_ref.v_ref, bf16[1024,2304]{1,0:T(8,128)(2,1)} %convolution_convert_fusion.q_ref.k_ref.v_ref, ...), custom_call_target="tpu_custom_call" | custom-call | tf_op jit(solution)/shard_map/attention/pallas_call | solution.py:614
  247.5 5.7 maximum_convert_fusion
  253.3 5.3 multiply_reduce_fusion.2
  261.4 31.3 %pooled_loss.1 = (f32[1,1]{1,0:T(1,128)}, f32[2,768]{1,0:T(2,128)}) custom-call(f32[2,768]{1,0:T(2,128)} %broadcast_divide_fusion.1.x_ref, s32[64,1]{1,0:T(8,128)} %copy.78.pos_ref, s32[64,7]{1,0:T(8,128)} %copy.79.neg_ref, s32[64,1]{1,0:T(8,128)} %copy.80.count_ref), custom_call_target="tpu_custom_call" | custom-call | tf_op jit(solution)/shard_map/pooled_loss/pallas_call | solution.py:356
  293.6 3.5 fusion.19
  298.2 9.1 %select_convert_fusion = bf16[1024,3072]{1,0:T(8,128)(2,1)S(1)} fusion(bf16[1024,3072]{1,0:T(8,128)(2,1)} %copy-done.31, bf16[1024,768]{1,0:T(8,128)(2,1)S(1)} %fusion.20, bf16[3072,768]{1,0:T(8,128)(2,1)} %bitcast.157), kind=kOutput, calls=%fused_computation.5 | convolution fusion | flops 4841275392 | bytes 18874368 | tf_op jit(solution)/shard_map/dot_general | solution.py:1072
  307.3 5.9 multiply_reduce_fusion
  316.4 42.1 %attention_back.1 = (bf16[3,1024,768]{2,1,0:T(8,128)(2,1)}, f32[6,2,8,256]{3,2,1,0:T(8,128)S(1)}) custom-call(s32[2]{0:T(128)S(1)} %copy-done.3, bf16[1024,2304]{1,0:T(8,128)(2,1)} %convolution_convert_fusion.q_ref.k_ref.v_ref, bf16[1024,2304]{1,0:T(8,128)(2,1)} %convolution_convert_fusion.q_ref.k_ref.v_ref, ...), custom_call_target="tpu_custom_call" | custom-call | tf_op jit(solution)/shard_map/attention_back/pallas_call | solution.py:680
  374.9 7.1 convolution_convert_fusion.2
  382.0 9.8 %convolution_convert_fusion.1 = bf16[3072,768]{1,0:T(8,128)(2,1)} fusion(bf16[1024,3072]{1,0:T(8,128)(2,1)} %copy-done.31, bf16[1024,768]{1,0:T(8,128)(2,1)S(1)} %fusion.20), kind=kOutput, calls=%fused_computation.13 | convolution fusion | flops 4834197504 | bytes 12582912 | tf_op jit(solution)/shard_map/dot_general | solution.py:1069
  391.8 4.2 fusion.6
  396.0 9.3 %scatter_custom_fusion.1 = bf16[2048,768]{1,0:T(8,128)(2,1)} fusion(s32[1024]{0:T(1024)} %copy-done.26, f32[1024,768]{1,0:T(8,128)} %copy-done.6, bf16[1024,768]{1,0:T(8,128)(2,1)S(1)} %gather_fusion.1, f32[1024,768]{1,0:T(8,128)} %get-tuple-element.139, bf16[]{:T(256)} %constant.52.clone.1, f32[1024]{0:T(1024)S(1)} %broadcast_multiply_fusion, ...), kind=kCustom, calls=%fused_computation.50 | custom fusion | flops 6291456 | bytes 11021824
  405.3 58.1 %rows_exchange.3 = bf16[8,256,768]{2,1,0:T(8,128)(2,1)} custom-call(bf16[8,256,768]{2,1,0:T(8,128)(2,1)} %bitcast.126), custom_call_target="tpu_custom_call" | custom-call | tf_op jit(solution)/shard_map/rows_exchange/pallas_call | solution.py:563
  463.4 108.7 %weight_grads_sum.1 = (f32[24,768]{1,0:T(8,128)}, f32[24,768]{1,0:T(8,128)}, f32[24,768]{1,0:T(8,128)}, f32[24,768]{1,0:T(8,128)}, f32[24,3072]{1,0:T(8,128)}, /*index=5*/f32[96,768]{1,0:T(8,128)}) custom-call(bf16[32,24,768]{2,1,0:T(8,128)(2,1)} %bitcast.130, bf16[32,24,768]{2,1,0:T(8,128)(2,1)} %bitcast.131, bf16[32,24,768]{2,1,0:T(8,128)(2,1)} %bitcast.132, ...), custom_call_target="tpu_custom_call" | custom-call | tf_op jit(solution)/shard_map/weight_grads_sum/pallas_call | solution.py:249
  586.2 87.3 %table_total.1 = (bf16[4096,768]{1,0:T(8,128)(2,1)}, f32[1,1]{1,0:T(1,128)}) custom-call(bf16[2048,768]{1,0:T(8,128)(2,1)} %bitcast.125, s32[1,2048]{1,0:T(1,128)} %bitcast.26.ask_ref), custom_call_target="tpu_custom_call" | custom-call | tf_op jit(solution)/shard_map/table_total/pallas_call | solution.py:425
  678.2 16.0 %small_total.1 = f32[24,128]{1,0:T(8,128)} custom-call(f32[24,128]{1,0:T(8,128)} %fusion.72.x_ref), custom_call_target="tpu_custom_call" | custom-call | tf_op jit(solution)/shard_map/small_total/pallas_call | solution.py:306
  708.9 29.2 %add_subtract_fusion = (f32[4016,768]{1,0:T(8,128)}, f32[4016,768]{1,0:T(8,128)}, f32[4016,768]{1,0:T(8,128)}) fusion(f32[4016,768]{1,0:T(8,128)} %param.33, f32[]{:T(128)S(6)} %min.3, bf16[4096,768]{1,0:T(8,128)(2,1)} %get-tuple-element.54, f32[4016,768]{1,0:T(8,128)} %param.34, f32[4016,768]{1,0:T(8,128)} %param.35), kind=kLoop, calls=%fused_computation.8 | loop fusion | flops 49348608 | bytes 80191488 | tf_op jit(solution)/shard_map/sub | solution.py:120
  (175 shorter events, 84.5 us)
Async XLA Ops:
  13.2 113.3 %all-to-all-start = ((s32[8,1,256]{2,1,0:T(1,128)}), s32[8,1,256]{2,1,0:T(1,128)}, u32[]{:S(2)}, u32[]{:S(2)}) async-start(s32[8,1,256]{2,1,0:T(1,128)} %bitcast.5), calls=%async_computation | async-start | bytes 16384 | tf_op jit(solution)/shard_map/all_to_all | solution.py:1030
  201.5 15.2 %copy-start.19 = (f32[768]{0:T(1024)S(1)}, f32[768]{0:T(1024)}, u32[]{:S(2)}) copy-start(f32[768]{0:T(1024)} %get-tuple-element.109) | copy-start | bytes 9220
  216.7 7.9 %copy-start.1 = (f32[6,2,1024]{2,1,0:T(2,128)S(1)}, f32[6,2,1024]{2,1,0:T(2,128)}, u32[]{:S(2)}) copy-start(f32[6,2,1024]{2,1,0:T(2,128)} %reshape.441.w_ref) | copy-start | bytes 147460
  216.7 7.9 %copy-start.3 = (s32[2]{0:T(128)S(1)}, s32[2]{0:T(128)}, u32[]{:S(2)}) copy-start(s32[2]{0:T(128)} %len_ref.3) | copy-start | bytes 28
  216.7 30.7 %slice-start = ((s8[4718592]{0:T(1024)(128)(4,1)}), s8[4194304]{0:T(1024)(128)(4,1)S(1)}, s32[]{:S(2)}) async-start(s8[4718592]{0:T(1024)(128)(4,1)} %bitcast.151), calls=%async_computation.1 | async-start | bytes 8388608
  224.6 21.2 %copy-start.28 = (bf16[32,24,768]{2,1,0:T(8,128)(2,1)S(1)}, bf16[32,24,768]{2,1,0:T(8,128)(2,1)}, u32[]{:S(2)}) copy-start(bf16[32,24,768]{2,1,0:T(8,128)(2,1)} %get-tuple-element.40) | copy-start | bytes 3538948
  224.6 22.8 %slice-start.1 = ((s8[4718592]{0:T(1024)(128)(4,1)}), s8[524288]{0:T(1024)(128)(4,1)S(1)}, s32[]{:S(2)}) async-start(s8[4718592]{0:T(1024)(128)(4,1)} %bitcast.151), calls=%async_computation.2 | async-start | bytes 1048576
  245.9 7.4 slice-start.4
  253.3 6.9 copy-start.16
  297.1 10.1 %slice-start.2 = ((s8[4718592]{0:T(1024)(128)(4,1)}), s8[4194304]{0:T(1024)(128)(4,1)S(1)}, s32[]{:S(2)}) async-start(s8[4718592]{0:T(1024)(128)(4,1)} %bitcast.154), calls=%async_computation.3 | async-start | bytes 8388608
  298.2 9.1 %copy-start.8 = (f32[1024,768]{1,0:T(8,128)S(1)}, f32[1024,768]{1,0:T(8,128)}, u32[]{:S(2)}) copy-start(f32[1024,768]{1,0:T(8,128)} %copy-done.7) | copy-start | bytes 9437188
  298.2 9.1 %slice-start.3 = ((s8[4718592]{0:T(1024)(128)(4,1)}), s8[524288]{0:T(1024)(128)(4,1)S(1)}, s32[]{:S(2)}) async-start(s8[4718592]{0:T(1024)(128)(4,1)} %bitcast.154), calls=%async_computation.4 | async-start | bytes 1048576
  314.9 57.4 %copy-start.6 = (f32[1024,768]{1,0:T(8,128)}, f32[1024,768]{1,0:T(8,128)S(1)}, u32[]{:S(2)}) copy-start(f32[1024,768]{1,0:T(8,128)S(1)} %multiply_add_fusion.1) | copy-start | bytes 9437188
  366.9 7.9 %slice-start.6 = ((s8[6291456]{0:T(1024)(128)(4,1)}), s8[4194304]{0:T(1024)(128)(4,1)S(1)}, s32[]{:S(2)}) async-start(s8[6291456]{0:T(1024)(128)(4,1)} %bitcast.163), calls=%async_computation.7 | async-start | bytes 8388608
  673.5 34.3 %copy-start.10 = (f32[96,768]{1,0:T(8,128)S(1)}, f32[96,768]{1,0:T(8,128)}, u32[]{:S(2)}) copy-start(f32[96,768]{1,0:T(8,128)} %param.45) | copy-start | bytes 884740
  673.5 34.3 %copy-start.11 = (f32[96,768]{1,0:T(8,128)S(1)}, f32[96,768]{1,0:T(8,128)}, u32[]{:S(2)}) copy-start(f32[96,768]{1,0:T(8,128)} %get-tuple-element.53) | copy-start | bytes 884740
  673.5 34.3 %copy-start.14 = (f32[96,768]{1,0:T(8,128)S(1)}, f32[96,768]{1,0:T(8,128)}, u32[]{:S(2)}) copy-start(f32[96,768]{1,0:T(8,128)} %param.46) | copy-start | bytes 884740
  673.5 34.3 %copy-start.15 = (f32[96,768]{1,0:T(8,128)S(1)}, f32[96,768]{1,0:T(8,128)}, u32[]{:S(2)}) copy-start(f32[96,768]{1,0:T(8,128)} %param.47) | copy-start | bytes 884740
  708.8 29.2 %copy-start.18 = (f32[3,768]{1,0:T(4,128)S(1)}, f32[3,768]{1,0:T(4,128)}, u32[]{:S(2)}) copy-start(f32[3,768]{1,0:T(4,128)} %param.48) | copy-start | bytes 27652
  708.8 29.2 %copy-start.22 = (f32[3,768]{1,0:T(4,128)S(1)}, f32[3,768]{1,0:T(4,128)}, u32[]{:S(2)}) copy-start(f32[3,768]{1,0:T(4,128)} %param.49) | copy-start | bytes 27652
  708.8 29.2 %copy-start.23 = (f32[3,768]{1,0:T(4,128)S(1)}, f32[3,768]{1,0:T(4,128)}, u32[]{:S(2)}) copy-start(f32[3,768]{1,0:T(4,128)} %param.50) | copy-start | bytes 27652
  708.8 29.9 %copy-start.17 = (f32[32,12]{0,1:T(8,128)S(1)}, f32[32,12]{0,1:T(8,128)}, u32[]{:S(2)}) copy-start(f32[32,12]{0,1:T(8,128)} %param.51) | copy-start | bytes 4612
  708.8 29.9 %copy-start.24 = (f32[32,12]{0,1:T(8,128)S(1)}, f32[32,12]{0,1:T(8,128)}, u32[]{:S(2)}) copy-start(f32[32,12]{0,1:T(8,128)} %param.52) | copy-start | bytes 4612
  708.9 29.9 %copy-start.25 = (f32[32,12]{0,1:T(8,128)S(1)}, f32[32,12]{0,1:T(8,128)}, u32[]{:S(2)}) copy-start(f32[32,12]{0,1:T(8,128)} %param.53) | copy-start | bytes 4612
  (17 other events, 64.5 us)

commit v4 on v3

--- a/solution.py
+++ b/solution.py
@@ -432,108 +432,6 @@
         name="table_total",
     )(arrived, asked)
 
-
-def gather_kernel(n_dp, n_pair, pieces, n_in, *refs):
-    k = len(pieces)
-    ins, outs = refs[:n_in], refs[n_in : 2 * n_in]
-    bufs = refs[2 * n_in : 2 * n_in + k]
-    send, recv, csend, crecv, wsem, isem = refs[2 * n_in + k :]
-    me = my_index(n_pair)
-    steps = (n_dp * n_pair - 1).bit_length() - 1
-    half = 1 << steps
-    orders = [bit_order(n_dp, n_pair, color) for _, _, _, color in pieces]
-
-    def load(a):
-        which, low, high, _ = pieces[a]
-        return pltpu.make_async_copy(
-            ins[which].at[:, pl.ds(low, high - low)], bufs[a].at[0], isem.at[a]
-        )
-
-    for a in range(k):
-        load(a).start()
-    greet([place(me ^ (1 << bit), n_pair) for bit in range(steps + 1)])
-
-    def write_out(a, lo, count, core):
-        which, low, high, _ = pieces[a]
-        for p in range(lo, lo + count):
-            block = me ^ (offset(orders[a], p) + core)
-            pltpu.make_async_copy(
-                bufs[a].at[p + core * half],
-                outs[which].at[block, :, pl.ds(low, high - low)],
-                wsem.at[a],
-            ).start()
-
-    def forward(a, s):
-        lo, count = (0, 1) if s == 0 else (1 << (s - 1), 1 << (s - 1))
-        return remote(
-            bufs[a].at[pl.ds(lo, count)],
-            bufs[a].at[pl.ds(half + lo, count)],
-            csend.at[a, s],
-            crecv.at[a, s],
-            place(me ^ 1, n_pair),
-        )
-
-    def hop(a, s):
-        return remote(
-            bufs[a].at[pl.ds(0, 1 << s)],
-            bufs[a].at[pl.ds(1 << s, 1 << s)],
-            send.at[a, s],
-            recv.at[a, s],
-            place(me ^ (1 << orders[a][s]), n_pair),
-        )
-
-    for a in range(k):
-        load(a).wait()
-        hop(a, 0).start()
-    for a in range(k):
-        forward(a, 0).start()
-        write_out(a, 0, 1, 0)
-    for s in range(steps):
-        for a in range(k):
-            hop(a, s).wait_recv()
-            if s + 1 < steps:
-                hop(a, s + 1).start()
-            forward(a, s + 1).start()
-            write_out(a, 1 << s, 1 << s, 0)
-        for a in range(k):
-            forward(a, s).wait_recv()
-            lo, count = (0, 1) if s == 0 else (1 << (s - 1), 1 << (s - 1))
-            write_out(a, lo, count, 1)
-    for a in range(k):
-        forward(a, steps).wait_recv()
-        write_out(a, half // 2, half // 2, 1)
-    for a in range(k):
-        for s in range(steps):
-            hop(a, s).wait_send()
-        for s in range(steps + 1):
-            forward(a, s).wait_send()
-        pltpu.make_async_copy(bufs[a], bufs[a], wsem.at[a]).wait()
-
-
-def gather_all(shards, pieces, n_dp, n_pair, cid):
-    n, k = n_dp * n_pair, len(pieces)
-    steps = (n - 1).bit_length() - 1
-    return pl.pallas_call(
-        functools.partial(gather_kernel, n_dp, n_pair, pieces, len(shards)),
-        out_shape=[jax.ShapeDtypeStruct((n,) + s.shape, s.dtype) for s in shards],
-        in_specs=[ANY] * len(shards),
-        out_specs=[ANY] * len(shards),
-        scratch_shapes=[
-            pltpu.VMEM((n, shards[p[0]].shape[0], p[2] - p[1]), jnp.bfloat16) for p in pieces
-        ]
-        + [
-            pltpu.SemaphoreType.DMA((k, steps)),
-            pltpu.SemaphoreType.DMA((k, steps)),
-            pltpu.SemaphoreType.DMA((k, steps + 1)),
-            pltpu.SemaphoreType.DMA((k, steps + 1)),
-            pltpu.SemaphoreType.DMA((k,)),
-            pltpu.SemaphoreType.DMA((k,)),
-        ],
-        compiler_params=pltpu.CompilerParams(
-            collective_id=cid, has_side_effects=True, vmem_limit_bytes=VMEM_LIMIT
-        ),
-        name="weights_gather",
-    )(*shards)
 
 def exchange_kernel(n_dp, x_ref, o_ref, send, recv, lsem):
     me = lax.axis_index("dp"); pr = lax.axis_index("pair")
@@ -712,6 +610,240 @@
     return pieces + [(down, 0, cut, 0), (down, cut, widths[down], 1)]
 
 
+NN = (((1,), (0,)), ((), ()))
+
+
+def triangle(size):
+    rows = lax.broadcasted_iota(jnp.int32, (size, size), 0)
+    columns = lax.broadcasted_iota(jnp.int32, (size, size), 1)
+    return jnp.where(rows < columns, 1.0, 0.0).astype(jnp.bfloat16)
+
+
+def digits(numbers):
+    high = numbers // 64
+    row = lax.broadcasted_iota(jnp.int32, (8, numbers.shape[1]), 0)
+    both = jnp.where(row == 0, high, jnp.where(row == 1, numbers - 64 * high, 0))
+    return both.astype(jnp.float32).astype(jnp.bfloat16)
+
+
+def upright(pairs):
+    row = lax.broadcasted_iota(jnp.int32, (8, 128), 0)
+    value = jnp.where(row == 0, 64.0, jnp.where(row == 1, 1.0, 0.0)).astype(jnp.bfloat16)
+    return lax.dot_general(pairs, value, TN, preferred_element_type=jnp.float32)
+
+
+def hits_by_lane(numbers, width, base):
+    lane = lax.broadcasted_iota(jnp.int32, (1, 128), 1).astype(jnp.float32) + base
+    tiles = [
+        jnp.where(numbers == lane + 128.0 * tile, 1.0, 0.0).astype(jnp.bfloat16)
+        for tile in range(width // 128)
+    ]
+    return jnp.concatenate(tiles, axis=1)
+
+
+def front_kernel(n_dp, n_pair, pieces, n_in, *refs):
+    k = len(pieces)
+    owner_ref, row_ref, table_ref = refs[:3]
+    shards = refs[3 : 3 + n_in]
+    emb_ref, key_ref, asked_ref = refs[3 + n_in : 6 + n_in]
+    outs = refs[6 + n_in : 6 + 2 * n_in]
+    rest = refs[6 + 2 * n_in :]
+    bufs, rest = rest[:k], rest[k:]
+    (wide, table, ask_out, ask_in, rows_out, rows_in, total, hop_send, hop_recv, core_send,
+     core_recv, out_sem, table_sem, ask_send, ask_recv, row_send, row_recv) = rest
+    dp, pair = lax.axis_index("dp"), lax.axis_index("pair")
+    me = dp * n_pair + pair
+    steps = (n_dp * n_pair - 1).bit_length() - 1
+    half = 1 << steps
+    orders = [bit_order(n_dp, n_pair, color) for _, _, _, color in pieces]
+    tokens = owner_ref.shape[1]
+    cap = ask_out.shape[2]
+    table_rows = table_ref.shape[0]
+    load = pltpu.make_async_copy(table_ref, wide, table_sem)
+    load.start()
+    peers = [{"dp": dp ^ j, "pair": pair} for j in range(1, n_dp)]
+    sem = pltpu.get_barrier_semaphore()
+    mates = [{"dp": dp, "pair": pair ^ j} for j in (1, 2)]
+    for target in peers + mates:
+        pl.semaphore_signal(sem, inc=1, device_id=target, device_id_type=MESH)
+    for a, (which, low, high, _) in enumerate(pieces):
+        bufs[a][0] = shards[which][:, low:high].astype(jnp.bfloat16)
+
+    owner = owner_ref[...]
+    by_owner = lax.broadcasted_iota(jnp.int32, (n_dp, tokens), 0) == owner
+    ranks = jnp.dot(
+        jnp.where(by_owner, 1.0, 0.0).astype(jnp.bfloat16),
+        triangle(tokens),
+        preferred_element_type=jnp.float32,
+    )
+    rank = jnp.sum(jnp.where(by_owner, ranks, 0.0), axis=0, keepdims=True)
+    key = owner * cap + rank.astype(jnp.int32)
+    key_ref[...] = key
+    wanted = digits(row_ref[...])
+    for j in range(n_dp):
+        slot = lax.broadcasted_iota(jnp.int32, (cap, tokens), 0) + (dp ^ j) * cap
+        chosen = jnp.where(slot == key, 1.0, 0.0).astype(jnp.bfloat16)
+        ask_out[j] = lax.dot_general(wanted, chosen, NT, preferred_element_type=jnp.float32)
+    pl.semaphore_wait(sem, n_dp + 1)
+
+    def ask(j):
+        return remote(ask_out.at[j], ask_in.at[j], ask_send.at[j], ask_recv.at[j], peers[j - 1])
+
+    def reply(j):
+        return remote(rows_out.at[j], rows_in.at[j], row_send.at[j], row_recv.at[j], peers[j - 1])
+
+    def forward(a, s):
+        lo, count = (0, 1) if s == 0 else (1 << (s - 1), 1 << (s - 1))
+        return remote(
+            bufs[a].at[pl.ds(lo, count)],
+            bufs[a].at[pl.ds(half + lo, count)],
+            core_send.at[a, s],
+            core_recv.at[a, s],
+            place(me ^ 1, n_pair),
+        )
+
+    def hop(a, s):
+        return remote(
+            bufs[a].at[pl.ds(0, 1 << s)],
+            bufs[a].at[pl.ds(1 << s, 1 << s)],
+            hop_send.at[a, s],
+            hop_recv.at[a, s],
+            place(me ^ (1 << orders[a][s]), n_pair),
+        )
+
+    def write_out(a, lo, count, core):
+        which, low, high, _ = pieces[a]
+        for p in range(lo, lo + count):
+            block = me ^ (offset(orders[a], p) + core)
+            pltpu.make_async_copy(
+                bufs[a].at[p + core * half],
+                outs[which].at[block, :, pl.ds(low, high - low)],
+                out_sem.at[a],
+            ).start()
+
+    def weights_step(s):
+        for a in range(k):
+            hop(a, s).wait_recv()
+            if s + 1 < steps:
+                hop(a, s + 1).start()
+            forward(a, s + 1).start()
+            write_out(a, 1 << s, 1 << s, 0)
+        for a in range(k):
+            forward(a, s).wait_recv()
+            lo, count = (0, 1) if s == 0 else (1 << (s - 1), 1 << (s - 1))
+            write_out(a, lo, count, 1)
+
+    far = sorted(range(1, n_dp), reverse=True)
+    for j in far:
+        ask(j).start()
+    for a in range(k):
+        hop(a, 0).start()
+    for a in range(k):
+        forward(a, 0).start()
+        write_out(a, 0, 1, 0)
+    load.wait()
+
+    def narrow(i, carry):
+        part = pl.ds(pl.multiple_of(i * 16, 16), 16)
+        table[part] = wide[part].astype(jnp.bfloat16)
+        return carry
+
+    lax.fori_loop(0, table_rows // 16, narrow, 0)
+    if table.shape[0] > table_rows:
+        table[table_rows:] = jnp.zeros((table.shape[0] - table_rows, table.shape[1]), jnp.bfloat16)
+
+    def answer(j, target):
+        asked = ask_out if j == 0 else ask_in
+        hit = hits_by_lane(upright(asked[j].astype(jnp.bfloat16)), table.shape[0], 0.0)
+        target[j] = jnp.dot(hit, table[...], preferred_element_type=jnp.float32).astype(jnp.bfloat16)
+        asked_ref[j] = (64.0 * asked[j, 0:1] + asked[j, 1:2]).astype(jnp.int32)
+
+    for turn, j in enumerate(far):
+        ask(j).wait_recv()
+        answer(j, rows_out)
+        reply(j).start()
+        if turn == 1:
+            weights_step(0)
+        if turn == 4:
+            weights_step(1)
+    answer(0, rows_in)
+    upright_key = upright(digits(key))
+
+    def seat(j, first):
+        place_hit = hits_by_lane(upright_key, cap, ((dp ^ j) * cap).astype(jnp.float32))
+        got = jnp.dot(place_hit, rows_in[j], preferred_element_type=jnp.float32)
+        total[...] = got if first else total[...] + got
+
+    seat(0, True)
+    near = list(reversed(far))
+    for turn, j in enumerate(near):
+        reply(j).wait_recv()
+        seat(j, False)
+        if turn == len(near) // 3:
+            for s in range(2, steps - 1):
+                weights_step(s)
+    emb_ref[...] = total[...].astype(jnp.bfloat16)
+    weights_step(steps - 1)
+    for a in range(k):
+        forward(a, steps).wait_recv()
+        write_out(a, half // 2, half // 2, 1)
+    for j in far:
+        ask(j).wait_send()
+        reply(j).wait_send()
+    for a in range(k):
+        for s in range(steps):
+            hop(a, s).wait_send()
+        for s in range(steps + 1):
+            forward(a, s).wait_send()
+        pltpu.make_async_copy(bufs[a], bufs[a], out_sem.at[a]).wait()
+
+
+def front(owner, row, table, shards, pieces, cap, n_dp, n_pair, cid):
+    n, k = n_dp * n_pair, len(pieces)
+    steps = (n - 1).bit_length() - 1
+    tokens = owner.shape[1]
+    table_rows, width = table.shape
+    padded = -(-table_rows // 256) * 256
+    sem = pltpu.SemaphoreType.DMA
+    return pl.pallas_call(
+        functools.partial(front_kernel, n_dp, n_pair, pieces, len(shards)),
+        out_shape=[
+            jax.ShapeDtypeStruct((tokens, width), jnp.bfloat16),
+            jax.ShapeDtypeStruct((1, tokens), jnp.int32),
+            jax.ShapeDtypeStruct((n_dp, 1, cap), jnp.int32),
+        ]
+        + [jax.ShapeDtypeStruct((n,) + s.shape, jnp.bfloat16) for s in shards],
+        in_specs=[VM, VM, ANY] + [VM] * len(shards),
+        out_specs=[VM] * 3 + [ANY] * len(shards),
+        scratch_shapes=[
+            pltpu.VMEM((n, shards[p[0]].shape[0], p[2] - p[1]), jnp.bfloat16) for p in pieces
+        ]
+        + [
+            pltpu.VMEM((table_rows, width), jnp.float32),
+            pltpu.VMEM((padded, width), jnp.bfloat16),
+            pltpu.VMEM((n_dp, 8, cap), jnp.float32),
+            pltpu.VMEM((n_dp, 8, cap), jnp.float32),
+            pltpu.VMEM((n_dp, cap, width), jnp.bfloat16),
+            pltpu.VMEM((n_dp, cap, width), jnp.bfloat16),
+            pltpu.VMEM((tokens, width), jnp.float32),
+            sem((k, steps)),
+            sem((k, steps)),
+            sem((k, steps + 1)),
+            sem((k, steps + 1)),
+            sem((k,)),
+            sem,
+            sem((n_dp,)),
+            sem((n_dp,)),
+            sem((n_dp,)),
+            sem((n_dp,)),
+        ],
+        compiler_params=pltpu.CompilerParams(
+            collective_id=cid, has_side_effects=True, vmem_limit_bytes=VMEM_LIMIT
+        ),
+        name="rows_and_weights",
+    )(owner, row, table, *shards)
+
+
 def local_plain(
     token_owner,
     token_row,
@@ -1008,30 +1140,23 @@
     tok_total = doc_count * seq_len
     owners = lax.axis_size("dp")
     capacity = max(2, 2 * tok_total // owners)
-    low_mats = (
-        qkv_weight.astype(jnp.bfloat16),
-        out_weight.astype(jnp.bfloat16),
-        in_weight.astype(jnp.bfloat16),
-        down_weight.astype(jnp.bfloat16),
-    )
     holders = lax.axis_size("pair")
-    pieces = weight_pieces([low.shape[1] for low in low_mats])
+    shards = (qkv_weight, out_weight, in_weight, down_weight)
+    embedded_low, slot_keys, asked_rows, *full = front(
+        token_owner.reshape(1, -1),
+        token_row.reshape(1, -1),
+        embed_table,
+        shards,
+        weight_pieces([shard.shape[1] for shard in shards]),
+        capacity,
+        owners,
+        holders,
+        1,
+    )
     qkv_full, out_full, in_full, down_full = (
-        full.reshape(-1, full.shape[2])
-        for full in gather_all(low_mats, pieces, owners, holders, 1)
-    )
-    tok_owner = token_owner.reshape(-1)
-    tok_row = token_row.reshape(-1)
-    owner_hits = (tok_owner[:, None] == jnp.arange(owners, dtype=jnp.int32)[None, :]).astype(
-        jnp.int32
-    )
-    slot_rank = jnp.sum((jnp.cumsum(owner_hits, axis=0) - 1) * owner_hits, axis=1)
-    requests = jnp.zeros((owners, capacity), jnp.int32).at[tok_owner, slot_rank].set(tok_row)
-    asked_rows = lax.all_to_all(requests, "dp", split_axis=0, concat_axis=0, tiled=True)
-    looked = jnp.take(embed_table, asked_rows.reshape(-1), axis=0).astype(jnp.bfloat16)
-    answer = exchange(looked.reshape(asked_rows.shape + (model_width,)), owners, 2)
-    replies, asked_rows = (answer, asked_rows)
-    embedded = replies[tok_owner, slot_rank].astype(jnp.float32)
+        matrix.reshape(-1, matrix.shape[2]) for matrix in full
+    )
+    embedded = embedded_low.astype(jnp.float32)
     positions = jnp.arange(seq_len)
     live = positions[None, :] < lengths[:, None]
     normed_one, inverse_one = rms_forward(embedded, norm_gains[0])
@@ -1108,11 +1233,12 @@
     grad_emb_part, gain_one = rms_backward(embedded, inverse_one, norm_gains[0], grad_normed_one)
     grad_embedded = grad_residual + grad_emb_part
     sendback = (
-        jnp.zeros((owners, capacity, model_width), jnp.bfloat16)
-        .at[tok_owner, slot_rank]
+        jnp.zeros((owners * capacity, model_width), jnp.bfloat16)
+        .at[slot_keys[0]]
         .set(grad_embedded.astype(jnp.bfloat16))
-    )
+    ).reshape(owners, capacity, model_width)
     arrived = exchange(sendback, owners, 4)
+    arrived = arrived[lax.axis_index("dp") ^ jnp.arange(owners)]
     table_rows = embed_table.shape[0]
     table_grad, table_square = table_total(
         arrived.reshape(-1, model_width),

time: 753 us -> 694 us (0.922)
  local copies, waits for them, and re-layouts: 51.9 us -> 15.5 us
  other arithmetic: 85.5 us -> 61.4 us
    pallas_call x1, Pallas kernels: 87.8 us -> 170 us  [front(): pl.pallas_call(functools.partial(front_kernel, n_dp, n_pair, pieces, len(...]
    pallas_call x2 -> x1, Pallas kernels: 117 us -> 57.1 us  [exchange(): pl.pallas_call(functools.partial(exchange_kernel, n_dp), out_shape=jax.Sh...]
    gather x2 -> x1, local copies, waits for them, and re-layouts: 27.7 us -> 4.3 us  [local_fast(): arrived = arrived[lax.axis_index('dp') ^ jnp.arange(owners)]]
    pallas_call x1, Pallas kernels: 31.3 us -> 14.4 us  [pooled_loss(): pl.pallas_call(functools.partial(loss_kernel, n, n_pair, docs), out_shape...]
    unnamed x13 -> x8, other arithmetic: 10.9 us -> 0.02 us
    scatter x0 -> x1, other arithmetic: none -> 9.3 us  [local_fast(): sendback = jnp.zeros((owners * capacity, model_width), jnp.bfloat16).at[s...]
    convert_element_type x6 -> x0, other arithmetic: 9.07 us -> none  [the longest x1 2.01 us: local_fast(): jnp.take(embed_table, asked_rows.reshape(-1), axis=0).astype(jnp.bfloat16)]
    unnamed x89 -> x136, local copies, waits for them, and re-layouts: 13.1 us -> 5.24 us
  transfers between devices with their start and end apart: 1 -> 0, of which waited for: 0 -> 0; matrix products, arithmetic and copies ran while one was open for 2% -> 0% of each run, Pallas kernels for 12% -> 0%
where the time goes in v4:
time: 694 us; the launch traced here: 683 us
  Pallas kernels  516 us (74%)
  matrix products  80.6 us (12%)
  other arithmetic  61.4 us (9%)
  local copies, waits for them, and re-layouts  15.5 us (2%)
  between operations  10.3 us (1%)
    pallas_call x1, Pallas kernels, front(): pl.pallas_call(functools.partial(front_kernel, n_dp, n_pair, pieces, len(...  170 us
    pallas_call x1, Pallas kernels, scatter_all(): pl.pallas_call(functools.partial(scatter_kernel, n_dp, n_pair, pieces, le...  109 us
    pallas_call x1, Pallas kernels, table_total(): pl.pallas_call(functools.partial(table_kernel, n_pair, rows, chunk), out_...  86.5 us
    pallas_call x1, Pallas kernels, exchange(): pl.pallas_call(functools.partial(exchange_kernel, n_dp), out_shape=jax.Sh...  57.1 us
    pallas_call x1, Pallas kernels, attention_back(): pl.pallas_call(backward_kernel, grid_spec=pltpu.PrefetchScalarGridSpec(nu...  42.2 us
    sub x7, other arithmetic, adam_step(): weight - rate * (first_hat / (jnp.sqrt(second_hat) + adam_eps) + shrink *...  34.8 us
    pallas_call x1, Pallas kernels, attention(): pl.pallas_call(forward_kernel, grid_spec=pltpu.PrefetchScalarGridSpec(num...  21.9 us
    pallas_call x1, Pallas kernels, small_total(): pl.pallas_call(functools.partial(total_kernel, n, n_pair), out_shape=jax....  15.2 us

profile of v4, /device:TPU:0, one launch (start us, length us, event | category | flops | bytes accessed | tf_op | source)
XLA Modules:
  0.0 683.4 jit_solution(12280546432555182099)
XLA Ops:
  1.9 169.6 %rows_and_weights.1 = (bf16[1024,768]{1,0:T(8,128)(2,1)}, s32[1,1024]{1,0:T(1,128)}, s32[8,1,256]{2,1,0:T(1,128)}, bf16[32,24,2304]{2,1,0:T(8,128)(2,1)}, bf16[3...) custom-call(s32[1,1024]{1,0:T(1,128)} %bitcast.120, s32[1,1024]{1,0:T(1,128)} %bitcast.118, ...), custom_call_target="tpu_custom_call" | custom-call | tf_op jit(solution)/shard_map/rows_and_weights/pallas_call | solution.py:808
  174.3 8.6 %convolution_convert_fusion.q_ref.k_ref.v_ref = bf16[1024,2304]{1,0:T(8,128)(2,1)} fusion(bf16[768,2304]{1,0:T(8,128)(2,1)} %bitcast.112, bf16[1024,768]{1,0:T(8,128)(2,1)} %get-tuple-element.42, f32[768]{0:T(1024)S(1)} %get-tuple-element.92, f32[1024]{0:T(1024)S(1)} %add_rsqrt_fusion.2), kind=kOutput, calls=%fused_computation.9 | convolution fusion | flops 3629383680 | bytes 9837568 | tf_op jit(solution)/shard_map/dot_general | solution.py:1164
  183.2 21.9 %attention.1 = bf16[1024,768]{1,0:T(8,128)(2,1)S(1)} custom-call(s32[2]{0:T(128)S(1)} %copy-done.3, bf16[1024,2304]{1,0:T(8,128)(2,1)} %convolution_convert_fusion.q_ref.k_ref.v_ref, bf16[1024,2304]{1,0:T(8,128)(2,1)} %convolution_convert_fusion.q_ref.k_ref.v_ref, bf16[1024,2304]{1,0:T(8,128)(2,1)} %convolution_convert_fusion.q_ref.k_ref.v_ref, ...), custom_call_target="tpu_custom_call" | custom-call | tf_op jit(solution)/shard_map/attention/pallas_call | solution.py:512
  206.6 9.3 %maximum_convert_fusion = bf16[1024,3072]{1,0:T(8,128)(2,1)S(1)} fusion(bf16[768,3072]{1,0:T(8,128)(2,1)} %bitcast.125, f32[1024,768]{1,0:T(8,128)S(1)} %get-tuple-element.115, f32[768]{0:T(1024)S(1)} %get-tuple-element.91, f32[1024]{0:T(1024)S(1)} %add_rsqrt_fusion.1), kind=kOutput, calls=%fused_computation.4 | convolution fusion | flops 4840488960 | bytes 14162944 | tf_op jit(solution)/shard_map/dot_general | solution.py:1171
  216.0 5.3 multiply_reduce_fusion.2
  224.7 14.4 %pooled_loss.1 = (f32[1,1]{1,0:T(1,128)}, f32[2,768]{1,0:T(2,128)}) custom-call(f32[2,768]{1,0:T(2,128)} %broadcast_divide_fusion.1.x_ref, s32[64,1]{1,0:T(8,128)} %copy.67.pos_ref, s32[64,7]{1,0:T(8,128)} %copy.68.neg_ref, s32[64,1]{1,0:T(8,128)} %copy.69.count_ref), custom_call_target="tpu_custom_call" | custom-call | tf_op jit(solution)/shard_map/pooled_loss/pallas_call | solution.py:356
  243.0 8.7 %select_convert_fusion = bf16[1024,3072]{1,0:T(8,128)(2,1)S(1)} fusion(bf16[1024,3072]{1,0:T(8,128)(2,1)S(1)} %copy-done.55, bf16[1024,768]{1,0:T(8,128)(2,1)S(1)} %fusion.20, bf16[3072,768]{1,0:T(8,128)(2,1)} %bitcast.129), kind=kOutput, calls=%fused_computation.3 | convolution fusion | flops 4841275392 | bytes 18874368 | tf_op jit(solution)/shard_map/dot_general | solution.py:1197
  251.8 6.0 multiply_reduce_fusion
  261.3 42.2 %attention_back.1 = (bf16[3,1024,768]{2,1,0:T(8,128)(2,1)}, f32[6,2,8,256]{3,2,1,0:T(8,128)S(1)}) custom-call(s32[2]{0:T(128)S(1)} %copy-done.3, bf16[1024,2304]{1,0:T(8,128)(2,1)} %convolution_convert_fusion.q_ref.k_ref.v_ref, bf16[1024,2304]{1,0:T(8,128)(2,1)} %convolution_convert_fusion.q_ref.k_ref.v_ref, ...), custom_call_target="tpu_custom_call" | custom-call | tf_op jit(solution)/shard_map/attention_back/pallas_call | solution.py:578
  303.5 3.0 fusion.32
  308.0 4.0 fusion.6
  312.0 9.3 %scatter_custom_fusion = bf16[2048,768]{1,0:T(8,128)(2,1)} fusion(s32[1024]{0:T(1024)S(1)} %bitcast.122, f32[1024,768]{1,0:T(8,128)} %copy-done.7, bf16[1024,768]{1,0:T(8,128)(2,1)S(1)} %copy-done.5, f32[1024,768]{1,0:T(8,128)} %get-tuple-element.119, f32[1024]{0:T(1024)S(1)} %broadcast_multiply_fusion, bf16[]{:T(256)} %constant.46.clone.1, ...), kind=kCustom, calls=%fused_computation.47 | custom fusion | flops 6291456 | bytes 11022338 | tf_op jit(solution)/shard_map/scatter | solution.py:1238
  321.3 57.1 %rows_exchange.1 = bf16[8,256,768]{2,1,0:T(8,128)(2,1)} custom-call(bf16[8,256,768]{2,1,0:T(8,128)(2,1)} %bitcast.104), custom_call_target="tpu_custom_call" | custom-call | tf_op jit(solution)/shard_map/rows_exchange/pallas_call | solution.py:461
  378.5 4.3 gather_fusion
  382.8 86.5 %table_total.1 = (bf16[4096,768]{1,0:T(8,128)(2,1)}, f32[1,1]{1,0:T(1,128)}) custom-call(bf16[2048,768]{1,0:T(8,128)(2,1)} %bitcast.103, s32[1,2048]{1,0:T(1,128)} %bitcast.119), custom_call_target="tpu_custom_call" | custom-call | tf_op jit(solution)/shard_map/table_total/pallas_call | solution.py:425
  469.3 4.7 fusion.38
  474.0 4.2 fusion.41
  478.2 4.3 fusion.44
  482.5 2.5 convolution_convert_fusion.4
  485.1 7.4 %convolution_convert_fusion.2 = bf16[768,3072]{1,0:T(8,128)(2,1)} fusion(bf16[1024,3072]{1,0:T(8,128)(2,1)S(1)} %bitcast.136, f32[1024,768]{1,0:T(8,128)S(1)} %copy-done.11, f32[768]{0:T(1024)S(1)} %copy-done.42, f32[1024]{0:T(1024)S(1)} %copy-done.40), kind=kOutput, calls=%fused_computation.11 | convolution fusion | flops 4836556800 | bytes 14162944 | tf_op jit(solution)/shard_map/dot_general | solution.py:1201
  492.5 7.0 %convolution_convert_fusion.1 = bf16[3072,768]{1,0:T(8,128)(2,1)} fusion(bf16[1024,3072]{1,0:T(8,128)(2,1)S(1)} %bitcast.138, bf16[1024,768]{1,0:T(8,128)(2,1)S(1)} %copy-done.13), kind=kOutput, calls=%fused_computation.10 | convolution fusion | flops 4834197504 | bytes 12582912 | tf_op jit(solution)/shard_map/dot_general | solution.py:1194
  499.5 108.9 %weight_grads_sum.1 = (f32[24,768]{1,0:T(8,128)}, f32[24,768]{1,0:T(8,128)}, f32[24,768]{1,0:T(8,128)}, f32[24,768]{1,0:T(8,128)}, f32[24,3072]{1,0:T(8,128)}, /*index=5*/f32[96,768]{1,0:T(8,128)}) custom-call(bf16[32,24,768]{2,1,0:T(8,128)(2,1)} %bitcast.107, bf16[32,24,768]{2,1,0:T(8,128)(2,1)} %bitcast.108, bf16[32,24,768]{2,1,0:T(8,128)(2,1)} %bitcast.109, ...), custom_call_target="tpu_custom_call" | custom-call | tf_op jit(solution)/shard_map/weight_grads_sum/pallas_call | solution.py:249
  623.8 15.2 %small_total.1 = f32[24,128]{1,0:T(8,128)} custom-call(f32[24,128]{1,0:T(8,128)} %fusion.69.x_ref), custom_call_target="tpu_custom_call" | custom-call | tf_op jit(solution)/shard_map/small_total/pallas_call | solution.py:306
  645.0 29.7 %add_subtract_fusion = (f32[4016,768]{1,0:T(8,128)}, f32[4016,768]{1,0:T(8,128)}, f32[4016,768]{1,0:T(8,128)}) fusion(f32[4016,768]{1,0:T(8,128)} %refs_2_.1, f32[]{:T(128)S(6)} %min.3, bf16[4096,768]{1,0:T(8,128)(2,1)} %get-tuple-element.60, f32[4016,768]{1,0:T(8,128)} %param.34, f32[4016,768]{1,0:T(8,128)} %param.35), kind=kLoop, calls=%fused_computation.6 | loop fusion | flops 49348608 | bytes 80191488 | tf_op jit(solution)/shard_map/sub | solution.py:120
  (203 shorter events, 39.2 us)
Async XLA Ops:
  172.4 85.3 %copy-start.41 = (f32[768]{0:T(1024)}, f32[768]{0:T(1024)S(1)}, u32[]{:S(2)}) copy-start(f32[768]{0:T(1024)S(1)} %get-tuple-element.91) | copy-start | bytes 9220
  172.4 139.6 %copy-start.37 = (f32[768]{0:T(1024)}, f32[768]{0:T(1024)S(1)}, u32[]{:S(2)}) copy-start(f32[768]{0:T(1024)S(1)} %get-tuple-element.92) | copy-start | bytes 9220
  174.2 137.8 %copy-start.35 = (f32[1024]{0:T(1024)}, f32[1024]{0:T(1024)S(1)}, u32[]{:S(2)}) copy-start(f32[1024]{0:T(1024)S(1)} %add_rsqrt_fusion.2) | copy-start | bytes 12292
  183.1 21.9 %copy-start.4 = (bf16[1024,768]{1,0:T(8,128)(2,1)S(1)}, bf16[1024,768]{1,0:T(8,128)(2,1)}, u32[]{:S(2)}) copy-start(bf16[1024,768]{1,0:T(8,128)(2,1)} %get-tuple-element.42) | copy-start | bytes 4718596
  183.2 21.9 %copy-start.51 = (bf16[32,24,768]{2,1,0:T(8,128)(2,1)S(1)}, bf16[32,24,768]{2,1,0:T(8,128)(2,1)}, u32[]{:S(2)}) copy-start(bf16[32,24,768]{2,1,0:T(8,128)(2,1)} %get-tuple-element.44) | copy-start | bytes 3538948
  205.1 10.9 %slice-start.2 = ((s8[4718592]{0:T(1024)(128)(4,1)}), s8[4194304]{0:T(1024)(128)(4,1)S(1)}, s32[]{:S(2)}) async-start(s8[4718592]{0:T(1024)(128)(4,1)} %bitcast.130), calls=%async_computation.2 | async-start | bytes 8388608
  206.6 9.3 %copy-start.9 = (f32[1024,768]{1,0:T(8,128)}, f32[1024,768]{1,0:T(8,128)S(1)}, u32[]{:S(2)}) copy-start(f32[1024,768]{1,0:T(8,128)S(1)} %get-tuple-element.115) | copy-start | bytes 9437188
  206.6 51.1 %copy-start.39 = (f32[1024]{0:T(1024)}, f32[1024]{0:T(1024)S(1)}, u32[]{:S(2)}) copy-start(f32[1024]{0:T(1024)S(1)} %add_rsqrt_fusion.1) | copy-start | bytes 12292
  221.3 17.9 %copy-start.48 = (s32[1,1024]{1,0:T(1,128)S(1)}, s32[1,1024]{1,0:T(1,128)}, u32[]{:S(2)}) copy-start(s32[1,1024]{1,0:T(1,128)} %get-tuple-element.51) | copy-start | bytes 12292
  241.9 9.8 %slice-start = ((s8[4718592]{0:T(1024)(128)(4,1)}), s8[4194304]{0:T(1024)(128)(4,1)S(1)}, s32[]{:S(2)}) async-start(s8[4718592]{0:T(1024)(128)(4,1)} %bitcast.126), calls=%async_computation | async-start | bytes 8388608
  261.3 42.2 %copy-start.20 = (bf16[32,24,2304]{2,1,0:T(8,128)(2,1)S(1)}, bf16[32,24,2304]{2,1,0:T(8,128)(2,1)}, u32[]{:S(2)}) copy-start(bf16[32,24,2304]{2,1,0:T(8,128)(2,1)} %get-tuple-element.43) | copy-start | bytes 10616836
  474.0 11.1 %slice-start.4 = ((s8[6291456]{0:T(1024)(128)(4,1)}), s8[4194304]{0:T(1024)(128)(4,1)S(1)}, s32[]{:S(2)}) async-start(s8[6291456]{0:T(1024)(128)(4,1)} %bitcast.135), calls=%async_computation.4 | async-start | bytes 8388608
  482.5 10.0 %slice-start.6 = ((s8[6291456]{0:T(1024)(128)(4,1)}), s8[4194304]{0:T(1024)(128)(4,1)S(1)}, s32[]{:S(2)}) async-start(s8[6291456]{0:T(1024)(128)(4,1)} %bitcast.137), calls=%async_computation.6 | async-start | bytes 8388608
  644.8 29.9 %copy-start.18 = (f32[24,2304]{1,0:T(8,128)S(1)}, f32[24,2304]{1,0:T(8,128)}, u32[]{:S(2)}) copy-start(f32[24,2304]{1,0:T(8,128)} %refs_3_.1) | copy-start | bytes 663556
  644.8 29.9 %copy-start.27 = (f32[24,2304]{1,0:T(8,128)S(1)}, f32[24,2304]{1,0:T(8,128)}, u32[]{:S(2)}) copy-start(f32[24,2304]{1,0:T(8,128)} %param.37) | copy-start | bytes 663556
  644.9 29.9 %copy-start.28 = (f32[24,2304]{1,0:T(8,128)S(1)}, f32[24,2304]{1,0:T(8,128)}, u32[]{:S(2)}) copy-start(f32[24,2304]{1,0:T(8,128)} %param.38) | copy-start | bytes 663556
  644.9 30.9 %copy-start.25 = (f32[24,768]{1,0:T(8,128)S(1)}, f32[24,768]{1,0:T(8,128)}, u32[]{:S(2)}) copy-start(f32[24,768]{1,0:T(8,128)} %get-tuple-element.57) | copy-start | bytes 221188
  644.9 30.9 %copy-start.26 = (f32[24,768]{1,0:T(8,128)S(1)}, f32[24,768]{1,0:T(8,128)}, u32[]{:S(2)}) copy-start(f32[24,768]{1,0:T(8,128)} %refs_4_.1) | copy-start | bytes 221188
  644.9 30.9 %copy-start.30 = (f32[24,768]{1,0:T(8,128)S(1)}, f32[24,768]{1,0:T(8,128)}, u32[]{:S(2)}) copy-start(f32[24,768]{1,0:T(8,128)} %param.40) | copy-start | bytes 221188
  644.9 30.9 %copy-start.31 = (f32[24,768]{1,0:T(8,128)S(1)}, f32[24,768]{1,0:T(8,128)}, u32[]{:S(2)}) copy-start(f32[24,768]{1,0:T(8,128)} %param.41) | copy-start | bytes 221188
  644.9 31.6 %copy-start.14 = (f32[24,3072]{1,0:T(8,128)S(1)}, f32[24,3072]{1,0:T(8,128)}, u32[]{:S(2)}) copy-start(f32[24,3072]{1,0:T(8,128)} %refs_5_.1) | copy-start | bytes 884740
  644.9 31.6 %copy-start.17 = (f32[24,3072]{1,0:T(8,128)S(1)}, f32[24,3072]{1,0:T(8,128)}, u32[]{:S(2)}) copy-start(f32[24,3072]{1,0:T(8,128)} %get-tuple-element.58) | copy-start | bytes 884740
  644.9 31.6 %copy-start.21 = (f32[24,3072]{1,0:T(8,128)S(1)}, f32[24,3072]{1,0:T(8,128)}, u32[]{:S(2)}) copy-start(f32[24,3072]{1,0:T(8,128)} %param.43) | copy-start | bytes 884740
  644.9 31.6 %copy-start.22 = (f32[24,3072]{1,0:T(8,128)S(1)}, f32[24,3072]{1,0:T(8,128)}, u32[]{:S(2)}) copy-start(f32[24,3072]{1,0:T(8,128)} %param.44) | copy-start | bytes 884740
  (40 other events, 179.4 us)

commit v5 on v4

--- a/solution.py
+++ b/solution.py
@@ -157,114 +157,6 @@
 
 def offset(order, position):
     return sum(((position >> step) & 1) << bit for step, bit in enumerate(order))
-
-
-def scatter_kernel(n_dp, n_pair, pieces, n_in, *refs):
-    k = len(pieces)
-    ins, outs = refs[:n_in], refs[n_in : 2 * n_in]
-    accs = refs[2 * n_in : 2 * n_in + k]
-    gots = refs[2 * n_in + k : 2 * n_in + 2 * k]
-    lsem, csend, crecv, send, recv = refs[2 * n_in + 2 * k :]
-    me = my_index(n_pair)
-    n = n_dp * n_pair
-    steps = (n - 1).bit_length() - 1
-    half = 1 << steps
-    orders = [bit_order(n_dp, n_pair, color) for _, _, _, color in pieces]
-    greet([place(me ^ (1 << bit), n_pair) for bit in range(steps + 1)])
-
-    def source(a, block):
-        which, low, high, _ = pieces[a]
-        return ins[which].at[block, :, pl.ds(low, high - low)]
-
-    def core_send(a, upper):
-        lo = half // 2 if upper else 0
-        for p in range(lo, lo + half // 2):
-            block = me ^ (offset(orders[a], p) + 1)
-            remote(source(a, block), gots[a].at[p], csend.at[a, upper], crecv.at[a, upper], place(me ^ 1, n_pair)).start()
-
-    def load(a):
-        for p in range(half):
-            pltpu.make_async_copy(source(a, me ^ offset(orders[a], p)), accs[a].at[p], lsem.at[a]).start()
-
-    def core_copy(a, upper):
-        lo = half // 2 if upper else 0
-        part = pl.ds(lo, half // 2)
-        return remote(gots[a].at[part], gots[a].at[part], csend.at[a, upper], crecv.at[a, upper], place(me ^ 1, n_pair))
-
-    def add(a, lo, count, base):
-        def body(j, carry):
-            accs[a][lo + j] = (
-                accs[a][lo + j].astype(jnp.float32) + gots[a][base + lo + j].astype(jnp.float32)
-            ).astype(jnp.bfloat16)
-            return carry
-        lax.fori_loop(0, count, body, 0)
-
-    def base_of(s):
-        return half + half - (2 << s)
-
-    def hop(a, s):
-        return remote(
-            accs[a].at[pl.ds(1 << s, 1 << s)], gots[a].at[pl.ds(base_of(s), 1 << s)],
-            send.at[a, s], recv.at[a, s], place(me ^ (1 << orders[a][s]), n_pair),
-        )
-
-    for upper in (1, 0):
-        for a in range(k):
-            core_send(a, upper)
-            if upper:
-                load(a)
-    for a in range(k):
-        pltpu.make_async_copy(accs[a], accs[a], lsem.at[a]).wait()
-        core_copy(a, 1).wait_recv()
-        add(a, half // 2, half // 2, 0)
-        hop(a, steps - 1).start()
-    for a in range(k):
-        core_copy(a, 0).wait_recv()
-        add(a, 0, half // 2, 0)
-    for s in reversed(range(steps)):
-        for a in range(k):
-            hop(a, s).wait_recv()
-            if s:
-                mid = 1 << (s - 1)
-                add(a, mid, mid, base_of(s))
-                hop(a, s - 1).start()
-                add(a, 0, mid, base_of(s))
-            else:
-                which, low, high, _ = pieces[a]
-                outs[which][:, low:high] = accs[a][0].astype(jnp.float32) + gots[a][
-                    base_of(0)
-                ].astype(jnp.float32)
-    for a in range(k):
-        core_copy(a, 1).wait_send()
-        core_copy(a, 0).wait_send()
-        for s in range(steps):
-            hop(a, s).wait_send()
-
-
-def scatter_all(grads, pieces, n_dp, n_pair, cid):
-    n, k = n_dp * n_pair, len(pieces)
-    steps = (n - 1).bit_length() - 1
-    half = n // 2
-    shape = lambda p, lead: (lead, grads[p[0]].shape[1], p[2] - p[1])
-    return pl.pallas_call(
-        functools.partial(scatter_kernel, n_dp, n_pair, pieces, len(grads)),
-        out_shape=[jax.ShapeDtypeStruct(g.shape[1:], jnp.float32) for g in grads],
-        in_specs=[ANY] * len(grads),
-        out_specs=[VM] * len(grads),
-        scratch_shapes=[pltpu.VMEM(shape(p, half), jnp.bfloat16) for p in pieces]
-        + [pltpu.VMEM(shape(p, 2 * half - 1), jnp.bfloat16) for p in pieces]
-        + [
-            pltpu.SemaphoreType.DMA((k,)),
-            pltpu.SemaphoreType.DMA((k, 2)),
-            pltpu.SemaphoreType.DMA((k, 2)),
-            pltpu.SemaphoreType.DMA((k, steps)),
-            pltpu.SemaphoreType.DMA((k, steps)),
-        ],
-        compiler_params=pltpu.CompilerParams(
-            collective_id=cid, has_side_effects=True, vmem_limit_bytes=VMEM_LIMIT
-        ),
-        name="weight_grads_sum",
-    )(*grads)
 
 
 def spread(n, n_pair, block, everyone, send, recv, own_sem):
@@ -364,110 +256,6 @@
     )(pooled, positives[:, None], negatives, counts[:, None])
 
 
-def table_kernel(n_pair, rows, chunk, arr_ref, ask_ref, out_ref, sq_ref, hot, stage, part, got_c, out_x, got_x, fin, fin_other,
-                 csend, crecv, xsend, xrecv, fsend, frecv, wsem):
-    me_dp, me_pair = lax.axis_index("dp"), lax.axis_index("pair")
-    core = lax.rem(me_pair, 2)
-    partner = {"dp": me_dp, "pair": me_pair ^ 1}
-    across = {"dp": me_dp, "pair": me_pair ^ 2}
-    count = rows // 2 // chunk
-    greet([partner, across])
-    slots = ask_ref.shape[1]
-
-    def summed(base):
-        ids = lax.broadcasted_iota(jnp.int32, (chunk, slots), 0) + base
-        hot[...] = jnp.where(ids == ask_ref[...], 1.0, 0.0).astype(jnp.bfloat16)
-        return jnp.dot(hot[...], arr_ref[...], preferred_element_type=jnp.float32)
-
-    def c_copy(i):
-        return remote(stage.at[i], got_c.at[i], csend.at[i], crecv.at[i], partner)
-
-    def x_copy(i):
-        return remote(out_x.at[i], got_x.at[i], xsend.at[i], xrecv.at[i], across)
-
-    def f_copy(i):
-        return remote(fin.at[i], fin_other.at[i], fsend.at[i], frecv.at[i], partner)
-
-    for i in range(count):
-        stage[i] = summed((1 - core) * (rows // 2) + i * chunk).astype(jnp.bfloat16)
-        c_copy(i).start()
-    for i in range(count):
-        part[...] = summed(core * (rows // 2) + i * chunk)
-        c_copy(i).wait_recv()
-        out_x[i] = (part[...] + got_c[i].astype(jnp.float32)).astype(jnp.bfloat16)
-        x_copy(i).start()
-    square = jnp.zeros((1, 1), jnp.float32)
-    for i in range(count):
-        x_copy(i).wait_recv()
-        value = (out_x[i].astype(jnp.float32) + got_x[i].astype(jnp.float32)).astype(jnp.bfloat16)
-        fin[i] = value
-        f_copy(i).start()
-        pltpu.make_async_copy(fin.at[i], out_ref.at[pl.ds(core * (rows // 2) + i * chunk, chunk)], wsem.at[0]).start()
-        wide = value.astype(jnp.float32)
-        square = square + jnp.sum(jnp.sum(wide * wide, axis=0, keepdims=True), axis=1, keepdims=True)
-    sq_ref[...] = jnp.where(me_pair < 2, square, 0.0)
-    for i in range(count):
-        f_copy(i).wait_recv()
-        pltpu.make_async_copy(fin_other.at[i], out_ref.at[pl.ds((1 - core) * (rows // 2) + i * chunk, chunk)], wsem.at[1]).start()
-    for i in range(count):
-        c_copy(i).wait_send()
-        x_copy(i).wait_send()
-        f_copy(i).wait_send()
-    pltpu.make_async_copy(fin, fin, wsem.at[0]).wait()
-    pltpu.make_async_copy(fin_other, fin_other, wsem.at[1]).wait()
-
-
-def table_total(arrived, asked, rows, n_pair, cid):
-    chunk, width = 512, arrived.shape[1]
-    count = rows // 2 // chunk
-    box = pltpu.VMEM((count, chunk, width), jnp.bfloat16)
-    sem = pltpu.SemaphoreType.DMA((count,))
-    return pl.pallas_call(
-        functools.partial(table_kernel, n_pair, rows, chunk),
-        out_shape=[jax.ShapeDtypeStruct((rows, width), jnp.bfloat16), jax.ShapeDtypeStruct((1, 1), jnp.float32)],
-        in_specs=[VM, VM], out_specs=[ANY, VM],
-        scratch_shapes=[pltpu.VMEM((chunk, asked.shape[1]), jnp.bfloat16), box, pltpu.VMEM((chunk, width), jnp.float32), box, box, box, box, box,
-            sem, sem, sem, sem, sem, sem, pltpu.SemaphoreType.DMA((2,))],
-        compiler_params=pltpu.CompilerParams(collective_id=cid, has_side_effects=True, vmem_limit_bytes=VMEM_LIMIT),
-        name="table_total",
-    )(arrived, asked)
-
-
-def exchange_kernel(n_dp, x_ref, o_ref, send, recv, lsem):
-    me = lax.axis_index("dp"); pr = lax.axis_index("pair")
-    sem = pltpu.get_barrier_semaphore()
-    def greet(k, _):
-        pl.semaphore_signal(sem, inc=1, device_id={"dp": lax.rem(me + k, n_dp), "pair": pr}, device_id_type=MESH)
-        return 0
-    lax.fori_loop(1, n_dp, greet, 0)
-    pl.semaphore_wait(sem, n_dp - 1)
-    own = pltpu.make_async_copy(x_ref.at[me], o_ref.at[me], lsem); own.start()
-    def cp(k):
-        dst = lax.rem(me + k, n_dp)
-        return pltpu.make_async_remote_copy(x_ref.at[dst], o_ref.at[me], send.at[k], recv.at[k],
-            device_id={"dp": dst, "pair": pr}, device_id_type=MESH)
-    def go(k, _):
-        cp(k).start(); return 0
-    lax.fori_loop(1, n_dp, go, 0)
-    def done(k, _):
-        src = lax.rem(me + n_dp - k, n_dp)
-        c = pltpu.make_async_remote_copy(x_ref.at[me], o_ref.at[src], send.at[k], recv.at[k],
-            device_id={"dp": src, "pair": pr}, device_id_type=MESH)
-        c.wait(); return 0
-    own.wait()
-    lax.fori_loop(1, n_dp, done, 0)
-
-def exchange(x, n_dp, cid):
-    return pl.pallas_call(
-        functools.partial(exchange_kernel, n_dp),
-        out_shape=jax.ShapeDtypeStruct(x.shape, x.dtype),
-        in_specs=[pl.BlockSpec(memory_space=pltpu.VMEM)], out_specs=pl.BlockSpec(memory_space=pltpu.VMEM),
-        scratch_shapes=[pltpu.SemaphoreType.DMA((n_dp,)), pltpu.SemaphoreType.DMA((n_dp,)), pltpu.SemaphoreType.DMA],
-        compiler_params=pltpu.CompilerParams(collective_id=cid, has_side_effects=True, vmem_limit_bytes=VMEM_LIMIT),
-        name="rows_exchange",
-    )(x)
-
-
 NT = (((1,), (1,)), ((), ()))
 TN = (((0,), (0,)), ((), ()))
 
@@ -521,7 +309,7 @@
         name="attention",
     )(lengths, qkv, qkv, qkv, w)
 
-def backward_kernel(len_ref, q_ref, k_ref, v_ref, g_ref, w_ref, o_ref, z_ref, table, total):
+def backward_kernel(len_ref, q_ref, k_ref, v_ref, g_ref, w_ref, o_ref, z_ref, table, total, box, sem):
     seq = q_ref.shape[0]
     tiles = seq // 128
     doc = pl.program_id(1)
@@ -551,8 +339,27 @@
         dk = jnp.dot(ds, q, preferred_element_type=jnp.float32)
         dq = lax.dot_general(ds, k, TN, preferred_element_type=jnp.float32) * 0.125
         parts.append((dq, dk, dv))
+    pair, pairs, docs = pl.program_id(0), pl.num_programs(0), pl.num_programs(1)
+    step = pair * docs + doc
+    slot = lax.rem(step, 2)
+
+    def out(i):
+        rows = pl.ds(pl.multiple_of(doc * seq, seq), seq)
+        columns = pl.ds(pl.multiple_of((i * pairs + pair) * 128, 128), 128)
+        return pltpu.make_async_copy(box.at[slot, i], o_ref.at[rows, columns], sem.at[slot, i])
+
     for i in range(3):
-        o_ref[i] = jnp.where(lane < 64, parts[0][i], parts[1][i]).astype(o_ref.dtype)
+        @pl.when(step >= 2)
+        def _():
+            out(i).wait()
+        box[slot, i] = jnp.where(lane < 64, parts[0][i], parts[1][i]).astype(o_ref.dtype)
+        out(i).start()
+
+    @pl.when(step == pairs * docs - 1)
+    def _():
+        for i in range(3):
+            out(i).wait()
+            pltpu.make_async_copy(box.at[1 - slot, i], box.at[1 - slot, i], sem.at[1 - slot, i]).wait()
     @pl.when(doc == pl.num_programs(1) - 1)
     def _():
         r = lax.broadcasted_iota(jnp.int32, (128, 128), 0)
@@ -580,9 +387,9 @@
         grid_spec=pltpu.PrefetchScalarGridSpec(
             num_scalar_prefetch=1, grid=(pairs, docs),
             in_specs=[spec(0), spec(pairs), spec(2 * pairs), spec(0), pl.BlockSpec((1, 2, 2 * seq), lambda h, d, *_: (h, 0, 0))],
-            out_specs=[pl.BlockSpec((3, seq, 128), lambda h, d, *_: (0, d, h)), pl.BlockSpec((1, 2, 8, 256), lambda h, d, *_: (h, 0, 0, 0))],
-            scratch_shapes=[pltpu.VMEM((2, seq, seq), jnp.float32), pltpu.VMEM((2, seq, seq), jnp.float32)]),
-        out_shape=[jax.ShapeDtypeStruct((3, tokens, pairs * 128), jnp.bfloat16), jax.ShapeDtypeStruct((pairs, 2, 8, 256), jnp.float32)],
+            out_specs=[pl.BlockSpec(memory_space=pl.ANY), pl.BlockSpec((1, 2, 8, 256), lambda h, d, *_: (h, 0, 0, 0))],
+            scratch_shapes=[pltpu.VMEM((2, seq, seq), jnp.float32), pltpu.VMEM((2, seq, seq), jnp.float32), pltpu.VMEM((2, 3, seq, 128), jnp.bfloat16), pltpu.SemaphoreType.DMA((2, 3))]),
+        out_shape=[jax.ShapeDtypeStruct((tokens, 3 * pairs * 128), jnp.bfloat16), jax.ShapeDtypeStruct((pairs, 2, 8, 256), jnp.float32)],
         compiler_params=pltpu.CompilerParams(dimension_semantics=("arbitrary", "arbitrary"), vmem_limit_bytes=50 * 1024 * 1024),
         name="attention_back",
     )(lengths, qkv, qkv, qkv, g, w)
@@ -602,15 +409,109 @@
     return jnp.dot(z.reshape(heads, 2048), hits, precision=HIGHEST).T
 
 def weight_pieces(widths):
-    down = len(widths) - 1
-    cut = widths[down] * 2 // 3 // 128 * 128
-    pieces = [(down - 1, 0, widths[down - 1], 0)]
-    pieces += [(which, 0, widths[which], 1) for which in range(down - 2)]
-    pieces += [(down - 2, 0, widths[down - 2], 0)]
-    return pieces + [(down, 0, cut, 0), (down, cut, widths[down], 1)]
+    cut = widths[3] * 2 // 3 // 128 * 128
+    return [
+        (0, 0, widths[0], 1),
+        (2, 0, widths[2], 0),
+        (1, 0, widths[1], 0),
+        (3, 0, cut, 0),
+        (3, cut, widths[3], 1),
+    ]
+
+
+def gradient_pieces(widths):
+    cut = widths[3] // 3 // 128 * 128
+    return [
+        (2, 0, widths[2], 0),
+        (0, 0, widths[0], 1),
+        (3, 0, cut, 0),
+        (3, cut, widths[3], 1),
+        (1, 0, widths[1], 1),
+    ]
 
 
 NN = (((1,), (0,)), ((), ()))
+
+
+def stage(r):
+    return (0, 1) if r == 0 else (1 << (r - 1), 1 << (r - 1))
+
+
+class Gather:
+    def __init__(self, n_dp, n_pair, pieces, outs, bufs, sems):
+        self.n_pair, self.pieces, self.outs, self.bufs = n_pair, pieces, outs, bufs
+        self.hop_sem, self.side_sem, self.core_sem, self.out_sem = sems
+        self.me = my_index(n_pair)
+        self.hops = (n_dp * n_pair - 1).bit_length() - 2
+        self.orders = [bit_order(n_dp, n_pair, piece[3]) for piece in pieces]
+        self.count = len(pieces)
+
+    def send(self, a, lo, count, to, sem, which, bit):
+        return remote(
+            self.bufs[a].at[pl.ds(lo, count)],
+            self.bufs[a].at[pl.ds(to, count)],
+            sem.at[0, a, which],
+            sem.at[1, a, which],
+            place(self.me ^ (1 << bit), self.n_pair),
+        )
+
+    def hop(self, a, r):
+        return self.send(a, 0, 1 << r, 1 << r, self.hop_sem, r, self.orders[a][r])
+
+    def side(self, a, r):
+        lo, count = stage(r)
+        return self.send(a, lo, count, (1 << self.hops) + lo, self.side_sem, r, self.orders[a][self.hops])
+
+    def core(self, a, r, sided):
+        lo, count = stage(r)
+        lo = lo + (sided << self.hops)
+        return self.send(
+            a, lo, count, (2 << self.hops) + lo, self.core_sem, 2 * r + sided, 0
+        )
+
+    def write_out(self, a, lo, count):
+        which, low, high, _ = self.pieces[a]
+        for p in range(lo, lo + count):
+            block = self.me ^ offset(self.orders[a] + [0], p)
+            pltpu.make_async_copy(
+                self.bufs[a].at[p], self.outs[which].at[block, :, pl.ds(low, high - low)], self.out_sem.at[a]
+            ).start()
+
+    def held(self, r):
+        lo, count = stage(r)
+        for a in range(self.count):
+            if r:
+                self.hop(a, r - 1).wait_recv()
+            if r < self.hops:
+                self.hop(a, r).start()
+            self.side(a, r).start()
+            self.core(a, r, 0).start()
+        for a in range(self.count):
+            self.write_out(a, lo, count)
+
+    def sided(self, r):
+        lo, count = stage(r)
+        for a in range(self.count):
+            self.side(a, r).wait_recv()
+            self.core(a, r, 1).start()
+            self.write_out(a, (1 << self.hops) + lo, count)
+
+    def cored(self, r):
+        lo, count = stage(r)
+        for sided in (0, 1):
+            for a in range(self.count):
+                self.core(a, r, sided).wait_recv()
+                self.write_out(a, (2 << self.hops) + (sided << self.hops) + lo, count)
+
+    def finish(self):
+        for a in range(self.count):
+            for r in range(self.hops):
+                self.hop(a, r).wait_send()
+            for r in range(self.hops + 1):
+                self.side(a, r).wait_send()
+                self.core(a, r, 0).wait_send()
+                self.core(a, r, 1).wait_send()
+            pltpu.make_async_copy(self.bufs[a], self.bufs[a], self.out_sem.at[a]).wait()
 
 
 def triangle(size):
@@ -649,13 +550,10 @@
     outs = refs[6 + n_in : 6 + 2 * n_in]
     rest = refs[6 + 2 * n_in :]
     bufs, rest = rest[:k], rest[k:]
-    (wide, table, ask_out, ask_in, rows_out, rows_in, total, hop_send, hop_recv, core_send,
-     core_recv, out_sem, table_sem, ask_send, ask_recv, row_send, row_recv) = rest
+    wide, table, ask_out, ask_in, rows_out, rows_in, total = rest[:7]
+    table_sem, ask_sem, row_sem, *sems = rest[7:]
     dp, pair = lax.axis_index("dp"), lax.axis_index("pair")
-    me = dp * n_pair + pair
-    steps = (n_dp * n_pair - 1).bit_length() - 1
-    half = 1 << steps
-    orders = [bit_order(n_dp, n_pair, color) for _, _, _, color in pieces]
+    weights = Gather(n_dp, n_pair, pieces, outs, bufs, sems)
     tokens = owner_ref.shape[1]
     cap = ask_out.shape[2]
     table_rows = table_ref.shape[0]
@@ -668,6 +566,8 @@
         pl.semaphore_signal(sem, inc=1, device_id=target, device_id_type=MESH)
     for a, (which, low, high, _) in enumerate(pieces):
         bufs[a][0] = shards[which][:, low:high].astype(jnp.bfloat16)
+    pl.semaphore_wait(sem, n_dp + 1)
+    weights.held(0)
 
     owner = owner_ref[...]
     by_owner = lax.broadcasted_iota(jnp.int32, (n_dp, tokens), 0) == owner
@@ -680,67 +580,23 @@
     key = owner * cap + rank.astype(jnp.int32)
     key_ref[...] = key
     wanted = digits(row_ref[...])
-    for j in range(n_dp):
+
+    def ask(j):
+        return remote(ask_out.at[j], ask_in.at[j], ask_sem.at[0, j], ask_sem.at[1, j], peers[j - 1])
+
+    def reply(j):
+        return remote(
+            rows_out.at[j], rows_in.at[j], row_sem.at[0, j], row_sem.at[1, j], peers[j - 1]
+        )
+
+    far = sorted(range(1, n_dp), reverse=True)
+    for j in far + [0]:
         slot = lax.broadcasted_iota(jnp.int32, (cap, tokens), 0) + (dp ^ j) * cap
         chosen = jnp.where(slot == key, 1.0, 0.0).astype(jnp.bfloat16)
         ask_out[j] = lax.dot_general(wanted, chosen, NT, preferred_element_type=jnp.float32)
-    pl.semaphore_wait(sem, n_dp + 1)
-
-    def ask(j):
-        return remote(ask_out.at[j], ask_in.at[j], ask_send.at[j], ask_recv.at[j], peers[j - 1])
-
-    def reply(j):
-        return remote(rows_out.at[j], rows_in.at[j], row_send.at[j], row_recv.at[j], peers[j - 1])
-
-    def forward(a, s):
-        lo, count = (0, 1) if s == 0 else (1 << (s - 1), 1 << (s - 1))
-        return remote(
-            bufs[a].at[pl.ds(lo, count)],
-            bufs[a].at[pl.ds(half + lo, count)],
-            core_send.at[a, s],
-            core_recv.at[a, s],
-            place(me ^ 1, n_pair),
-        )
-
-    def hop(a, s):
-        return remote(
-            bufs[a].at[pl.ds(0, 1 << s)],
-            bufs[a].at[pl.ds(1 << s, 1 << s)],
-            hop_send.at[a, s],
-            hop_recv.at[a, s],
-            place(me ^ (1 << orders[a][s]), n_pair),
-        )
-
-    def write_out(a, lo, count, core):
-        which, low, high, _ = pieces[a]
-        for p in range(lo, lo + count):
-            block = me ^ (offset(orders[a], p) + core)
-            pltpu.make_async_copy(
-                bufs[a].at[p + core * half],
-                outs[which].at[block, :, pl.ds(low, high - low)],
-                out_sem.at[a],
-            ).start()
-
-    def weights_step(s):
-        for a in range(k):
-            hop(a, s).wait_recv()
-            if s + 1 < steps:
-                hop(a, s + 1).start()
-            forward(a, s + 1).start()
-            write_out(a, 1 << s, 1 << s, 0)
-        for a in range(k):
-            forward(a, s).wait_recv()
-            lo, count = (0, 1) if s == 0 else (1 << (s - 1), 1 << (s - 1))
-            write_out(a, lo, count, 1)
-
-    far = sorted(range(1, n_dp), reverse=True)
-    for j in far:
-        ask(j).start()
-    for a in range(k):
-        hop(a, 0).start()
-    for a in range(k):
-        forward(a, 0).start()
-        write_out(a, 0, 1, 0)
+        if j:
+            ask(j).start()
+    weights.held(1)
     load.wait()
 
     def narrow(i, carry):
@@ -762,11 +618,11 @@
         ask(j).wait_recv()
         answer(j, rows_out)
         reply(j).start()
-        if turn == 1:
-            weights_step(0)
-        if turn == 4:
-            weights_step(1)
+        if turn == n_dp // 4:
+            weights.held(2)
+            weights.sided(0)
     answer(0, rows_in)
+    weights.sided(1)
     upright_key = upright(digits(key))
 
     def seat(j, first):
@@ -775,32 +631,27 @@
         total[...] = got if first else total[...] + got
 
     seat(0, True)
-    near = list(reversed(far))
-    for turn, j in enumerate(near):
+    weights.cored(0)
+    for r in range(3, weights.hops + 1):
+        weights.held(r)
+        weights.sided(r - 1)
+        weights.cored(r - 2)
+    for j in far:
         reply(j).wait_recv()
         seat(j, False)
-        if turn == len(near) // 3:
-            for s in range(2, steps - 1):
-                weights_step(s)
     emb_ref[...] = total[...].astype(jnp.bfloat16)
-    weights_step(steps - 1)
-    for a in range(k):
-        forward(a, steps).wait_recv()
-        write_out(a, half // 2, half // 2, 1)
+    weights.sided(weights.hops)
+    for r in (weights.hops - 1, weights.hops):
+        weights.cored(r)
     for j in far:
         ask(j).wait_send()
         reply(j).wait_send()
-    for a in range(k):
-        for s in range(steps):
-            hop(a, s).wait_send()
-        for s in range(steps + 1):
-            forward(a, s).wait_send()
-        pltpu.make_async_copy(bufs[a], bufs[a], out_sem.at[a]).wait()
+    weights.finish()
 
 
 def front(owner, row, table, shards, pieces, cap, n_dp, n_pair, cid):
     n, k = n_dp * n_pair, len(pieces)
-    steps = (n - 1).bit_length() - 1
+    hops = (n - 1).bit_length() - 2
     tokens = owner.shape[1]
     table_rows, width = table.shape
     padded = -(-table_rows // 256) * 256
@@ -826,22 +677,348 @@
             pltpu.VMEM((n_dp, cap, width), jnp.bfloat16),
             pltpu.VMEM((n_dp, cap, width), jnp.bfloat16),
             pltpu.VMEM((tokens, width), jnp.float32),
-            sem((k, steps)),
-            sem((k, steps)),
-            sem((k, steps + 1)),
-            sem((k, steps + 1)),
+            sem,
+            sem((2, n_dp)),
+            sem((2, n_dp)),
+            sem((2, k, hops)),
+            sem((2, k, hops + 1)),
+            sem((2, k, 2 * hops + 2)),
             sem((k,)),
-            sem,
-            sem((n_dp,)),
-            sem((n_dp,)),
-            sem((n_dp,)),
-            sem((n_dp,)),
         ],
         compiler_params=pltpu.CompilerParams(
             collective_id=cid, has_side_effects=True, vmem_limit_bytes=VMEM_LIMIT
         ),
         name="rows_and_weights",
     )(owner, row, table, *shards)
+
+
+class Scatter:
+    def __init__(self, n_dp, n_pair, pieces, ins, outs, boxes, sems):
+        self.n_pair, self.pieces, self.ins, self.outs = n_pair, pieces, ins, outs
+        k = len(pieces)
+        self.acc, self.from_core = boxes[:k], boxes[k : 2 * k]
+        self.from_side, self.from_hop = boxes[2 * k : 3 * k], boxes[3 * k :]
+        self.load_sem, self.core_sem, self.side_sem, self.hop_sem = sems
+        self.me = my_index(n_pair)
+        self.hops = (n_dp * n_pair - 1).bit_length() - 2
+        self.orders = [bit_order(n_dp, n_pair, piece[3]) for piece in pieces]
+        self.count = k
+
+    def source(self, a, block):
+        which, low, high, _ = self.pieces[a]
+        return self.ins[which].at[block, :, pl.ds(low, high - low)]
+
+    def near(self, bit):
+        return place(self.me ^ (1 << bit), self.n_pair)
+
+    def load(self):
+        for a in range(self.count):
+            for p in range(2 << self.hops):
+                pltpu.make_async_copy(
+                    self.source(a, self.me ^ offset(self.orders[a], p)),
+                    self.acc[a].at[p],
+                    self.load_sem.at[a],
+                ).start()
+
+    def loaded(self):
+        for a in range(self.count):
+            pltpu.make_async_copy(self.acc[a], self.acc[a], self.load_sem.at[a]).wait()
+
+    def core(self, a, r, sided, part=None):
+        lo, count = stage(r)
+        lo = lo + (sided << self.hops)
+        to = self.from_core[a].at[pl.ds(lo, count)]
+        source = to
+        if part is not None:
+            to = self.from_core[a].at[lo + part]
+            source = self.source(a, self.me ^ (offset(self.orders[a], lo + part) + 1))
+        slot = 2 * r + sided
+        return remote(
+            source, to, self.core_sem.at[0, a, slot], self.core_sem.at[1, a, slot], self.near(0)
+        )
+
+    def core_out(self, r):
+        for sided in (1, 0):
+            for a in range(self.count):
+                for part in range(stage(r)[1]):
+                    self.core(a, r, sided, part).start()
+
+    def add(self, a, lo, count, box, at):
+        acc = self.acc[a]
+
+        def body(j, carry):
+            acc[lo + j] = (
+                acc[lo + j].astype(jnp.float32) + box[at + j].astype(jnp.float32)
+            ).astype(jnp.bfloat16)
+            return carry
+
+        lax.fori_loop(0, count, body, 0)
+
+    def side(self, a, r):
+        lo, count = stage(r)
+        return remote(
+            self.acc[a].at[pl.ds((1 << self.hops) + lo, count)],
+            self.from_side[a].at[pl.ds(lo, count)],
+            self.side_sem.at[0, a, r],
+            self.side_sem.at[1, a, r],
+            self.near(self.orders[a][self.hops]),
+        )
+
+    def hop(self, a, r):
+        return remote(
+            self.acc[a].at[pl.ds(1 << r, 1 << r)],
+            self.from_hop[a].at[pl.ds(self.hop_base(r), 1 << r)],
+            self.hop_sem.at[0, a, r],
+            self.hop_sem.at[1, a, r],
+            self.near(self.orders[a][r]),
+        )
+
+    def hop_base(self, r):
+        return (1 << self.hops) - (2 << r)
+
+    def core_in(self, r):
+        lo, count = stage(r)
+        for sided in (1, 0):
+            for a in range(self.count):
+                self.core(a, r, sided).wait_recv()
+                at = lo + (sided << self.hops)
+                self.add(a, at, count, self.from_core[a], at)
+                if sided:
+                    self.side(a, r).start()
+
+    def side_in(self, r):
+        lo, count = stage(r)
+        for a in range(self.count):
+            self.side(a, r).wait_recv()
+            self.add(a, lo, count, self.from_side[a], lo)
+            if r == self.hops:
+                self.hop(a, r - 1).start()
+
+    def hop_in(self, r):
+        for a in range(self.count):
+            self.hop(a, r).wait_recv()
+            base = self.hop_base(r)
+            if r:
+                mid = 1 << (r - 1)
+                self.add(a, mid, mid, self.from_hop[a], base + mid)
+                self.hop(a, r - 1).start()
+                self.add(a, 0, mid, self.from_hop[a], base)
+            else:
+                which, low, high, _ = self.pieces[a]
+                self.outs[which][:, low:high] = self.acc[a][0].astype(jnp.float32) + self.from_hop[
+                    a
+                ][base].astype(jnp.float32)
+
+    def finish(self):
+        for a in range(self.count):
+            for r in range(self.hops):
+                self.hop(a, r).wait_send()
+            for r in range(self.hops + 1):
+                self.side(a, r).wait_send()
+                self.core(a, r, 0).wait_send()
+                self.core(a, r, 1).wait_send()
+
+
+def back_kernel(n_dp, n_pair, pieces, n_in, chunk, *refs):
+    k = len(pieces)
+    grad_ref, key_ref, ask_ref = refs[:3]
+    ins = refs[3 : 3 + n_in]
+    out_ref, square_ref = refs[3 + n_in : 5 + n_in]
+    outs = refs[5 + n_in : 5 + 2 * n_in]
+    rest = refs[5 + 2 * n_in :]
+    boxes, rest = rest[: 4 * k], rest[4 * k :]
+    hits, rows_out, rows_in, hot, part, stage_out, got_core, out_side, got_side, other = rest[:10]
+    row_sem, core_sem, side_sem, last_sem, out_sem, *sems = rest[10:]
+    dp, pair = lax.axis_index("dp"), lax.axis_index("pair")
+    core = lax.rem(pair, 2)
+    weights = Scatter(n_dp, n_pair, pieces, ins, outs, boxes, sems)
+    groups, _, cap, width = rows_out.shape
+    slots = ask_ref.shape[1]
+    count = stage_out.shape[1]
+    half = count * chunk
+    tokens = key_ref.shape[1]
+    peers = [{"dp": dp ^ j, "pair": pair} for j in range(1, n_dp)]
+    partner, across = {"dp": dp, "pair": pair ^ 1}, {"dp": dp, "pair": pair ^ 2}
+    weights.load()
+    greet(peers + [partner, across])
+    weights.core_out(weights.hops)
+
+    def row(g, j):
+        return remote(
+            rows_out.at[g, j],
+            rows_in.at[g, pl.ds(j * cap, cap)],
+            row_sem.at[0, g, j],
+            row_sem.at[1, g, j],
+            peers[j - 1],
+        )
+
+    far = sorted(range(1, n_dp), reverse=True)
+
+    def rows_send(g):
+        columns = pl.ds(g * width, width)
+        for j in far + [0]:
+            if g == 0:
+                slot = lax.broadcasted_iota(jnp.int32, (cap, tokens), 0) + (dp ^ j) * cap
+                hits[j] = jnp.where(slot == key_ref[...], 1.0, 0.0).astype(jnp.bfloat16)
+            got = jnp.dot(hits[j], grad_ref[:, columns], preferred_element_type=jnp.float32)
+            if j:
+                rows_out[g, j] = got.astype(jnp.bfloat16)
+                row(g, j).start()
+            else:
+                rows_in[g, 0:cap] = got.astype(jnp.bfloat16)
+
+    def summed(g, base):
+        ids = lax.broadcasted_iota(jnp.int32, (chunk, slots), 0) + base
+        hot[...] = jnp.where(ids == ask_ref[...], 1.0, 0.0).astype(jnp.bfloat16)
+        return jnp.dot(hot[...], rows_in[g], preferred_element_type=jnp.float32)
+
+    def to_core(g, i):
+        return remote(
+            stage_out.at[g, i], got_core.at[g, i], core_sem.at[0, g, i], core_sem.at[1, g, i], partner
+        )
+
+    def to_side(g, i):
+        return remote(
+            out_side.at[g, i], got_side.at[g, i], side_sem.at[0, g, i], side_sem.at[1, g, i], across
+        )
+
+    def to_other(g, i):
+        return remote(
+            out_side.at[g, i], other.at[g, i], last_sem.at[0, g, i], last_sem.at[1, g, i], partner
+        )
+
+    def write_out(box, g, i, which):
+        rows = pl.ds(which * half + i * chunk, chunk)
+        return pltpu.make_async_copy(
+            box.at[g, i], out_ref.at[rows, pl.ds(g * width, width)], out_sem.at[g, i]
+        )
+
+    def local_sums(g):
+        for j in far:
+            row(g, j).wait_recv()
+        for i in range(count):
+            stage_out[g, i] = summed(g, (1 - core) * half + i * chunk).astype(jnp.bfloat16)
+            to_core(g, i).start()
+        for i in range(count):
+            part[...] = summed(g, core * half + i * chunk)
+            to_core(g, i).wait_recv()
+            out_side[g, i] = (part[...] + got_core[g, i].astype(jnp.float32)).astype(jnp.bfloat16)
+            to_side(g, i).start()
+
+    def finish_sums(g, square):
+        for i in range(count):
+            to_side(g, i).wait()
+            wide = out_side[g, i].astype(jnp.float32) + got_side[g, i].astype(jnp.float32)
+            value = wide.astype(jnp.bfloat16)
+            out_side[g, i] = value
+            to_other(g, i).start()
+            write_out(out_side, g, i, core).start()
+            wide = value.astype(jnp.float32)
+            square = square + jnp.sum(wide * wide, axis=0, keepdims=True)
+        return square
+
+    def hand_over(g):
+        for i in range(count):
+            to_other(g, i).wait_recv()
+            write_out(out_side, g, i, core).wait()
+            write_out(other, g, i, 1 - core).start()
+
+    rows_send(0)
+    for r in reversed(range(weights.hops)):
+        weights.core_out(r)
+    for g in range(1, groups):
+        rows_send(g)
+    weights.loaded()
+    for r in reversed(range(weights.hops + 1)):
+        weights.core_in(r)
+    square = jnp.zeros((1, width), jnp.float32)
+    turn = weights.hops
+    for g in range(groups):
+        local_sums(g)
+        if g == 0:
+            for r in reversed(range(weights.hops + 1)):
+                weights.side_in(r)
+        else:
+            square = finish_sums(g - 1, square)
+            if turn > 1:
+                turn = turn - 1
+                weights.hop_in(turn)
+    square = finish_sums(groups - 1, square)
+    while turn > 0:
+        turn = turn - 1
+        weights.hop_in(turn)
+    square = jnp.sum(square, axis=1, keepdims=True)
+    square_ref[...] = jnp.where(pair < 2, square, 0.0)
+    for g in range(groups):
+        hand_over(g)
+    for g in range(groups):
+        for j in far:
+            row(g, j).wait_send()
+        for i in range(count):
+            to_core(g, i).wait_send()
+            to_other(g, i).wait_send()
+            write_out(other, g, i, 1 - core).wait()
+    weights.finish()
+
+
+def back(grad, key, asked, grads, pieces, table_rows, groups, cid):
+    n_dp, n_pair = lax.axis_size("dp"), lax.axis_size("pair")
+    n, k = n_dp * n_pair, len(pieces)
+    hops = (n - 1).bit_length() - 2
+    chunk = 512
+    rows = -(-table_rows // (2 * chunk)) * 2 * chunk
+    count = rows // 2 // chunk
+    tokens, full = grad.shape
+    width = full // groups
+    slots = asked.shape[1]
+    cap = slots // n_dp
+    sem = pltpu.SemaphoreType.DMA
+    box = pltpu.VMEM((groups, count, chunk, width), jnp.bfloat16)
+
+    def blocks(lead):
+        return [
+            pltpu.VMEM((lead, grads[p[0]].shape[1], p[2] - p[1]), jnp.bfloat16) for p in pieces
+        ]
+
+    return pl.pallas_call(
+        functools.partial(back_kernel, n_dp, n_pair, pieces, len(grads), chunk),
+        out_shape=[
+            jax.ShapeDtypeStruct((rows, full), jnp.bfloat16),
+            jax.ShapeDtypeStruct((1, 1), jnp.float32),
+        ]
+        + [jax.ShapeDtypeStruct(g.shape[1:], jnp.float32) for g in grads],
+        in_specs=[VM] * 3 + [ANY] * len(grads),
+        out_specs=[ANY, VM] + [VM] * len(grads),
+        scratch_shapes=blocks(n // 2)
+        + blocks(n // 2)
+        + blocks(n // 4)
+        + blocks(n // 4 - 1)
+        + [
+            pltpu.VMEM((n_dp, cap, tokens), jnp.bfloat16),
+            pltpu.VMEM((groups, n_dp, cap, width), jnp.bfloat16),
+            pltpu.VMEM((groups, slots, width), jnp.bfloat16),
+            pltpu.VMEM((chunk, slots), jnp.bfloat16),
+            pltpu.VMEM((chunk, width), jnp.float32),
+            box,
+            box,
+            box,
+            box,
+            box,
+            sem((2, groups, n_dp)),
+            sem((2, groups, count)),
+            sem((2, groups, count)),
+            sem((2, groups, count)),
+            sem((groups, count)),
+            sem((k,)),
+            sem((2, k, 2 * hops + 2)),
+            sem((2, k, hops + 1)),
+            sem((2, k, hops)),
+        ],
+        compiler_params=pltpu.CompilerParams(
+            collective_id=cid, has_side_effects=True, vmem_limit_bytes=VMEM_LIMIT
+        ),
+        name="table_and_weights",
+    )(grad, key, asked, *grads)
 
 
 def local_plain(
@@ -1213,53 +1390,34 @@
     grad_attended = lax.dot_general(
         grad_attn_branch, out_back, CONTRACT_COLS, preferred_element_type=jnp.float32
     ).astype(jnp.bfloat16)
-    grad_parts, diagonals = attention_back(
+    grad_qkv_rows, diagonals = attention_back(
         lengths, qkv_rows, grad_attended, bias_rows(position_bias, seq_len, -1), seq_len
     )
     bias_grad_local = bias_gradient(diagonals, seq_len, bucket_count)
-    grad_qkv = [
-        lax.dot_general(normed_one, part, CONTRACT_ROWS, preferred_element_type=jnp.float32)
-        for part in grad_parts
-    ]
-    grad_normed_one = sum(
-        lax.dot_general(
-            part,
-            qkv_back[:, index * model_width : (index + 1) * model_width],
-            CONTRACT_COLS,
-            preferred_element_type=jnp.float32,
-        )
-        for index, part in enumerate(grad_parts)
+    grad_qkv = lax.dot_general(
+        normed_one, grad_qkv_rows, CONTRACT_ROWS, preferred_element_type=jnp.float32
+    )
+    grad_normed_one = lax.dot_general(
+        grad_qkv_rows, qkv_back, CONTRACT_COLS, preferred_element_type=jnp.float32
     )
     grad_emb_part, gain_one = rms_backward(embedded, inverse_one, norm_gains[0], grad_normed_one)
     grad_embedded = grad_residual + grad_emb_part
-    sendback = (
-        jnp.zeros((owners * capacity, model_width), jnp.bfloat16)
-        .at[slot_keys[0]]
-        .set(grad_embedded.astype(jnp.bfloat16))
-    ).reshape(owners, capacity, model_width)
-    arrived = exchange(sendback, owners, 4)
-    arrived = arrived[lax.axis_index("dp") ^ jnp.arange(owners)]
     table_rows = embed_table.shape[0]
-    table_grad, table_square = table_total(
-        arrived.reshape(-1, model_width),
+    parts = owners * holders
+    table_grad, table_square, *weight_grads = back(
+        grad_embedded.astype(jnp.bfloat16),
+        slot_keys,
         asked_rows.reshape(1, -1),
-        -(-table_rows // 1024) * 1024,
-        holders,
-        5,
-    )
-    table_grad = table_grad[:table_rows].astype(jnp.float32)
-    parts = owners * holders
-    weight_grads = scatter_all(
         [
             grad.astype(jnp.bfloat16).reshape(parts, -1, grad.shape[1])
-            for grad in (*grad_qkv, grad_out, grad_in, grad_down)
+            for grad in (grad_qkv, grad_out, grad_in, grad_down)
         ],
-        weight_pieces([model_width] * 4 + [grad_in.shape[1], model_width]),
-        owners,
-        holders,
-        6,
-    )
-    weight_grads = (jnp.concatenate(weight_grads[:3], axis=1), *weight_grads[3:])
+        gradient_pieces([grad.shape[1] for grad in (grad_qkv, grad_out, grad_in, grad_down)]),
+        table_rows,
+        3 if model_width % 384 == 0 else 1,
+        2,
+    )
+    table_grad = table_grad[:table_rows].astype(jnp.float32)
     square_part = table_square[0, 0] + jnp.sum(
         jnp.stack([jnp.sum(grad_piece * grad_piece) for grad_piece in weight_grads])
     )

time: 694 us -> 524 us (0.76)
  Pallas kernels: 516 us -> 362 us
    pallas_call x3 -> x1, Pallas kernels: 252 us -> 148 us  [back(): pl.pallas_call(functools.partial(back_kernel, n_dp, n_pair, pieces, len(g...]
    pallas_call x1, Pallas kernels: 170 us -> 119 us  [front(): pl.pallas_call(functools.partial(front_kernel, n_dp, n_pair, pieces, len(...]
    scatter x1 -> x0, other arithmetic: 9.3 us -> none  [local_fast(): sendback = jnp.zeros((owners * capacity, model_width), jnp.bfloat16).at[s...]
    dot_general x6 -> x2, matrix products: 21.6 us -> 12.4 us  [the longest x1 6.99 us: local_fast(): lax.dot_general(grad_qkv_rows, qkv_back, CONTRACT_COLS, preferred_element...]
where the time goes in v5:
time: 524 us; the launch traced here: 514 us
  Pallas kernels  362 us (69%)
  matrix products  74 us (14%)
  other arithmetic  58.3 us (11%)
  local copies, waits for them, and re-layouts  10.2 us (2%)
  between operations  9.93 us (2%)
    pallas_call x1, Pallas kernels, back(): pl.pallas_call(functools.partial(back_kernel, n_dp, n_pair, pieces, len(g...  148 us
    pallas_call x1, Pallas kernels, front(): pl.pallas_call(functools.partial(front_kernel, n_dp, n_pair, pieces, len(...  119 us
    pallas_call x1, Pallas kernels, attention_back(): pl.pallas_call(backward_kernel, grid_spec=pltpu.PrefetchScalarGridSpec(nu...  43.3 us
    sub x7, other arithmetic, adam_step(): weight - rate * (first_hat / (jnp.sqrt(second_hat) + adam_eps) + shrink *...  34.7 us
    pallas_call x1, Pallas kernels, attention(): pl.pallas_call(forward_kernel, grid_spec=pltpu.PrefetchScalarGridSpec(num...  21.7 us
    pallas_call x1, Pallas kernels, small_total(): pl.pallas_call(functools.partial(total_kernel, n, n_pair), out_shape=jax....  15.2 us
    pallas_call x1, Pallas kernels, pooled_loss(): pl.pallas_call(functools.partial(loss_kernel, n, n_pair, docs), out_shape...  14.6 us

profile of v5, /device:TPU:0, one launch (start us, length us, event | category | flops | bytes accessed | tf_op | source)
XLA Modules:
  0.0 514.1 jit_solution(5221414730975797928)
XLA Ops:
  1.9 119.4 %rows_and_weights.1 = (bf16[1024,768]{1,0:T(8,128)(2,1)}, s32[1,1024]{1,0:T(1,128)}, s32[8,1,256]{2,1,0:T(1,128)}, bf16[32,24,2304]{2,1,0:T(8,128)(2,1)}, bf16[3...) custom-call(s32[1,1024]{1,0:T(1,128)} %bitcast.83, s32[1,1024]{1,0:T(1,128)} %bitcast.81, ...), custom_call_target="tpu_custom_call" | custom-call | tf_op jit(solution)/shard_map/rows_and_weights/pallas_call | solution.py:659
  122.2 1.8 fusion.12
  124.1 8.6 %convolution_convert_fusion.q_ref.k_ref.v_ref = bf16[1024,2304]{1,0:T(8,128)(2,1)} fusion(bf16[768,2304]{1,0:T(8,128)(2,1)} %bitcast.95, bf16[1024,768]{1,0:T(8,128)(2,1)} %get-tuple-element.40, f32[768]{0:T(1024)S(1)} %get-tuple-element.88, f32[1024]{0:T(1024)S(1)} %add_rsqrt_fusion.2), kind=kOutput, calls=%fused_computation.7 | convolution fusion | flops 3629383680 | bytes 9837568 | tf_op jit(solution)/shard_map/dot_general | solution.py:1341
  132.9 21.7 %attention.1 = bf16[1024,768]{1,0:T(8,128)(2,1)S(1)} custom-call(s32[2]{0:T(128)S(1)} %copy-done.1, bf16[1024,2304]{1,0:T(8,128)(2,1)} %convolution_convert_fusion.q_ref.k_ref.v_ref, bf16[1024,2304]{1,0:T(8,128)(2,1)} %convolution_convert_fusion.q_ref.k_ref.v_ref, bf16[1024,2304]{1,0:T(8,128)(2,1)} %convolution_convert_fusion.q_ref.k_ref.v_ref, ...), custom_call_target="tpu_custom_call" | custom-call | tf_op jit(solution)/shard_map/attention/pallas_call | solution.py:300
  156.2 9.0 %maximum_convert_fusion = bf16[1024,3072]{1,0:T(8,128)(2,1)S(1)} fusion(bf16[768,3072]{1,0:T(8,128)(2,1)} %bitcast.87, f32[1024,768]{1,0:T(8,128)S(1)} %get-tuple-element.111, f32[768]{0:T(1024)S(1)} %get-tuple-element.87, f32[1024]{0:T(1024)S(1)} %add_rsqrt_fusion.1), kind=kOutput, calls=%fused_computation.2 | convolution fusion | flops 4840488960 | bytes 14162944 | tf_op jit(solution)/shard_map/dot_general | solution.py:1348
  165.3 6.8 %multiply_reduce_fusion.2 = (f32[1024]{0:T(1024)S(1)}, f32[1024,768]{1,0:T(8,128)}) fusion(f32[1024,768]{1,0:T(8,128)S(1)} %get-tuple-element.111, bf16[1024,3072]{1,0:T(8,128)(2,1)S(1)} %maximum_convert_fusion, bf16[3072,768]{1,0:T(8,128)(2,1)S(1)} %bitcast.94), kind=kOutput, calls=%fused_computation.39 | convolution fusion | flops 4834196480 | bytes 17305600 | tf_op jit(solution)/shard_map/dot_general | solution.py:1351
  172.2 2.4 bitcast_reduce_fusion
  177.5 14.6 %pooled_loss.1 = (f32[1,1]{1,0:T(1,128)}, f32[2,768]{1,0:T(2,128)}) custom-call(f32[2,768]{1,0:T(2,128)} %broadcast_divide_fusion.1.x_ref, s32[64,1]{1,0:T(8,128)} %copy.67.pos_ref, s32[64,7]{1,0:T(8,128)} %copy.68.neg_ref, s32[64,1]{1,0:T(8,128)} %copy.69.count_ref), custom_call_target="tpu_custom_call" | custom-call | tf_op jit(solution)/shard_map/pooled_loss/pallas_call | solution.py:248
  193.0 3.5 fusion.19
  197.5 10.0 %select_convert_fusion = bf16[1024,3072]{1,0:T(8,128)(2,1)S(1)} fusion(bf16[1024,3072]{1,0:T(8,128)(2,1)} %copy-done.44, bf16[1024,768]{1,0:T(8,128)(2,1)S(1)} %fusion.20, bf16[3072,768]{1,0:T(8,128)(2,1)} %bitcast.91), kind=kOutput, calls=%fused_computation.1 | convolution fusion | flops 4841275392 | bytes 18874368 | tf_op jit(solution)/shard_map/dot_general | solution.py:1374
  207.6 5.9 %multiply_reduce_fusion = (f32[768]{0:T(1024)}, f32[1024]{0:T(1024)S(1)}, f32[1024,768]{1,0:T(8,128)S(1)}) fusion(f32[1024,768]{1,0:T(8,128)S(1)} %copy-done.8, f32[1024]{0:T(1024)S(1)} %add_rsqrt_fusion.1, f32[768]{0:T(1024)S(1)} %get-tuple-element.87, bf16[1024,3072]{1,0:T(8,128)(2,1)S(1)} %select_convert_fusion, bf16[768,3072]{1,0:T(8,128)(2,1)S(1)} %bitcast.90), kind=kOutput, calls=%fused_computation.35 | convolution fusion | flops 4836554752 | bytes 17315840 | tf_op jit(solution)/shard_map/dot_general | solution.py:1381
  217.0 43.3 %attention_back.1 = (bf16[1024,2304]{1,0:T(8,128)(2,1)}, f32[6,2,8,256]{3,2,1,0:T(8,128)S(1)}) custom-call(s32[2]{0:T(128)S(1)} %copy-done.1, bf16[1024,2304]{1,0:T(8,128)(2,1)} %convolution_convert_fusion.q_ref.k_ref.v_ref, bf16[1024,2304]{1,0:T(8,128)(2,1)} %convolution_convert_fusion.q_ref.k_ref.v_ref, ...), custom_call_target="tpu_custom_call" | custom-call | tf_op jit(solution)/shard_map/attention_back/pallas_call | solution.py:385
  260.3 7.0 %fusion.6 = (f32[768]{0:T(1024)}, f32[1024]{0:T(1024)S(1)}, f32[1024,768]{1,0:T(8,128)S(1)}) fusion(bf16[1024,768]{1,0:T(8,128)(2,1)S(1)} %copy-done.6, f32[1024]{0:T(1024)S(1)} %add_rsqrt_fusion.2, f32[768]{0:T(1024)S(1)} %get-tuple-element.88, bf16[1024,2304]{1,0:T(8,128)(2,1)} %get-tuple-element.47, bf16[768,2304]{1,0:T(8,128)(2,1)S(1)} %bitcast.96), kind=kOutput, calls=%fused_computation.19 | convolution fusion | flops 3629381888 | bytes 12990464 | tf_op jit(solution)/shard_map/dot_general | solution.py:1400
  267.4 2.0 fusion.11.refs_0_
  270.3 5.5 %convolution_convert_fusion.3 = bf16[768,2304]{1,0:T(8,128)(2,1)} fusion(bf16[1024,2304]{1,0:T(8,128)(2,1)S(1)} %copy-done.39, bf16[1024,768]{1,0:T(8,128)(2,1)S(1)} %copy-done.6, f32[768]{0:T(1024)S(1)} %get-tuple-element.88, f32[1024]{0:T(1024)S(1)} %add_rsqrt_fusion.2), kind=kOutput, calls=%fused_computation.10 | convolution fusion | flops 3628793856 | bytes 9837568 | tf_op jit(solution)/shard_map/dot_general | solution.py:1397
  275.7 2.5 convolution_convert_fusion.5
  278.3 7.2 %convolution_convert_fusion.2 = bf16[768,3072]{1,0:T(8,128)(2,1)} fusion(bf16[1024,3072]{1,0:T(8,128)(2,1)S(1)} %bitcast.100, f32[1024,768]{1,0:T(8,128)S(1)} %copy-done.9, f32[768]{0:T(1024)S(1)} %get-tuple-element.87, f32[1024]{0:T(1024)S(1)} %add_rsqrt_fusion.1), kind=kOutput, calls=%fused_computation.9 | convolution fusion | flops 4836556800 | bytes 14162944 | tf_op jit(solution)/shard_map/dot_general | solution.py:1378
  285.4 7.1 %convolution_convert_fusion.1 = bf16[3072,768]{1,0:T(8,128)(2,1)} fusion(bf16[1024,3072]{1,0:T(8,128)(2,1)S(1)} %bitcast.102, bf16[1024,768]{1,0:T(8,128)(2,1)S(1)} %copy-done.11), kind=kOutput, calls=%fused_computation.8 | convolution fusion | flops 4834197504 | bytes 12582912 | tf_op jit(solution)/shard_map/dot_general | solution.py:1371
  292.6 147.5 %table_and_weights.1 = (bf16[4096,768]{1,0:T(8,128)(2,1)}, f32[1,1]{1,0:T(1,128)}, f32[24,2304]{1,0:T(8,128)}, f32[24,768]{1,0:T(8,128)}, f32[24,3072]{1,0:T(8,128)}, /*index=5*/f32[96,768]{1,0:T(8,128)}) custom-call(bf16[1024,768]{1,0:T(8,128)(2,1)} %fusion.11.refs_0_, s32[1,1024]{1,0:T(1,128)} %get-tuple-element.49.refs_1_, s32[1,2048]{1,0:T(1,128)} %bitcast.82, ...), custom_call_target="tpu_custom_call" | custom-call | tf_op jit(solution)/shard_map/table_and_weights/pallas_call | solution.py:983
  440.1 1.6 multiply_reduce_fusion.6
  444.5 1.6 multiply_reduce_fusion.5
  446.8 1.6 multiply_reduce_fusion.4
  454.7 15.2 %small_total.1 = f32[24,128]{1,0:T(8,128)} custom-call(f32[24,128]{1,0:T(8,128)} %fusion.36.x_ref), custom_call_target="tpu_custom_call" | custom-call | tf_op jit(solution)/shard_map/small_total/pallas_call | solution.py:198
  475.8 29.7 %add_subtract_fusion = (f32[4016,768]{1,0:T(8,128)}, f32[4016,768]{1,0:T(8,128)}, f32[4016,768]{1,0:T(8,128)}) fusion(f32[4016,768]{1,0:T(8,128)} %refs_2_.1, f32[]{:T(128)S(6)} %min.3, bf16[4096,768]{1,0:T(8,128)(2,1)} %get-tuple-element.56, f32[4016,768]{1,0:T(8,128)} %param.34, f32[4016,768]{1,0:T(8,128)} %param.35), kind=kLoop, calls=%fused_computation.4 | loop fusion | flops 49348608 | bytes 80191488 | tf_op jit(solution)/shard_map/sub | solution.py:120
  (169 shorter events, 28.6 us)
Async XLA Ops:
  132.9 21.7 %copy-start.5 = (bf16[1024,768]{1,0:T(8,128)(2,1)S(1)}, bf16[1024,768]{1,0:T(8,128)(2,1)}, u32[]{:S(2)}) copy-start(bf16[1024,768]{1,0:T(8,128)(2,1)} %get-tuple-element.40) | copy-start | bytes 4718596
  132.9 21.7 %copy-start.41 = (bf16[32,24,768]{2,1,0:T(8,128)(2,1)S(1)}, bf16[32,24,768]{2,1,0:T(8,128)(2,1)}, u32[]{:S(2)}) copy-start(bf16[32,24,768]{2,1,0:T(8,128)(2,1)} %get-tuple-element.42) | copy-start | bytes 3538948
  154.6 10.6 %slice-start.2 = ((s8[4718592]{0:T(1024)(128)(4,1)}), s8[4194304]{0:T(1024)(128)(4,1)S(1)}, s32[]{:S(2)}) async-start(s8[4718592]{0:T(1024)(128)(4,1)} %bitcast.92), calls=%async_computation.2 | async-start | bytes 8388608
  156.2 9.1 %copy-start.7 = (f32[1024,768]{1,0:T(8,128)}, f32[1024,768]{1,0:T(8,128)S(1)}, u32[]{:S(2)}) copy-start(f32[1024,768]{1,0:T(8,128)S(1)} %get-tuple-element.111) | copy-start | bytes 9437188
  196.5 11.1 %slice-start = ((s8[4718592]{0:T(1024)(128)(4,1)}), s8[4194304]{0:T(1024)(128)(4,1)S(1)}, s32[]{:S(2)}) async-start(s8[4718592]{0:T(1024)(128)(4,1)} %bitcast.88), calls=%async_computation | async-start | bytes 8388608
  197.5 10.0 %copy-start.10 = (bf16[1024,768]{1,0:T(8,128)(2,1)}, bf16[1024,768]{1,0:T(8,128)(2,1)S(1)}, u32[]{:S(2)}) copy-start(bf16[1024,768]{1,0:T(8,128)(2,1)S(1)} %fusion.20) | copy-start | bytes 4718596
  197.5 10.0 %copy-start.8 = (f32[1024,768]{1,0:T(8,128)S(1)}, f32[1024,768]{1,0:T(8,128)}, u32[]{:S(2)}) copy-start(f32[1024,768]{1,0:T(8,128)} %copy-done.7) | copy-start | bytes 9437188
  197.5 10.0 %slice-start.1 = ((s8[4718592]{0:T(1024)(128)(4,1)}), s8[524288]{0:T(1024)(128)(4,1)S(1)}, s32[]{:S(2)}) async-start(s8[4718592]{0:T(1024)(128)(4,1)} %bitcast.88), calls=%async_computation.1 | async-start | bytes 1048576
  217.0 43.3 %copy-start.6 = (bf16[1024,768]{1,0:T(8,128)(2,1)S(1)}, bf16[1024,768]{1,0:T(8,128)(2,1)}, u32[]{:S(2)}) copy-start(bf16[1024,768]{1,0:T(8,128)(2,1)} %get-tuple-element.40) | copy-start | bytes 4718596
  217.0 43.3 %copy-start.40 = (bf16[32,24,2304]{2,1,0:T(8,128)(2,1)S(1)}, bf16[32,24,2304]{2,1,0:T(8,128)(2,1)}, u32[]{:S(2)}) copy-start(bf16[32,24,2304]{2,1,0:T(8,128)(2,1)} %get-tuple-element.41) | copy-start | bytes 10616836
  267.3 10.9 %slice-start.4 = ((s8[6291456]{0:T(1024)(128)(4,1)}), s8[4194304]{0:T(1024)(128)(4,1)S(1)}, s32[]{:S(2)}) async-start(s8[6291456]{0:T(1024)(128)(4,1)} %bitcast.99), calls=%async_computation.4 | async-start | bytes 8388608
  275.7 9.7 %slice-start.6 = ((s8[6291456]{0:T(1024)(128)(4,1)}), s8[4194304]{0:T(1024)(128)(4,1)S(1)}, s32[]{:S(2)}) async-start(s8[6291456]{0:T(1024)(128)(4,1)} %bitcast.101), calls=%async_computation.6 | async-start | bytes 8388608
  475.7 29.9 %copy-start.16 = (f32[24,2304]{1,0:T(8,128)S(1)}, f32[24,2304]{1,0:T(8,128)}, u32[]{:S(2)}) copy-start(f32[24,2304]{1,0:T(8,128)} %get-tuple-element.52) | copy-start | bytes 663556
  475.7 29.9 %copy-start.17 = (f32[24,2304]{1,0:T(8,128)S(1)}, f32[24,2304]{1,0:T(8,128)}, u32[]{:S(2)}) copy-start(f32[24,2304]{1,0:T(8,128)} %refs_3_.1) | copy-start | bytes 663556
  475.7 29.9 %copy-start.24 = (f32[24,2304]{1,0:T(8,128)S(1)}, f32[24,2304]{1,0:T(8,128)}, u32[]{:S(2)}) copy-start(f32[24,2304]{1,0:T(8,128)} %param.37) | copy-start | bytes 663556
  475.7 29.9 %copy-start.25 = (f32[24,2304]{1,0:T(8,128)S(1)}, f32[24,2304]{1,0:T(8,128)}, u32[]{:S(2)}) copy-start(f32[24,2304]{1,0:T(8,128)} %param.38) | copy-start | bytes 663556
  475.7 30.9 %copy-start.22 = (f32[24,768]{1,0:T(8,128)S(1)}, f32[24,768]{1,0:T(8,128)}, u32[]{:S(2)}) copy-start(f32[24,768]{1,0:T(8,128)} %get-tuple-element.53) | copy-start | bytes 221188
  475.7 30.9 %copy-start.23 = (f32[24,768]{1,0:T(8,128)S(1)}, f32[24,768]{1,0:T(8,128)}, u32[]{:S(2)}) copy-start(f32[24,768]{1,0:T(8,128)} %refs_4_.1) | copy-start | bytes 221188
  475.7 30.8 %copy-start.27 = (f32[24,768]{1,0:T(8,128)S(1)}, f32[24,768]{1,0:T(8,128)}, u32[]{:S(2)}) copy-start(f32[24,768]{1,0:T(8,128)} %param.40) | copy-start | bytes 221188
  475.8 30.8 %copy-start.28 = (f32[24,768]{1,0:T(8,128)S(1)}, f32[24,768]{1,0:T(8,128)}, u32[]{:S(2)}) copy-start(f32[24,768]{1,0:T(8,128)} %param.41) | copy-start | bytes 221188
  475.8 31.6 %copy-start.12 = (f32[24,3072]{1,0:T(8,128)S(1)}, f32[24,3072]{1,0:T(8,128)}, u32[]{:S(2)}) copy-start(f32[24,3072]{1,0:T(8,128)} %refs_5_.1) | copy-start | bytes 884740
  475.8 31.5 %copy-start.15 = (f32[24,3072]{1,0:T(8,128)S(1)}, f32[24,3072]{1,0:T(8,128)}, u32[]{:S(2)}) copy-start(f32[24,3072]{1,0:T(8,128)} %get-tuple-element.54) | copy-start | bytes 884740
  475.8 31.5 %copy-start.18 = (f32[24,3072]{1,0:T(8,128)S(1)}, f32[24,3072]{1,0:T(8,128)}, u32[]{:S(2)}) copy-start(f32[24,3072]{1,0:T(8,128)} %param.43) | copy-start | bytes 884740
  475.8 31.5 %copy-start.19 = (f32[24,3072]{1,0:T(8,128)S(1)}, f32[24,3072]{1,0:T(8,128)}, u32[]{:S(2)}) copy-start(f32[24,3072]{1,0:T(8,128)} %param.44) | copy-start | bytes 884740
  (29 other events, 142.3 us)
